TPU v7x, 32 devices: a whole 2x2x4 slice. The times are simulated.
32 devices in a mesh: dp: 4 (over y, x), expert: 8 (over z, core).
Axes of the slice: x: 2, y: 2, z: 4, core: 2. Of those that a mesh axis runs over, the one named last changes fastest.
Arguments:
- tokens: bfloat16 [32768, 768], P(('dp', 'expert')), may hold values from -6 to 6
- routes: int32 [32768, 1], P(('dp', 'expert')), may hold values from 0 to 15
- slot_order: int32 [32768], P(('dp', 'expert')), may hold values from 0 to 1023, as said below
- prefix_len: int32 [32], P(('dp', 'expert')), may hold values from 102 to 512
- ln1_gain: float32 [768], replicated, may hold values from 0.5 to 1.5
- ln1_bias: float32 [768], replicated, may hold values from -0.6 to 0.6
- mixer_weight: bfloat16 [768, 3072], P(None, ('dp', 'expert')), may hold values from -0.3125 to 0.3125
- ln2_gain: float32 [768], replicated, may hold values from 0.5 to 1.5
- ln2_bias: float32 [768], replicated, may hold values from -0.6 to 0.6
- router_weight: bfloat16 [768, 16], replicated, may hold values from -0.15625 to 0.15625
- expert_in: bfloat16 [16, 3072, 768], P('expert', 'dp'), may hold values from -0.21875 to 0.21875
- expert_out: bfloat16 [16, 3072, 768], P('expert', 'dp'), may hold values from -0.3125 to 0.3125
- cotangent: bfloat16 [32768, 768], P(('dp', 'expert')), may hold values from -6 to 6
Outputs:
- mixed_out: bfloat16 [32768, 768], P(('dp', 'expert'))
- tokens_grad: float32 [32768, 768], P(('dp', 'expert'))
- ln1_gain_grad: float32 [768], replicated
- ln1_bias_grad: float32 [768], replicated
- mixer_grad: float32 [768, 3072], P(None, ('dp', 'expert'))
- ln2_gain_grad: float32 [768], replicated
- ln2_bias_grad: float32 [768], replicated
- router_grad: float32 [768, 16], replicated
- expert_in_grad: float32 [16, 3072, 768], P('expert', 'dp')
- expert_out_grad: float32 [16, 3072, 768], P('expert', 'dp')
- balance: float32 [], replicated
Inputs may be any that keep to these rules, and one draw needn't show every extreme that they name: `routes`: every expert is named by some token. `slot_order`: within each aligned block of 1024 tokens every value appears once.
All inputs are finite; a program needn't handle non-finite values.
Results may differ from a plain program's by a relative error of at most 0.015.
The roundings to bfloat16 on the way count: a program that leaves them out, or rounds other values in their place, can miss the bound.
Values may be sent and summed in bfloat16 or wider, within the bound.
A program may use at most 256 MiB of HBM per device.

v0:
```python
import jax
import jax.numpy as jnp
from jax import lax
from jax.sharding import PartitionSpec as P

HEADS = 12
HEAD_DIM = 64
SEQ = 1024


epsilon = 1e-05
masked_score = -1000000000.0


def layer_norm(values, gain_vec, offset):
    center = values - jnp.mean(values, axis=-1, keepdims=True)
    spread = jnp.mean(center * center, axis=-1, keepdims=True)
    return center * lax.rsqrt(spread + epsilon) * gain_vec + offset


def exact_gelu(values):
    return jax.nn.gelu(values, approximate=False)


def contract_rows(first_op, second_op):
    return lax.dot_general(
        first_op, second_op, (((0,), (0,)), ((), ())), preferred_element_type=jnp.float32
    )


def times_transposed(first_op, second_op):
    return lax.dot_general(
        first_op, second_op, (((1,), (1,)), ((), ())), preferred_element_type=jnp.float32
    )


def split_heads(row_block):
    seq_count = row_block.shape[0] // SEQ
    shaped = row_block.reshape(seq_count, SEQ, HEADS, HEAD_DIM).transpose(0, 2, 1, 3)
    return shaped.reshape(seq_count * HEADS, SEQ, HEAD_DIM)


def join_heads(head_rows):
    seq_count = head_rows.shape[0] // HEADS
    shaped = head_rows.reshape(seq_count, HEADS, SEQ, HEAD_DIM).transpose(0, 2, 1, 3)
    return shaped.reshape(seq_count * SEQ, HEADS * HEAD_DIM)


def block_scores(query_block, key_block, row_offset, prefix):
    scores = times_transposed(query_block, key_block) * HEAD_DIM ** (-0.5)
    row_places = row_offset + jnp.arange(query_block.shape[0])
    col_places = jnp.arange(key_block.shape[0])
    visible = (col_places[None, :] <= row_places[:, None]) | (col_places[None, :] < prefix)
    return jnp.where(visible, scores, masked_score)


def head_forward(query_rows, key_rows, value_rows, prefix):
    half_rows = query_rows.shape[0] // 2
    outputs = []
    lse_parts = []
    for row_offset, key_count in ((0, half_rows), (half_rows, 2 * half_rows)):
        scores = block_scores(
            query_rows[row_offset : row_offset + half_rows],
            key_rows[:key_count],
            row_offset,
            prefix,
        )
        maxima = jnp.max(scores, axis=1, keepdims=True)
        weights = jnp.exp(scores - maxima)
        denominator = jnp.sum(weights, axis=1, keepdims=True)
        probabilities = (weights / denominator).astype(jnp.bfloat16)
        outputs.append(
            jnp.dot(probabilities, value_rows[:key_count], preferred_element_type=jnp.float32)
        )
        lse_parts.append((maxima + jnp.log(denominator))[:, 0])
    return (jnp.concatenate(outputs, 0), jnp.concatenate(lse_parts, 0))


def head_backward(query_rows, key_rows, value_rows, prefix, lse_rows, grad_rows):
    half_rows = query_rows.shape[0] // 2
    score_scale = HEAD_DIM ** (-0.5)
    query_parts = []
    key_grad = jnp.zeros(key_rows.shape, jnp.float32)
    value_grad = jnp.zeros(value_rows.shape, jnp.float32)
    for row_offset, key_count in ((0, half_rows), (half_rows, 2 * half_rows)):
        query_block = query_rows[row_offset : row_offset + half_rows]
        scores = block_scores(query_block, key_rows[:key_count], row_offset, prefix)
        probabilities = jnp.exp(scores - lse_rows[row_offset : row_offset + half_rows, None])
        grad_block = grad_rows[row_offset : row_offset + half_rows]
        value_grad = value_grad.at[:key_count].add(
            contract_rows(probabilities.astype(jnp.bfloat16), grad_block)
        )
        probs_grad = times_transposed(grad_block, value_rows[:key_count])
        row_total = jnp.sum(probabilities * probs_grad, axis=1, keepdims=True)
        scores_grad = (probabilities * (probs_grad - row_total)).astype(jnp.bfloat16)
        query_parts.append(
            jnp.dot(scores_grad, key_rows[:key_count], preferred_element_type=jnp.float32)
            * score_scale
        )
        key_grad = key_grad.at[:key_count].add(
            contract_rows(scores_grad, query_block) * score_scale
        )
    return (jnp.concatenate(query_parts, 0), key_grad, value_grad)


def forward_item(packed):
    return head_forward(packed[0], packed[1], packed[2], packed[3])


def backward_item(packed):
    return head_backward(packed[0], packed[1], packed[2], packed[3], packed[4], packed[5])


def on_device(
    tokens,
    routes,
    slot_order,
    prefix_len,
    ln1_gain,
    ln1_bias,
    mixer_weight,
    ln2_gain,
    ln2_bias,
    router_weight,
    expert_in,
    expert_out,
    cotangent,
):
    model_width = tokens.shape[1]
    token_count = tokens.shape[0]
    expert_total = router_weight.shape[1]
    local_experts = expert_in.shape[0]
    capacity = token_count // expert_total
    owner_count = lax.axis_size("expert")
    full_mixer = lax.all_gather(mixer_weight, ("dp", "expert"), axis=1, tiled=True)
    inner_weight = full_mixer[:, : 3 * model_width]
    outer_weight = full_mixer[:, 3 * model_width :]
    inputs = tokens.astype(jnp.float32)
    normed, norm_pull = jax.vjp(layer_norm, inputs, ln1_gain, ln1_bias)
    normed_low = normed.astype(jnp.bfloat16)
    projected = jnp.dot(normed_low, inner_weight, preferred_element_type=jnp.float32).astype(
        jnp.bfloat16
    )
    query_heads = split_heads(projected[:, :model_width])
    key_heads = split_heads(projected[:, model_width : 2 * model_width])
    value_heads = split_heads(projected[:, 2 * model_width :])
    prefix_heads = jnp.repeat(prefix_len, HEADS)
    head_out, head_lse = lax.map(forward_item, (query_heads, key_heads, value_heads, prefix_heads))
    attended = join_heads(head_out).astype(jnp.bfloat16)
    middle = inputs + jnp.dot(attended, outer_weight, preferred_element_type=jnp.float32)
    normed2, norm2_pull = jax.vjp(layer_norm, middle, ln2_gain, ln2_bias)
    normed2_low = normed2.astype(jnp.bfloat16)
    route_flat = routes[:, 0]
    route_hot = route_flat[:, None] == jnp.arange(expert_total)[None, :]
    route_float = route_hot.astype(jnp.float32)
    logits = jnp.dot(normed2_low, router_weight, preferred_element_type=jnp.float32)
    chosen = jnp.sum(logits * route_float, axis=1)
    gate_value = jax.nn.sigmoid(chosen)
    counts = lax.psum(jnp.sum(route_float, axis=0), ("dp", "expert"))
    earlier = (slot_order[None, :] < slot_order[:, None]).astype(jnp.bfloat16)
    ahead_count = jnp.dot(
        earlier, route_hot.astype(jnp.bfloat16), preferred_element_type=jnp.float32
    )
    slot_rank = jnp.sum(ahead_count * route_float, axis=1).astype(jnp.int32)
    slot_index = route_flat * capacity + slot_rank
    is_kept = slot_rank < capacity
    slot_hot = (
        (slot_index[:, None] == jnp.arange(expert_total * capacity)[None, :]) & is_kept[:, None]
    ).astype(jnp.bfloat16)
    slotted = contract_rows(slot_hot, normed2_low).astype(jnp.bfloat16)
    outgoing = slotted.reshape(owner_count, local_experts * capacity, model_width)
    arrived = lax.all_to_all(outgoing, "expert", split_axis=0, concat_axis=0, tiled=True).reshape(
        owner_count, local_experts, capacity, model_width
    )
    full_in, full_out = (
        lax.all_gather(expert_in, "dp", axis=1, tiled=True),
        lax.all_gather(expert_out, "dp", axis=1, tiled=True),
    )
    pre_act = jnp.einsum("secd,efd->secf", arrived, full_in, preferred_element_type=jnp.float32)
    activated = exact_gelu(pre_act).astype(jnp.bfloat16)
    produced = jnp.einsum(
        "secf,efd->secd", activated, full_out, preferred_element_type=jnp.float32
    ).astype(jnp.bfloat16)
    returned_slots = lax.all_to_all(
        produced.reshape(owner_count, local_experts * capacity, model_width),
        "expert",
        split_axis=0,
        concat_axis=0,
        tiled=True,
    )
    returned = jnp.dot(
        slot_hot,
        returned_slots.reshape(expert_total * capacity, model_width),
        preferred_element_type=jnp.float32,
    )
    output = middle + gate_value[:, None] * returned
    mixed_out = output.astype(jnp.bfloat16)
    out_grad = cotangent.astype(jnp.float32)
    mean_load = jnp.sum(counts) / expert_total
    load_weight = (
        (jnp.sum(route_float * counts[None, :], axis=1) - mean_load) / mean_load / jnp.sum(counts)
    )
    balance_part = jnp.sum(load_weight * gate_value)
    gate_grad = jnp.sum(out_grad * returned, axis=1) + load_weight
    logit_grad = gate_grad * gate_value * (1.0 - gate_value)
    logit_full = (logit_grad[:, None] * route_float).astype(jnp.bfloat16)
    router_part = contract_rows(normed2_low, logit_full)
    normed2_grad = times_transposed(logit_full, router_weight)
    slot_grad = contract_rows(
        slot_hot, (gate_value[:, None] * out_grad).astype(jnp.bfloat16)
    ).astype(jnp.bfloat16)
    sent_grad = lax.all_to_all(
        slot_grad.reshape(owner_count, local_experts * capacity, model_width),
        "expert",
        split_axis=0,
        concat_axis=0,
        tiled=True,
    )
    sent_grad = sent_grad.reshape(owner_count, local_experts, capacity, model_width)
    act_grad = jnp.einsum("secd,efd->secf", sent_grad, full_out, preferred_element_type=jnp.float32)
    pre_grad = jax.vjp(exact_gelu, pre_act)[1](act_grad)[0].astype(jnp.bfloat16)
    out_part = jnp.einsum(
        "secf,secd->efd", activated, sent_grad, preferred_element_type=jnp.float32
    )
    in_part = jnp.einsum("secf,secd->efd", pre_grad, arrived, preferred_element_type=jnp.float32)
    slotted_grad = jnp.einsum(
        "secf,efd->secd", pre_grad, full_in, preferred_element_type=jnp.float32
    ).astype(jnp.bfloat16)
    expert_in_grad, expert_out_grad = (
        lax.psum_scatter(
            in_part.astype(jnp.bfloat16), "dp", scatter_dimension=1, tiled=True
        ).astype(jnp.float32),
        lax.psum_scatter(
            out_part.astype(jnp.bfloat16), "dp", scatter_dimension=1, tiled=True
        ).astype(jnp.float32),
    )
    back_grad = lax.all_to_all(
        slotted_grad.reshape(owner_count, local_experts * capacity, model_width),
        "expert",
        split_axis=0,
        concat_axis=0,
        tiled=True,
    )
    normed2_grad = normed2_grad + jnp.dot(
        slot_hot,
        back_grad.reshape(expert_total * capacity, model_width),
        preferred_element_type=jnp.float32,
    )
    middle_part, ln2_gain_part, ln2_bias_part = norm2_pull(normed2_grad)
    middle_grad = out_grad + middle_part
    attn_grad = middle_grad.astype(jnp.bfloat16)
    outer_grad = contract_rows(attended, attn_grad)
    attended_grad = times_transposed(attn_grad, outer_weight).astype(jnp.bfloat16)
    grad_heads = split_heads(attended_grad)
    query_grad, key_grad, value_grad = lax.map(
        backward_item, (query_heads, key_heads, value_heads, prefix_heads, head_lse, grad_heads)
    )
    projected_grad = jnp.concatenate(
        [join_heads(query_grad), join_heads(key_grad), join_heads(value_grad)], axis=1
    ).astype(jnp.bfloat16)
    inner_grad = contract_rows(normed_low, projected_grad)
    normed_grad = jnp.dot(projected_grad, inner_weight.T, preferred_element_type=jnp.float32)
    input_part, ln1_gain_part, ln1_bias_part = norm_pull(normed_grad)
    tokens_grad = middle_grad + input_part
    mixer_grad = lax.psum_scatter(
        jnp.concatenate([inner_grad, outer_grad], axis=1),
        ("dp", "expert"),
        scatter_dimension=1,
        tiled=True,
    )
    summed = lax.psum(
        (ln1_gain_part, ln1_bias_part, ln2_gain_part, ln2_bias_part, router_part, balance_part),
        ("dp", "expert"),
    )
    return (
        mixed_out,
        tokens_grad,
        summed[0],
        summed[1],
        mixer_grad,
        summed[2],
        summed[3],
        summed[4],
        expert_in_grad,
        expert_out_grad,
        summed[5],
    )


def solution(mesh):
    in_specs = (
        P(("dp", "expert"), None),
        P(("dp", "expert"), None),
        P(("dp", "expert")),
        P(("dp", "expert")),
        P(),
        P(),
        P(None, ("dp", "expert")),
        P(),
        P(),
        P(),
        P("expert", "dp", None),
        P("expert", "dp", None),
        P(("dp", "expert"), None),
    )
    out_specs = (
        P(("dp", "expert"), None),
        P(("dp", "expert"), None),
        P(),
        P(),
        P(None, ("dp", "expert")),
        P(),
        P(),
        P(),
        P("expert", "dp", None),
        P("expert", "dp", None),
        P(),
    )
    return jax.shard_map(
        on_device, mesh=mesh, in_specs=in_specs, out_specs=out_specs, check_vma=False
    )
```

profile of v0, /device:TPU:0, one launch (start us, length us, event | category | flops | bytes accessed | tf_op | source)
XLA Modules:
  0.0 896.2 jit_solution(8644722328064655067)
XLA Ops:
  12.6 64.8 %all-gather.4.cloned.1.call-done = bf16[768,3072]{0,1:T(8,128)(2,1)} async-done(((bf16[768,96]{0,1:T(8,128)(2,1)}), bf16[768,3072]{0,1:T(8,128)(2,1)}) %all-gather.4.cloned.1.call-update) | async-done | bytes 4718608 | tf_op jit(solution)/shard_map/all_gather | solution.py:135
  77.4 6.7 convolution_convert_fusion
  105.7 120.6 %while.35 = (s32[]{:T(128)}, bf16[12,1024,64]{1,2,0:T(8,128)(2,1)S(1)}, f32[12,1024]{1,0:T(8,128)}, s32[12]{0:T(128)S(1)}, bf16[12,1024,64]{2,1,0:T(8,128)(2,1)}...) while((s32[]{:T(128)}, ...), condition=%wide.region_7.8_spmd, body=%wide.region_2.7_spmd.sunk | while | flops 209455104 | bytes 10938013 | solution.py:148
  234.8 4.3 all-to-all-start
  239.3 56.9 %psum.49 = f32[16]{0:T(128)S(1)} all-reduce(f32[16]{0:T(128)S(1)} %convert_reduce_fusion.1), channel_id=1, replica_groups=mesh['dp'=4,'expert'=8] {'dp','expert'}, use_global_device_ids=true, to_apply=%region_14.15 | all-reduce | flops 16 | bytes 128 | tf_op jit(solution)/shard_map/psum | solution.py:159
  309.0 35.2 %fusion.57 = (bf16[8,2,64,3072]{3,2,0,1:T(8,128)(2,1)}, f32[8,2,64,3072]{3,2,0,1:T(8,128)}, f32[2,8,64,3072]{3,2,1,0:T(8,128)}) fusion(bf16[2,3072,768]{2,1,0:T(8,128)(2,1)} %all-gather.6.cloned.1.call-done, bf16[8,2,64,768]{3,2,1,0:T(8,128)(2,1)} %bitcast.40), kind=kOutput, calls=%fused_computation.110 | convolution fusion | flops 5036310528 | bytes 42467328 | tf_op jit(solution)/shard_map/secd,efd->secf/dot_general | solution.py:179
  346.7 20.4 %fusion.54 = bf16[8,2,64,3072]{3,2,0,1:T(8,128)(2,1)} fusion(f32[8,2,64,3072]{3,2,0,1:T(8,128)} %get-tuple-element.398, f32[2,8,64,3072]{3,2,1,0:T(8,128)} %get-tuple-element.419, bf16[2,3072,768]{2,1,0:T(8,128)(2,1)} %all-gather.8.cloned.1.call-done, bf16[8,2,64,768]{3,2,1,0:T(8,128)(2,1)S(1)} %bitcast.346), kind=kOutput, calls=%fused_computation.102 | convolution fusion | flops 4875878400 | bytes 42467328 | tf_op jit(solution)/shard_map/secd,efd->secf/dot_general | solution.py:220
  367.1 9.8 %bitcast_convert_fusion.1 = bf16[2,3072,768]{2,1,0:T(8,128)(2,1)} fusion(bf16[8,2,64,3072]{3,2,0,1:T(8,128)(2,1)} %fusion.54, bf16[8,2,64,768]{3,2,1,0:T(8,128)(2,1)} %bitcast.40), kind=kOutput, calls=%fused_computation.93 | convolution fusion | flops 4836556800 | bytes 17301504 | tf_op jit(solution)/shard_map/secf,secd->efd/dot_general | solution.py:225
  377.0 10.4 %fusion.134 = bf16[8,2,64,768]{3,2,0,1:T(8,128)(2,1)S(1)} fusion(bf16[8,2,64,3072]{3,2,0,1:T(8,128)(2,1)} %fusion.54, bf16[2,3072,768]{2,1,0:T(8,128)(2,1)} %all-gather.6.cloned.1.call-done), kind=kOutput, calls=%fused_computation.193 | convolution fusion | flops 4832624640 | bytes 17301504 | tf_op jit(solution)/shard_map/secf,efd->secd/dot_general | solution.py:226
  392.2 10.3 %fusion.137 = bf16[8,2,64,768]{3,2,0,1:T(8,128)(2,1)S(1)} fusion(bf16[8,2,64,3072]{3,2,0,1:T(8,128)(2,1)} %get-tuple-element.397, bf16[2,3072,768]{2,1,0:T(8,128)(2,1)} %all-gather.8.cloned.1.call-done), kind=kOutput, calls=%fused_computation.194 | convolution fusion | flops 4832624640 | bytes 17301504 | tf_op jit(solution)/shard_map/secf,efd->secd/dot_general | solution.py:181
  403.8 26.1 %all-to-all-done.3 = bf16[8,128,768]{2,1,0:T(8,128)(2,1)S(1)} async-done(((bf16[8,128,768]{2,1,0:T(8,128)(2,1)}), bf16[8,128,768]{2,1,0:T(8,128)(2,1)S(1)}, u32[]{:S(2)}, u32[]{:S(2)}) %all-to-all-start.3) | async-done | bytes 1572896 | tf_op jit(solution)/shard_map/all_to_all | solution.py:237
  429.9 4.3 all-to-all-start.1
  434.3 12.4 %bitcast_convert_fusion = bf16[2,3072,768]{2,1,0:T(8,128)(2,1)} fusion(bf16[8,2,64,3072]{3,2,0,1:T(8,128)(2,1)} %get-tuple-element.397, bf16[8,2,64,768]{3,2,1,0:T(8,128)(2,1)S(1)} %bitcast.347), kind=kOutput, calls=%fused_computation.92 | convolution fusion | flops 4836556800 | bytes 17301504 | tf_op jit(solution)/shard_map/secf,secd->efd/dot_general | solution.py:222
  451.5 20.5 %all-to-all-done.1 = bf16[8,128,768]{2,1,0:T(8,128)(2,1)} async-done(((bf16[8,128,768]{2,1,0:T(8,128)(2,1)}), bf16[8,128,768]{2,1,0:T(8,128)(2,1)}, u32[]{:S(2)}, u32[]{:S(2)}) %all-to-all-start.1) | async-done | bytes 1572896 | tf_op jit(solution)/shard_map/all_to_all | solution.py:184
  491.6 228.1 %while.36 = (s32[]{:T(128)}, bf16[12,1024,64]{1,2,0:T(8,128)(2,1)}, bf16[12,1024,64]{1,2,0:T(8,128)(2,1)}, bf16[12,1024,64]{1,2,0:T(8,128)(2,1)}, s32[12]{0:T(12...) while((s32[]{:T(128)}, bf16[12,1024,64]{1,2,0:T(8,128)(2,1)}, ...), condition=%wide.region_22.23_spmd, body=%wide.region_19.22_spmd.sunk | while | flops 512590848 | bytes 27299008 | solution.py:255
  719.7 4.8 fusion.177
  724.6 9.4 %fusion.119 = f32[768,2304]{1,0:T(8,128)} fusion(bf16[1024,768]{0,1:T(8,128)(2,1)} %bitcast.75, bf16[1024,768]{0,1:T(8,128)(2,1)} %bitcast.72, bf16[1024,768]{0,1:T(8,128)(2,1)} %bitcast.69, bf16[1024,768]{0,1:T(8,128)(2,1)S(1)} %copy-done.2, f32[768]{0:T(1024)S(1)} %copy-done.47, f32[768]{0:T(1024)S(1)} %copy-done.35, f32[1024]{0:T(1024)S(1)} %copy-done.25, ...), kind=kOutput, calls=%fused_computation.185 | convolution fusion | flops 3642753024 | bytes 13383680 | tf_op jit(solution)/shard_map/dot_general | solution.py:26
  734.0 8.8 pad_maximum_fusion.1
  742.8 9.6 %copy.97 = f32[768,3072]{0,1:T(8,128)} copy(f32[768,3072]{1,0:T(8,128)} %pad_maximum_fusion.1) | data formatting | bytes 18874368
  755.2 9.2 %fusion.176 = (f32[768]{0:T(1024)S(1)}, f32[1024,768]{1,0:T(8,128)}) fusion(bf16[768,3072]{0,1:T(8,128)(2,1)} %all-gather.4.cloned.1.call-done, bf16[1024,768]{0,1:T(8,128)(2,1)} %bitcast.75, bf16[1024,768]{0,1:T(8,128)(2,1)} %bitcast.72, bf16[1024,768]{0,1:T(8,128)(2,1)} %bitcast.69), kind=kOutput, calls=%fused_computation.243 | convolution fusion | flops 3638820096 | bytes 11406336 | tf_op jit(solution)/shard_map/dot_general | solution.py:262
  780.6 42.1 %all-reduce.2 = (f32[768]{0:T(1024)}, f32[768]{0:T(1024)}, f32[768]{0:T(1024)}, f32[768]{0:T(1024)}, f32[768,16]{0,1:T(8,128)}, /*index=5*/f32[]{:T(128)}) all-reduce(f32[768]{0:T(1024)S(1)} %get-tuple-element.352, f32[768]{0:T(1024)S(1)} %get-tuple-element.423, ...), channel_id=1, replica_groups=mesh['dp'=4,'expert'=8] {'dp','expert'}, use_global_device_ids=true, to_apply=%region_26.27 | all-reduce | flops 15361 | bytes 122888 | tf_op jit(solution)/shard_map/psum | solution.py:271
  822.7 4.3 convert_element_type.161
  827.0 4.2 convert_element_type.163
  831.2 57.7 %reduce-scatter.10.cloned.1.call-done = f32[96,768]{1,0:T(8,128)} async-done(((f32[3072,768]{1,0:T(8,128)}), f32[96,768]{1,0:T(8,128)}) %reduce-scatter.10.cloned.1.call-update) | async-done | bytes 294928
  (560 shorter events, 444.7 us)
Async XLA Ops:
  7.2 292.8 %copy-start = (bf16[768,16]{0,1:T(8,128)(2,1)S(1)}, bf16[768,16]{0,1:T(8,128)(2,1)}, u32[]{:S(2)}) copy-start(bf16[768,16]{0,1:T(8,128)(2,1)} %param.38) | copy-start | bytes 73732
  7.2 70.2 %all-gather.4.cloned.1.call-start = ((), (), s32[]{:S(2)}) async-start(), calls=%async_computation.7 | async-start | bytes 4866048 | tf_op jit(solution)/shard_map/all_gather | solution.py:135
  8.0 301.0 %all-gather.6.cloned.1.call-start = ((), (), s32[]{:S(2)}) async-start(), calls=%async_computation.8 | async-start | bytes 11796480 | tf_op jit(solution)/shard_map/all_gather | solution.py:176
  8.7 338.0 %all-gather.8.cloned.1.call-start = ((), (), s32[]{:S(2)}) async-start(), calls=%async_computation.9 | async-start | bytes 11796480 | tf_op jit(solution)/shard_map/all_gather | solution.py:177
  10.3 290.9 %copy-start.43 = (pred[1024]{0:T(1024)(128)(4,1)}, pred[1024]{0:T(1024)(128)(4,1)S(1)}, u32[]{:S(2)}) copy-start(pred[1024]{0:T(1024)(128)(4,1)S(1)} %broadcast_compare_fusion) | copy-start | bytes 3076
  11.0 66.4 %copy-start.34 = (f32[768]{0:T(1024)S(1)}, f32[768]{0:T(1024)}, u32[]{:S(2)}) copy-start(f32[768]{0:T(1024)} %param.33) | copy-start | bytes 9220
  11.0 66.4 %copy-start.46 = (f32[768]{0:T(1024)S(1)}, f32[768]{0:T(1024)}, u32[]{:S(2)}) copy-start(f32[768]{0:T(1024)} %param.34) | copy-start | bytes 9220
  11.8 214.5 %copy-start.1 = (bf16[1024,768]{0,1:T(8,128)(2,1)}, bf16[1024,768]{0,1:T(8,128)(2,1)S(1)}, u32[]{:S(2)}) copy-start(bf16[1024,768]{0,1:T(8,128)(2,1)S(1)} %copy.64) | copy-start | bytes 4718596
  12.1 65.3 %copy-start.18 = (f32[1024]{0:T(1024)}, f32[1024]{0:T(1024)S(1)}, u32[]{:S(2)}) copy-start(f32[1024]{0:T(1024)S(1)} %broadcast_multiply_fusion.1) | copy-start | bytes 12292
  12.5 64.9 %copy-start.26 = (f32[1024]{0:T(1024)}, f32[1024]{0:T(1024)S(1)}, u32[]{:S(2)}) copy-start(f32[1024]{0:T(1024)S(1)} %fusion.97) | copy-start | bytes 12292
  12.6 64.9 %copy-start.24 = (f32[1024]{0:T(1024)}, f32[1024]{0:T(1024)S(1)}, u32[]{:S(2)}) copy-start(f32[1024]{0:T(1024)S(1)} %fusion.162) | copy-start | bytes 12292
  12.6 288.7 %copy-start.41 = (s32[1024,1]{0,1:T(1,128)}, s32[1024,1]{0,1:T(1,128)S(1)}, u32[]{:S(2)}) copy-start(s32[1024,1]{0,1:T(1,128)S(1)} %multiply_add_fusion) | copy-start | bytes 12292
  231.4 68.6 %copy-start.8 = (bf16[1024,768]{0,1:T(8,128)(2,1)}, bf16[1024,768]{0,1:T(8,128)(2,1)S(1)}, u32[]{:S(2)}) copy-start(bf16[1024,768]{0,1:T(8,128)(2,1)S(1)} %add_convert_fusion.1) | copy-start | bytes 4718596
  234.8 70.5 %all-to-all-start = ((bf16[8,128,768]{2,1,0:T(8,128)(2,1)}), bf16[8,128,768]{2,1,0:T(8,128)(2,1)}, u32[]{:S(2)}, u32[]{:S(2)}) async-start(bf16[8,128,768]{2,1,0:T(8,128)(2,1)} %bitcast.39), calls=%async_computation | async-start | bytes 3145728 | tf_op jit(solution)/shard_map/all_to_all | solution.py:172
  297.9 7.4 copy-start.10
  305.3 41.4 %all-to-all-start.2 = ((bf16[8,128,768]{2,1,0:T(8,128)(2,1)}), bf16[8,128,768]{2,1,0:T(8,128)(2,1)S(1)}, u32[]{:S(2)}, u32[]{:S(2)}) async-start(bf16[8,128,768]{2,1,0:T(8,128)(2,1)} %bitcast.349), calls=%async_computation.2 | async-start | bytes 3145728 | tf_op jit(solution)/shard_map/all_to_all | solution.py:212
  308.9 513.8 %reduce-scatter.6.cloned.1.call-start = ((), (), s32[]{:S(2)}) async-start(), calls=%async_computation.10 | async-start | bytes 11796480 | tf_op jit(solution)/shard_map/reduce_scatter | solution.py:230
  388.6 41.3 %all-to-all-start.3 = ((bf16[8,128,768]{2,1,0:T(8,128)(2,1)}), bf16[8,128,768]{2,1,0:T(8,128)(2,1)S(1)}, u32[]{:S(2)}, u32[]{:S(2)}) async-start(bf16[8,128,768]{2,1,0:T(8,128)(2,1)} %bitcast.56), calls=%async_computation.3 | async-start | bytes 3145728 | tf_op jit(solution)/shard_map/all_to_all | solution.py:237
  429.9 42.1 %all-to-all-start.1 = ((bf16[8,128,768]{2,1,0:T(8,128)(2,1)}), bf16[8,128,768]{2,1,0:T(8,128)(2,1)}, u32[]{:S(2)}, u32[]{:S(2)}) async-start(bf16[8,128,768]{2,1,0:T(8,128)(2,1)} %bitcast.48), calls=%async_computation.1 | async-start | bytes 3145728 | tf_op jit(solution)/shard_map/all_to_all | solution.py:184
  434.2 392.8 %reduce-scatter.8.cloned.1.call-start = ((), (), s32[]{:S(2)}) async-start(), calls=%async_computation.11 | async-start | bytes 11796480 | tf_op jit(solution)/shard_map/reduce_scatter | solution.py:233
  446.7 442.2 %reduce-scatter.10.cloned.1.call-start = ((), (), s32[]{:S(2)}) async-start(), calls=%async_computation.12 | async-start | bytes 9732096
  447.4 24.6 %copy-start.11 = (bf16[1024,768]{0,1:T(8,128)(2,1)S(1)}, bf16[1024,768]{0,1:T(8,128)(2,1)}, u32[]{:S(2)}) copy-start(bf16[1024,768]{0,1:T(8,128)(2,1)} %copy-done.10) | copy-start | bytes 4718596
  719.7 4.9 copy-start.35
  719.7 4.9 copy-start.47
  (36 other events, 106.3 us)
Sparse Core Ops, SparseCore 0:
  11.1 66.3 all-gather.3
  79.3 94.5 all-gather.5
  175.7 96.9 all-gather.7
  377.1 94.6 reduce-scatter.5
  474.7 94.8 reduce-scatter.7
  752.5 136.3 reduce-scatter.9
where the time goes:
time: 910 us; the launch traced here: 896 us
  matrix products  405 us (45%)
  waiting for transfers between devices  174 us (19%)
  blocking collectives  99 us (11%)
  local copies, waits for them, and re-layouts  98.1 us (11%)
  other arithmetic  85.2 us (9%)
  between operations  17.2 us (2%)
  starting transfers between devices  16 us (2%)
    dot_general x74, matrix products, times_transposed(): lax.dot_general(first_op, second_op, (((1,), (1,)), ((), ())), preferred_...  118 us
    dot_general x53, matrix products, contract_rows(): lax.dot_general(first_op, second_op, (((0,), (0,)), ((), ())), preferred_...  96.2 us
    all_gather x1, waiting for transfers between devices, on_device(): lax.all_gather(mixer_weight, ('dp', 'expert'), axis=1, tiled=True)  64.8 us
    unnamed x7, waiting for transfers between devices  59.8 us
    psum x1, blocking collectives, on_device(): counts = lax.psum(jnp.sum(route_float, axis=0), ('dp', 'expert'))  56.9 us
    psum x1, blocking collectives, on_device(): lax.psum((ln1_gain_part, ln1_bias_part, ln2_gain_part, ln2_bias_part, rou...  42.1 us
    dot_general x1, matrix products, on_device(): jnp.einsum('secd,efd->secf', arrived, full_in, preferred_element_type=jnp...  35.2 us
    dot_general x24, matrix products, head_forward(): jnp.dot(probabilities, value_rows[:key_count], preferred_element_type=jnp...  33.7 us
  transfers between devices with their start and end apart: 10, of which 5 were waited for; matrix products, arithmetic and copies ran while one was open for 62% of the time, Pallas kernels for 0%

commit v1 on v0

--- a/solution.py
+++ b/solution.py
@@ -1,11 +1,11 @@
+import functools
+
 import jax
 import jax.numpy as jnp
 from jax import lax
+from jax.experimental import pallas as pl
+from jax.experimental.pallas import tpu as pltpu
 from jax.sharding import PartitionSpec as P
-
-HEADS = 12
-HEAD_DIM = 64
-SEQ = 1024
 
 
 epsilon = 1e-05
@@ -34,81 +34,123 @@
     )
 
 
-def split_heads(row_block):
-    seq_count = row_block.shape[0] // SEQ
-    shaped = row_block.reshape(seq_count, SEQ, HEADS, HEAD_DIM).transpose(0, 2, 1, 3)
-    return shaped.reshape(seq_count * HEADS, SEQ, HEAD_DIM)
-
-
-def join_heads(head_rows):
-    seq_count = head_rows.shape[0] // HEADS
-    shaped = head_rows.reshape(seq_count, HEADS, SEQ, HEAD_DIM).transpose(0, 2, 1, 3)
-    return shaped.reshape(seq_count * SEQ, HEADS * HEAD_DIM)
-
-
-def block_scores(query_block, key_block, row_offset, prefix):
-    scores = times_transposed(query_block, key_block) * HEAD_DIM ** (-0.5)
-    row_places = row_offset + jnp.arange(query_block.shape[0])
-    col_places = jnp.arange(key_block.shape[0])
-    visible = (col_places[None, :] <= row_places[:, None]) | (col_places[None, :] < prefix)
-    return jnp.where(visible, scores, masked_score)
-
-
-def head_forward(query_rows, key_rows, value_rows, prefix):
-    half_rows = query_rows.shape[0] // 2
-    outputs = []
-    lse_parts = []
-    for row_offset, key_count in ((0, half_rows), (half_rows, 2 * half_rows)):
-        scores = block_scores(
-            query_rows[row_offset : row_offset + half_rows],
-            key_rows[:key_count],
-            row_offset,
-            prefix,
-        )
-        maxima = jnp.max(scores, axis=1, keepdims=True)
-        weights = jnp.exp(scores - maxima)
-        denominator = jnp.sum(weights, axis=1, keepdims=True)
-        probabilities = (weights / denominator).astype(jnp.bfloat16)
-        outputs.append(
-            jnp.dot(probabilities, value_rows[:key_count], preferred_element_type=jnp.float32)
-        )
-        lse_parts.append((maxima + jnp.log(denominator))[:, 0])
-    return (jnp.concatenate(outputs, 0), jnp.concatenate(lse_parts, 0))
-
-
-def head_backward(query_rows, key_rows, value_rows, prefix, lse_rows, grad_rows):
-    half_rows = query_rows.shape[0] // 2
-    score_scale = HEAD_DIM ** (-0.5)
-    query_parts = []
-    key_grad = jnp.zeros(key_rows.shape, jnp.float32)
-    value_grad = jnp.zeros(value_rows.shape, jnp.float32)
-    for row_offset, key_count in ((0, half_rows), (half_rows, 2 * half_rows)):
-        query_block = query_rows[row_offset : row_offset + half_rows]
-        scores = block_scores(query_block, key_rows[:key_count], row_offset, prefix)
-        probabilities = jnp.exp(scores - lse_rows[row_offset : row_offset + half_rows, None])
-        grad_block = grad_rows[row_offset : row_offset + half_rows]
-        value_grad = value_grad.at[:key_count].add(
-            contract_rows(probabilities.astype(jnp.bfloat16), grad_block)
-        )
-        probs_grad = times_transposed(grad_block, value_rows[:key_count])
-        row_total = jnp.sum(probabilities * probs_grad, axis=1, keepdims=True)
-        scores_grad = (probabilities * (probs_grad - row_total)).astype(jnp.bfloat16)
-        query_parts.append(
-            jnp.dot(scores_grad, key_rows[:key_count], preferred_element_type=jnp.float32)
-            * score_scale
-        )
-        key_grad = key_grad.at[:key_count].add(
-            contract_rows(scores_grad, query_block) * score_scale
-        )
-    return (jnp.concatenate(query_parts, 0), key_grad, value_grad)
-
-
-def forward_item(packed):
-    return head_forward(packed[0], packed[1], packed[2], packed[3])
-
-
-def backward_item(packed):
-    return head_backward(packed[0], packed[1], packed[2], packed[3], packed[4], packed[5])
+BF=jnp.bfloat16; F32=jnp.float32
+NEG=-1e9
+QB=256
+def key_extent(i, n):
+    return max((i+1)*QB, 512)
+
+def nt(a,b): return lax.dot_general(a,b,(((1,),(1,)),((),())),preferred_element_type=F32)
+def nn(a,b): return lax.dot_general(a,b,(((1,),(0,)),((),())),preferred_element_type=F32)
+
+def fill_bias(bias_ref, prefix):
+    kp=lax.broadcasted_iota(jnp.int32,(QB,QB),0); qp=lax.broadcasted_iota(jnp.int32,(QB,QB),1)
+    causal=kp<=qp
+    bias_ref[0]=jnp.where(causal|(kp<prefix),0.0,NEG)
+    bias_ref[1]=jnp.where(kp+QB<prefix,0.0,NEG)+jnp.zeros((QB,QB),F32)
+    bias_ref[2]=jnp.where(causal|(kp+QB<prefix),0.0,NEG)
+    bias_ref[3]=jnp.where(causal,0.0,NEG)
+
+def block_bias(j,i):
+    if j==0 and i==0: return 0
+    if j==1 and i==0: return 1
+    if j==1 and i==1: return 2
+    if j==i: return 3
+    return None
+
+def fwd_kernel(pre_ref,q_ref,k_ref,v_ref,o_ref,lse_ref,bias_ref):
+    @pl.when(pl.program_id(0)==0)
+    def _(): fill_bias(bias_ref,pre_ref[0])
+    T=q_ref.shape[0]
+    lane=lax.broadcasted_iota(jnp.int32,(1,128),1)
+    vT=v_ref[...].T
+    ones=jnp.ones((16,T),BF)
+    for i in range(T//QB):
+        K=key_extent(i,T)
+        q=q_ref[i*QB:(i+1)*QB,:]*jnp.asarray(0.125,BF)
+        outs=[]
+        for h in range(2):
+            qh=jnp.where((lane<64) if h==0 else (lane>=64), q, jnp.zeros_like(q))
+            parts=[]
+            for j in range(K//QB):
+                s=nt(k_ref[j*QB:(j+1)*QB,:],qh)
+                b=block_bias(j,i)
+                if b is not None: s=s+bias_ref[b]
+                parts.append(s)
+            m=functools.reduce(jnp.maximum,[jnp.max(s,axis=0,keepdims=True) for s in parts])
+            vh=jnp.concatenate([vT[h*64:(h+1)*64],ones],axis=0)
+            acc=None
+            for j,s in enumerate(parts):
+                p=jnp.exp(s-m).astype(BF)
+                c=nn(vh[:,j*QB:(j+1)*QB],p)
+                acc=c if acc is None else acc+c
+            l=acc[64:65]
+            outs.append(acc[:64]*(1.0/l))
+            lse_ref[0,h:h+1,i*QB:(i+1)*QB]=m+jnp.log(l)
+        o_ref[i*QB:(i+1)*QB,:]=jnp.concatenate(outs,axis=0).T.astype(BF)
+
+def attn_fwd(prefix,proj):
+    T=proj.shape[0]; W=proj.shape[1]//3; n=W//128
+    return pl.pallas_call(fwd_kernel,grid=(n,),
+        in_specs=[pl.BlockSpec(memory_space=pltpu.SMEM)]+[pl.BlockSpec((T,128),functools.partial(lambda c,j:(0,c*n+j),c)) for c in range(3)],
+        out_specs=[pl.BlockSpec((T,128),lambda j:(0,j)),pl.BlockSpec((1,2,T),lambda j:(j,0,0))],
+        out_shape=[jax.ShapeDtypeStruct((T,W),BF),jax.ShapeDtypeStruct((n,2,T),F32)],
+        scratch_shapes=[pltpu.VMEM((4,QB,QB),F32)],
+        compiler_params=pltpu.CompilerParams(vmem_limit_bytes=60<<20),
+        name="attn_fwd")(prefix,proj,proj,proj)
+
+def bwd_kernel(pre_ref,q_ref,k_ref,v_ref,o_ref,g_ref,lse_ref,dq_ref,dk_ref,dv_ref,bias_ref,dk_acc,dv_acc):
+    @pl.when(pl.program_id(0)==0)
+    def _(): fill_bias(bias_ref,pre_ref[0])
+    T=q_ref.shape[0]; nb=T//QB
+    lane=lax.broadcasted_iota(jnp.int32,(1,128),1)
+    kT=k_ref[...].T
+    started=[False]*nb
+    for i in range(nb-1,-1,-1):
+        K=key_extent(i,T)
+        rows=slice(i*QB,(i+1)*QB)
+        q=q_ref[rows,:]*jnp.asarray(0.125,BF)
+        g=g_ref[rows,:]
+        dT=(g.astype(F32)*o_ref[rows,:].astype(F32)).T
+        outs=[]
+        for h in range(2):
+            sel=(lane<64) if h==0 else (lane>=64)
+            qh=jnp.where(sel,q,jnp.zeros_like(q)); gh=jnp.where(sel,g,jnp.zeros_like(g))
+            lse=lse_ref[0,h:h+1,rows]
+            delta=jnp.sum(dT[h*64:(h+1)*64],axis=0,keepdims=True)
+            dq=None
+            for j in range(K//QB):
+                kr=slice(j*QB,(j+1)*QB)
+                s=nt(k_ref[kr,:],qh)
+                b=block_bias(j,i)
+                if b is not None: s=s+bias_ref[b]
+                p=jnp.exp(s-lse)
+                dp=nt(v_ref[kr,:],gh)
+                ds=(p*(dp-delta)).astype(BF)
+                dv=nn(p.astype(BF),gh)
+                dk=nn(ds,qh)
+                first=(i==nb-1 and h==0)
+                if first: dv_acc[kr,:]=dv; dk_acc[kr,:]=dk
+                else:
+                    dv_acc[kr,:]+=dv; dk_acc[kr,:]+=dk
+                c=nn(kT[h*64:(h+1)*64,kr],ds)
+                dq=c if dq is None else dq+c
+            outs.append(dq)
+        dq_ref[rows,:]=(jnp.concatenate(outs,axis=0).T*0.125).astype(BF)
+    dk_ref[...]=dk_acc[...].astype(BF)
+    dv_ref[...]=dv_acc[...].astype(BF)
+
+def attn_bwd(prefix,proj,att,grad,lse):
+    T=proj.shape[0]; W=proj.shape[1]//3; n=W//128
+    cb=lambda: pl.BlockSpec((T,128),lambda j:(0,j))
+    return pl.pallas_call(bwd_kernel,grid=(n,),
+        in_specs=[pl.BlockSpec(memory_space=pltpu.SMEM)]+[pl.BlockSpec((T,128),functools.partial(lambda c,j:(0,c*n+j),c)) for c in range(3)]
+          +[cb(),cb(),pl.BlockSpec((1,2,T),lambda j:(j,0,0))],
+        out_specs=[cb()]*3,
+        out_shape=[jax.ShapeDtypeStruct((T,W),BF)]*3,
+        scratch_shapes=[pltpu.VMEM((4,QB,QB),F32),pltpu.VMEM((T,128),F32),pltpu.VMEM((T,128),F32)],
+        compiler_params=pltpu.CompilerParams(vmem_limit_bytes=60<<20),
+        name="attn_bwd")(prefix,proj,proj,proj,att,grad,lse)
 
 
 def on_device(
@@ -141,12 +183,7 @@
     projected = jnp.dot(normed_low, inner_weight, preferred_element_type=jnp.float32).astype(
         jnp.bfloat16
     )
-    query_heads = split_heads(projected[:, :model_width])
-    key_heads = split_heads(projected[:, model_width : 2 * model_width])
-    value_heads = split_heads(projected[:, 2 * model_width :])
-    prefix_heads = jnp.repeat(prefix_len, HEADS)
-    head_out, head_lse = lax.map(forward_item, (query_heads, key_heads, value_heads, prefix_heads))
-    attended = join_heads(head_out).astype(jnp.bfloat16)
+    attended, head_lse = attn_fwd(prefix_len, projected)
     middle = inputs + jnp.dot(attended, outer_weight, preferred_element_type=jnp.float32)
     normed2, norm2_pull = jax.vjp(layer_norm, middle, ln2_gain, ln2_bias)
     normed2_low = normed2.astype(jnp.bfloat16)
@@ -251,15 +288,12 @@
     attn_grad = middle_grad.astype(jnp.bfloat16)
     outer_grad = contract_rows(attended, attn_grad)
     attended_grad = times_transposed(attn_grad, outer_weight).astype(jnp.bfloat16)
-    grad_heads = split_heads(attended_grad)
-    query_grad, key_grad, value_grad = lax.map(
-        backward_item, (query_heads, key_heads, value_heads, prefix_heads, head_lse, grad_heads)
-    )
-    projected_grad = jnp.concatenate(
-        [join_heads(query_grad), join_heads(key_grad), join_heads(value_grad)], axis=1
-    ).astype(jnp.bfloat16)
-    inner_grad = contract_rows(normed_low, projected_grad)
-    normed_grad = jnp.dot(projected_grad, inner_weight.T, preferred_element_type=jnp.float32)
+    parts = attn_bwd(prefix_len, projected, attended, attended_grad, head_lse)
+    inner_grad = jnp.concatenate([contract_rows(normed_low, part) for part in parts], axis=1)
+    normed_grad = sum(
+        times_transposed(part, inner_weight[:, c * model_width : (c + 1) * model_width])
+        for c, part in enumerate(parts)
+    )
     input_part, ln1_gain_part, ln1_bias_part = norm_pull(normed_grad)
     tokens_grad = middle_grad + input_part
     mixer_grad = lax.psum_scatter(

time: 910 us -> 628 us (0.69)
  matrix products: 405 us -> 151 us
  local copies, waits for them, and re-layouts: 98.1 us -> 15.6 us
  waiting for transfers between devices: 174 us -> 240 us
  other arithmetic: 85.2 us -> 23.1 us
  Pallas kernels: 0 us -> 56.9 us
    dot_general x74 -> x5, matrix products: 118 us -> 15.8 us  [times_transposed(): lax.dot_general(first_op, second_op, (((1,), (1,)), ((), ())), preferred_...]
    dot_general x53 -> x7, matrix products: 96.2 us -> 16.4 us  [contract_rows(): lax.dot_general(first_op, second_op, (((0,), (0,)), ((), ())), preferred_...]
    reduce_scatter x0 -> x1, waiting for transfers between devices: none -> 79.7 us  [on_device(): lax.psum_scatter(jnp.concatenate([inner_grad, outer_grad], axis=1), ('dp'...]
    dot_general x49 -> x0, matrix products: 73.7 us -> none  [the longest x24 33.7 us: head_forward(): jnp.dot(probabilities, value_rows[:key_count], preferred_element_type=jnp...]
    unnamed x7 -> x6, waiting for transfers between devices: 59.8 us -> 2.11 us
    pallas_call x0 -> x2, Pallas kernels: none -> 56.9 us  [the longest x1 34.1 us: attn_bwd(): pl.pallas_call(bwd_kernel, grid=(n,), in_specs=[pl.BlockSpec(memory_space...]
    lt x48 -> x0, other arithmetic: 31.3 us -> none  [block_scores(): col_places[None, :] < prefix]
    all_gather x1, waiting for transfers between devices: 0.01 us -> 31 us  [on_device(): lax.all_gather(expert_out, 'dp', axis=1, tiled=True)]
  transfers between devices with their start and end apart: 10 -> 10, of which waited for: 5 -> 6; matrix products, arithmetic and copies ran while one was open for 62% -> 30% of each run, Pallas kernels for 0% -> 9%
where the time goes in v1:
time: 628 us; the launch traced here: 619 us
  waiting for transfers between devices  240 us (38%)
  matrix products  151 us (24%)
  blocking collectives  96.8 us (15%)
  Pallas kernels  56.9 us (9%)
  other arithmetic  23.1 us (4%)
  starting transfers between devices  18 us (3%)
  between operations  17.3 us (3%)
  local copies, waits for them, and re-layouts  15.6 us (2%)
    reduce_scatter x1, waiting for transfers between devices, on_device(): lax.psum_scatter(jnp.concatenate([inner_grad, outer_grad], axis=1), ('dp'...  79.7 us
    all_gather x1, waiting for transfers between devices, on_device(): lax.all_gather(mixer_weight, ('dp', 'expert'), axis=1, tiled=True)  64.8 us
    psum x1, blocking collectives, on_device(): counts = lax.psum(jnp.sum(route_float, axis=0), ('dp', 'expert'))  57.2 us
    psum x1, blocking collectives, on_device(): lax.psum((ln1_gain_part, ln1_bias_part, ln2_gain_part, ln2_bias_part, rou...  39.6 us
    dot_general x1, matrix products, on_device(): jnp.einsum('secd,efd->secf', arrived, full_in, preferred_element_type=jnp...  35 us
    pallas_call x1, Pallas kernels, attn_bwd(): pl.pallas_call(bwd_kernel, grid=(n,), in_specs=[pl.BlockSpec(memory_space...  34.1 us
    all_to_all x1, waiting for transfers between devices, on_device(): lax.all_to_all(slotted_grad.reshape(owner_count, local_experts * capacity...  33.6 us
    all_gather x1, waiting for transfers between devices, on_device(): lax.all_gather(expert_out, 'dp', axis=1, tiled=True)  31 us
  transfers between devices with their start and end apart: 10, of which 6 were waited for; matrix products, arithmetic and copies ran while one was open for 30% of the time, Pallas kernels for 9%

profile of v1, /device:TPU:0, one launch (start us, length us, event | category | flops | bytes accessed | tf_op | source)
XLA Modules:
  0.0 618.7 jit_solution(838520234735814430)
XLA Ops:
  12.6 64.8 %all-gather.4.cloned.1.call-done = bf16[768,3072]{0,1:T(8,128)(2,1)} async-done(((bf16[768,96]{0,1:T(8,128)(2,1)}), bf16[768,3072]{0,1:T(8,128)(2,1)}) %all-gather.4.cloned.1.call-update) | async-done | bytes 4718608 | tf_op jit(solution)/shard_map/all_gather | solution.py:177
  77.4 8.1 %convolution_convert_fusion.q_ref.k_ref.v_ref = bf16[1024,2304]{1,0:T(8,128)(2,1)} fusion(bf16[768,3072]{0,1:T(8,128)(2,1)} %all-gather.4.cloned.1.call-done, bf16[1024,768]{0,1:T(8,128)(2,1)S(1)} %copy.33, f32[768]{0:T(1024)S(1)} %copy-done.49, f32[768]{0:T(1024)S(1)} %copy-done.24, f32[1024]{0:T(1024)S(1)} %fusion.116, f32[1024]{0:T(1024)S(1)} %broadcast_multiply_fusion.1), kind=kOutput, calls=%fused_computation.42 | convolution fusion | flops 3630956544 | bytes 9844736 | tf_op jit(solution)/shard_map/dot_general | solution.py:183
  85.5 22.8 %attn_fwd.1 = (bf16[1024,768]{1,0:T(8,128)(2,1)}, f32[6,2,1024]{2,1,0:T(2,128)}) custom-call(s32[1]{0:T(128)S(6)} %copy.67.pre_ref, bf16[1024,2304]{1,0:T(8,128)(2,1)} %convolution_convert_fusion.q_ref.k_ref.v_ref, bf16[1024,2304]{1,0:T(8,128)(2,1)} %convolution_convert_fusion.q_ref.k_ref.v_ref, bf16[1024,2304]{1,0:T(8,128)(2,1)} %convolution_convert_fusion.q_ref.k_ref.v_ref), custom_call_target="tpu_custom_call" | custom-call | tf_op jit(solution)/shard_map/attn_fwd/pallas_call | solution.py:94
  116.6 4.3 all-to-all-start
  121.1 57.2 %psum.49 = f32[16]{0:T(128)S(1)} all-reduce(f32[16]{0:T(128)S(1)} %convert_reduce_fusion.1), channel_id=1, replica_groups=mesh['dp'=4,'expert'=8] {'dp','expert'}, use_global_device_ids=true, to_apply=%region_8.0 | all-reduce | flops 16 | bytes 128 | tf_op jit(solution)/shard_map/psum | solution.py:196
  191.5 35.0 %fusion.9 = (bf16[8,2,64,3072]{3,2,0,1:T(8,128)(2,1)}, f32[8,2,64,3072]{3,2,0,1:T(8,128)}, f32[2,8,64,3072]{3,2,1,0:T(8,128)}) fusion(bf16[2,3072,768]{2,1,0:T(8,128)(2,1)} %all-gather.6.cloned.1.call-done, bf16[8,2,64,768]{3,2,1,0:T(8,128)(2,1)} %bitcast.4), kind=kOutput, calls=%fused_computation.19 | convolution fusion | flops 5036310528 | bytes 42467328 | tf_op jit(solution)/shard_map/secd,efd->secf/dot_general | solution.py:216
  229.2 12.3 %bitcast_convert_fusion = bf16[2,3072,768]{2,1,0:T(8,128)(2,1)} fusion(bf16[8,2,64,3072]{3,2,0,1:T(8,128)(2,1)} %get-tuple-element.58, bf16[8,2,64,768]{3,2,1,0:T(8,128)(2,1)S(1)} %bitcast.148), kind=kOutput, calls=%fused_computation.1 | convolution fusion | flops 4836556800 | bytes 17301504 | tf_op jit(solution)/shard_map/secf,secd->efd/dot_general | solution.py:259
  242.0 31.0 %all-gather.8.cloned.1.call-done = bf16[2,3072,768]{2,1,0:T(8,128)(2,1)} async-done(((bf16[2,768,768]{2,1,0:T(8,128)(2,1)}), bf16[2,3072,768]{2,1,0:T(8,128)(2,1)}) %all-gather.8.cloned.1.call-update) | async-done | bytes 9437200 | tf_op jit(solution)/shard_map/all_gather | solution.py:214
  273.0 20.6 %fusion.6 = bf16[8,2,64,3072]{3,2,0,1:T(8,128)(2,1)} fusion(f32[8,2,64,3072]{3,2,0,1:T(8,128)} %get-tuple-element.59, f32[2,8,64,3072]{3,2,1,0:T(8,128)} %get-tuple-element.65, bf16[2,3072,768]{2,1,0:T(8,128)(2,1)} %all-gather.8.cloned.1.call-done, bf16[8,2,64,768]{3,2,1,0:T(8,128)(2,1)S(1)} %bitcast.149), kind=kOutput, calls=%fused_computation.11 | convolution fusion | flops 4875878400 | bytes 42467328 | tf_op jit(solution)/shard_map/secd,efd->secf/dot_general | solution.py:257
  293.5 9.9 %bitcast_convert_fusion.1 = bf16[2,3072,768]{2,1,0:T(8,128)(2,1)} fusion(bf16[8,2,64,3072]{3,2,0,1:T(8,128)(2,1)} %fusion.6, bf16[8,2,64,768]{3,2,1,0:T(8,128)(2,1)} %bitcast.4), kind=kOutput, calls=%fused_computation.2 | convolution fusion | flops 4836556800 | bytes 17301504 | tf_op jit(solution)/shard_map/secf,secd->efd/dot_general | solution.py:262
  303.5 10.2 %fusion.86 = bf16[8,2,64,768]{3,2,0,1:T(8,128)(2,1)S(1)} fusion(bf16[8,2,64,3072]{3,2,0,1:T(8,128)(2,1)} %get-tuple-element.58, bf16[2,3072,768]{2,1,0:T(8,128)(2,1)} %all-gather.8.cloned.1.call-done), kind=kOutput, calls=%fused_computation.100 | convolution fusion | flops 4832624640 | bytes 17301504 | tf_op jit(solution)/shard_map/secf,efd->secd/dot_general | solution.py:218
  314.9 5.0 all-to-all-start.1
  320.0 10.4 %fusion.83 = bf16[8,2,64,768]{3,2,0,1:T(8,128)(2,1)S(1)} fusion(bf16[8,2,64,3072]{3,2,0,1:T(8,128)(2,1)} %fusion.6, bf16[2,3072,768]{2,1,0:T(8,128)(2,1)} %all-gather.6.cloned.1.call-done), kind=kOutput, calls=%fused_computation.99 | convolution fusion | flops 4832624640 | bytes 17301504 | tf_op jit(solution)/shard_map/secf,efd->secd/dot_general | solution.py:263
  331.7 26.1 %all-to-all-done.1 = bf16[8,128,768]{2,1,0:T(8,128)(2,1)S(1)} async-done(((bf16[8,128,768]{2,1,0:T(8,128)(2,1)}), bf16[8,128,768]{2,1,0:T(8,128)(2,1)S(1)}, u32[]{:S(2)}, u32[]{:S(2)}) %all-to-all-start.1) | async-done | bytes 1572896 | tf_op jit(solution)/shard_map/all_to_all | solution.py:221
  357.8 4.3 all-to-all-start.3
  362.4 3.9 fusion.52
  366.3 33.6 %all-to-all-done.3 = bf16[8,128,768]{2,1,0:T(8,128)(2,1)} async-done(((bf16[8,128,768]{2,1,0:T(8,128)(2,1)}), bf16[8,128,768]{2,1,0:T(8,128)(2,1)}, u32[]{:S(2)}, u32[]{:S(2)}) %all-to-all-start.3) | async-done | bytes 1572896 | tf_op jit(solution)/shard_map/all_to_all | solution.py:274
  409.5 4.5 convolution_convert_fusion.1.g_ref
  414.0 34.1 %attn_bwd.1 = (bf16[1024,768]{1,0:T(8,128)(2,1)}, bf16[1024,768]{1,0:T(8,128)(2,1)}, bf16[1024,768]{1,0:T(8,128)(2,1)}) custom-call(s32[1]{0:T(128)S(6)} %copy.67.pre_ref, bf16[1024,2304]{1,0:T(8,128)(2,1)} %convolution_convert_fusion.q_ref.k_ref.v_ref, bf16[1024,2304]{1,0:T(8,128)(2,1)} %convolution_convert_fusion.q_ref.k_ref.v_ref, ...), custom_call_target="tpu_custom_call" | custom-call | tf_op jit(solution)/shard_map/attn_bwd/pallas_call | solution.py:146
  457.3 4.0 pad_maximum_fusion
  483.5 39.6 %all-reduce = (f32[768]{0:T(1024)}, f32[768]{0:T(1024)}, f32[768]{0:T(1024)}, f32[768]{0:T(1024)}, f32[768,16]{0,1:T(8,128)}, /*index=5*/f32[]{:T(128)}) all-reduce(f32[768]{0:T(1024)S(1)} %get-tuple-element.45, f32[768]{0:T(1024)S(1)} %get-tuple-element.48, ...), channel_id=1, replica_groups=mesh['dp'=4,'expert'=8] {'dp','expert'}, use_global_device_ids=true, to_apply=%region_16.0 | all-reduce | flops 15361 | bytes 122888 | tf_op jit(solution)/shard_map/psum | solution.py:305
  523.0 4.2 convert_element_type.112
  527.2 4.4 convert_element_type.110
  531.7 79.7 %reduce-scatter.4.cloned.1.call-done = f32[768,96]{0,1:T(8,128)} async-done(((f32[768,3072]{0,1:T(8,128)}), f32[768,96]{0,1:T(8,128)}) %reduce-scatter.4.cloned.1.call-update) | async-done | bytes 294928 | tf_op jit(solution)/shard_map/reduce_scatter | solution.py:299
  (165 shorter events, 71.4 us)
Async XLA Ops:
  7.2 174.9 %copy-start = (bf16[768,16]{0,1:T(8,128)(2,1)S(1)}, bf16[768,16]{0,1:T(8,128)(2,1)}, u32[]{:S(2)}) copy-start(bf16[768,16]{0,1:T(8,128)(2,1)} %param.22) | copy-start | bytes 73732
  7.2 70.2 %all-gather.4.cloned.1.call-start = ((), (), s32[]{:S(2)}) async-start(), calls=%async_computation.7 | async-start | bytes 4866048 | tf_op jit(solution)/shard_map/all_gather | solution.py:177
  8.0 183.5 %all-gather.6.cloned.1.call-start = ((), (), s32[]{:S(2)}) async-start(), calls=%async_computation.8 | async-start | bytes 11796480 | tf_op jit(solution)/shard_map/all_gather | solution.py:213
  8.7 264.3 %all-gather.8.cloned.1.call-start = ((), (), s32[]{:S(2)}) async-start(), calls=%async_computation.9 | async-start | bytes 11796480 | tf_op jit(solution)/shard_map/all_gather | solution.py:214
  10.3 173.4 %copy-start.43 = (pred[1024]{0:T(1024)(128)(4,1)}, pred[1024]{0:T(1024)(128)(4,1)S(1)}, u32[]{:S(2)}) copy-start(pred[1024]{0:T(1024)(128)(4,1)S(1)} %broadcast_compare_fusion) | copy-start | bytes 3076
  11.0 172.7 %copy-start.41 = (s32[1024,1]{0,1:T(1,128)}, s32[1024,1]{0,1:T(1,128)S(1)}, u32[]{:S(2)}) copy-start(s32[1024,1]{0,1:T(1,128)S(1)} %multiply_add_fusion) | copy-start | bytes 12292
  11.0 66.4 %copy-start.24 = (f32[768]{0:T(1024)S(1)}, f32[768]{0:T(1024)}, u32[]{:S(2)}) copy-start(f32[768]{0:T(1024)} %param.17) | copy-start | bytes 9220
  11.0 66.4 %copy-start.49 = (f32[768]{0:T(1024)S(1)}, f32[768]{0:T(1024)}, u32[]{:S(2)}) copy-start(f32[768]{0:T(1024)} %param.18) | copy-start | bytes 9220
  11.8 96.5 %copy-start.1 = (bf16[1024,768]{0,1:T(8,128)(2,1)}, bf16[1024,768]{0,1:T(8,128)(2,1)S(1)}, u32[]{:S(2)}) copy-start(bf16[1024,768]{0,1:T(8,128)(2,1)S(1)} %copy.33) | copy-start | bytes 4718596
  12.1 73.4 %copy-start.18 = (f32[1024]{0:T(1024)}, f32[1024]{0:T(1024)S(1)}, u32[]{:S(2)}) copy-start(f32[1024]{0:T(1024)S(1)} %broadcast_multiply_fusion.1) | copy-start | bytes 12292
  12.6 72.9 %copy-start.28 = (f32[1024]{0:T(1024)}, f32[1024]{0:T(1024)S(1)}, u32[]{:S(2)}) copy-start(f32[1024]{0:T(1024)S(1)} %fusion.50) | copy-start | bytes 12292
  12.6 72.9 %copy-start.26 = (f32[1024]{0:T(1024)}, f32[1024]{0:T(1024)S(1)}, u32[]{:S(2)}) copy-start(f32[1024]{0:T(1024)S(1)} %fusion.116) | copy-start | bytes 12292
  113.2 68.9 %copy-start.7 = (bf16[1024,768]{0,1:T(8,128)(2,1)}, bf16[1024,768]{0,1:T(8,128)(2,1)S(1)}, u32[]{:S(2)}) copy-start(bf16[1024,768]{0,1:T(8,128)(2,1)S(1)} %add_convert_fusion.1) | copy-start | bytes 4718596
  116.6 71.1 %all-to-all-start = ((bf16[8,128,768]{2,1,0:T(8,128)(2,1)}), bf16[8,128,768]{2,1,0:T(8,128)(2,1)}, u32[]{:S(2)}, u32[]{:S(2)}) async-start(bf16[8,128,768]{2,1,0:T(8,128)(2,1)} %bitcast.3), calls=%async_computation | async-start | bytes 3145728 | tf_op jit(solution)/shard_map/all_to_all | solution.py:209
  181.9 5.8 copy-start.9
  187.8 41.4 %all-to-all-start.2 = ((bf16[8,128,768]{2,1,0:T(8,128)(2,1)}), bf16[8,128,768]{2,1,0:T(8,128)(2,1)S(1)}, u32[]{:S(2)}, u32[]{:S(2)}) async-start(bf16[8,128,768]{2,1,0:T(8,128)(2,1)} %bitcast.151), calls=%async_computation.2 | async-start | bytes 3145728 | tf_op jit(solution)/shard_map/all_to_all | solution.py:249
  191.4 331.6 %reduce-scatter.8.cloned.1.call-start = ((), (), s32[]{:S(2)}) async-start(), calls=%async_computation.12 | async-start | bytes 11796480 | tf_op jit(solution)/shard_map/reduce_scatter | solution.py:270
  241.5 285.7 %reduce-scatter.6.cloned.1.call-start = ((), (), s32[]{:S(2)}) async-start(), calls=%async_computation.11 | async-start | bytes 11796480 | tf_op jit(solution)/shard_map/reduce_scatter | solution.py:267
  314.9 42.8 %all-to-all-start.1 = ((bf16[8,128,768]{2,1,0:T(8,128)(2,1)}), bf16[8,128,768]{2,1,0:T(8,128)(2,1)S(1)}, u32[]{:S(2)}, u32[]{:S(2)}) async-start(bf16[8,128,768]{2,1,0:T(8,128)(2,1)} %bitcast.12), calls=%async_computation.1 | async-start | bytes 3145728 | tf_op jit(solution)/shard_map/all_to_all | solution.py:221
  330.4 31.9 %copy-start.10 = (bf16[1024,768]{0,1:T(8,128)(2,1)S(1)}, bf16[1024,768]{0,1:T(8,128)(2,1)}, u32[]{:S(2)}) copy-start(bf16[1024,768]{0,1:T(8,128)(2,1)} %copy-done.9) | copy-start | bytes 4718596
  330.4 31.9 %copy-start.42 = (s32[1024,1]{0,1:T(1,128)S(1)}, s32[1024,1]{0,1:T(1,128)}, u32[]{:S(2)}) copy-start(s32[1024,1]{0,1:T(1,128)} %copy-done.41) | copy-start | bytes 12292
  330.4 31.9 %copy-start.44 = (pred[1024]{0:T(1024)(128)(4,1)S(1)}, pred[1024]{0:T(1024)(128)(4,1)}, u32[]{:S(2)}) copy-start(pred[1024]{0:T(1024)(128)(4,1)} %copy-done.43) | copy-start | bytes 3076
  357.8 42.1 %all-to-all-start.3 = ((bf16[8,128,768]{2,1,0:T(8,128)(2,1)}), bf16[8,128,768]{2,1,0:T(8,128)(2,1)}, u32[]{:S(2)}, u32[]{:S(2)}) async-start(bf16[8,128,768]{2,1,0:T(8,128)(2,1)} %bitcast.20), calls=%async_computation.3 | async-start | bytes 3145728 | tf_op jit(solution)/shard_map/all_to_all | solution.py:274
  362.1 249.3 %reduce-scatter.4.cloned.1.call-start = ((), (), s32[]{:S(2)}) async-start(), calls=%async_computation.10 | async-start | bytes 9732096 | tf_op jit(solution)/shard_map/reduce_scatter | solution.py:299
  (37 other events, 103.9 us)
Sparse Core Ops, SparseCore 0:
  11.1 66.3 all-gather.3
  79.3 95.3 all-gather.5
  176.5 96.4 all-gather.7
  275.9 94.8 reduce-scatter.7
  373.8 94.8 reduce-scatter.5
  475.1 136.2 reduce-scatter.3

commit v2 on v1

--- a/solution.py
+++ b/solution.py
@@ -9,17 +9,12 @@
 
 
 epsilon = 1e-05
-masked_score = -1000000000.0
 
 
 def layer_norm(values, gain_vec, offset):
     center = values - jnp.mean(values, axis=-1, keepdims=True)
     spread = jnp.mean(center * center, axis=-1, keepdims=True)
     return center * lax.rsqrt(spread + epsilon) * gain_vec + offset
-
-
-def exact_gelu(values):
-    return jax.nn.gelu(values, approximate=False)
 
 
 def contract_rows(first_op, second_op):
@@ -152,6 +147,97 @@
         compiler_params=pltpu.CompilerParams(vmem_limit_bytes=60<<20),
         name="attn_bwd")(prefix,proj,proj,proj,att,grad,lse)
 
+def tn(a,b): return lax.dot_general(a,b,(((0,),(0,)),((),())),preferred_element_type=F32)
+
+ERF_TOP=3.832506856900711
+ERF_NUM=(0.00022905065861350646,0.0034082910107109506,0.050955695062380861,0.18520832239976145,1.128379143519084)
+ERF_DEN=(-1.1791602954361697e-7,0.000023547966471313185,0.0010179625278914885,0.014070470171167667,0.11098505178285362,0.49746925110067538,1.0)
+
+def erf32(x):
+    x=jnp.clip(x,-ERF_TOP,ERF_TOP); y=x*x
+    n=ERF_NUM[0]
+    for c in ERF_NUM[1:]: n=n*y+c
+    d=ERF_DEN[0]
+    for c in ERF_DEN[1:]: d=d*y+c
+    return x*n/d
+
+def expert_kernel(nr,nw,tiles,*refs):
+    rw_ref=refs[0]; refs=refs[1:]
+    x_refs,refs=refs[:nr],refs[nr:]
+    c_refs,refs=refs[:nr],refs[nr:]
+    wi_refs,refs=refs[:nw],refs[nw:]
+    wo_refs,refs=refs[:nw],refs[nw:]
+    p_refs,refs=refs[:nr],refs[nr:]
+    d_refs,refs=refs[:nr],refs[nr:]
+    gi_refs,refs=refs[:nw],refs[nw:]
+    go_refs,refs=refs[:nw],refs[nw:]
+    rg_ref,x_s,g_s,gate_s,p_acc,d_acc=refs
+    step=pl.program_id(0)
+    S,C,D=x_refs[0].shape; R=S*C
+    @pl.when(step==0)
+    def _():
+        for r in range(nr):
+            rows=slice(r*R,(r+1)*R)
+            x=x_refs[r][...].reshape(R,D)
+            gate=jax.nn.sigmoid(jnp.sum(x.astype(F32)*rw_ref[...],axis=1,keepdims=True))
+            x_s[rows,:]=x
+            g_s[rows,:]=(gate*c_refs[r][...].reshape(R,D).astype(F32)).astype(BF)
+            gate_s[rows,:]=gate
+        p_acc[...]=jnp.zeros_like(p_acc); d_acc[...]=jnp.zeros_like(d_acc)
+    for w in range(nw):
+        @pl.when(step//tiles==w)
+        def _(w=w):
+            wi=wi_refs[w][0]; wo=wo_refs[w][0]
+            pre=nt(x_s[...],wi)
+            da=nt(g_s[...],wo)
+            phi=0.5+0.5*erf32(pre*0.7071067811865476)
+            act=(pre*phi).astype(BF)
+            dens=0.3989422804014327*jnp.exp(-0.5*pre*pre)
+            dp=(da*(phi+pre*dens)).astype(BF)
+            p_acc[...]+=nn(act,wo)
+            d_acc[...]+=nn(dp,wi)
+            gi_refs[w][...]=tn(dp,x_s[...]).astype(gi_refs[w].dtype)
+            go_refs[w][...]=tn(act,g_s[...]).astype(go_refs[w].dtype)
+    @pl.when(step==nw*tiles-1)
+    def _():
+        rg=jnp.zeros((1,D),F32)
+        for r in range(nr):
+            rows=slice(r*R,(r+1)*R)
+            p=p_acc[rows,:]; gate=gate_s[rows,:]
+            dot=jnp.sum(p*c_refs[r][...].reshape(R,D).astype(F32),axis=1,keepdims=True)
+            lg=dot*(gate*(1.0-gate))
+            p_refs[r][...]=p.reshape(S,C,D).astype(p_refs[r].dtype)
+            d_refs[r][...]=(d_acc[rows,:]+lg*rw_ref[...]).reshape(S,C,D).astype(d_refs[r].dtype)
+            rg=rg+jnp.sum(lg*x_s[rows,:].astype(F32),axis=0,keepdims=True)
+        rg_ref[...]=rg
+
+def run_expert(e,rw,xs,cs,wis,wos):
+    nr,nw=len(xs),len(wis)
+    S,C,D=xs[0].shape; Q=wis[0].shape[1]; R=nr*S*C
+    tile=Q
+    for t in (384,256,192,128):
+        if Q%t==0: tile=t; break
+    tiles=Q//tile
+    whole=lambda shape: pl.BlockSpec(shape,lambda i:(0,)*len(shape))
+    at=lambda w: (lambda i: jnp.clip(i-w*tiles,0,tiles-1))
+    wspec=lambda w: pl.BlockSpec((1,tile,D),lambda i,f=at(w):(e,f(i),0))
+    gspec=lambda w: pl.BlockSpec((tile,D),lambda i,f=at(w):(f(i),0))
+    rows_spec=whole((S,C,D))
+    kind=lambda k: F32 if k==0 else BF
+    outs=pl.pallas_call(functools.partial(expert_kernel,nr,nw,tiles),grid=(nw*tiles,),
+        in_specs=[whole((1,D))]+[rows_spec]*(2*nr)+[wspec(w) for w in range(nw)]*2,
+        out_specs=[rows_spec]*(2*nr)+[gspec(w) for w in range(nw)]*2+[whole((1,D))],
+        out_shape=[jax.ShapeDtypeStruct((S,C,D),kind(r)) for r in range(nr)]*2
+          +[jax.ShapeDtypeStruct((Q,D),kind(w)) for w in range(nw)]*2+[jax.ShapeDtypeStruct((1,D),F32)],
+        scratch_shapes=[pltpu.VMEM((R,D),BF),pltpu.VMEM((R,D),BF),pltpu.VMEM((R,1),F32),pltpu.VMEM((R,D),F32),pltpu.VMEM((R,D),F32)],
+        compiler_params=pltpu.CompilerParams(vmem_limit_bytes=60<<20),
+        cost_estimate=pl.CostEstimate(flops=12*R*nw*Q*D,bytes_accessed=nw*Q*D*10+R*D*10,transcendentals=R*nw*Q),
+        name="expert")(rw,*xs,*cs,*wis,*wos)
+    return outs[:nr],outs[nr:2*nr],outs[2*nr:2*nr+nw],outs[2*nr+nw:2*nr+2*nw],outs[-1]
+
+def low_shift(n,nx,k): return [(i,i//nx*nx+(i%nx+k)%nx) for i in range(n)]
+def high_shift(n,nx,k): return [(i,(i+k*nx)%n) for i in range(n)]
+
 
 def on_device(
     tokens,
@@ -174,6 +260,40 @@
     local_experts = expert_in.shape[0]
     capacity = token_count // expert_total
     owner_count = lax.axis_size("expert")
+    dp_count = lax.axis_size("dp")
+    low = max(d for d in range(1, dp_count + 1) if dp_count % d == 0 and d * d <= dp_count)
+    high = dp_count // low
+    to_low = lambda a, k: lax.ppermute(a, "dp", low_shift(dp_count, low, k))
+    to_high = lambda a, k: lax.ppermute(a, "dp", high_shift(dp_count, low, k))
+    swap_owner = lambda a: lax.all_to_all(a, "expert", split_axis=0, concat_axis=0, tiled=True)
+    ins = [expert_in] + [to_low(expert_in, k) for k in range(1, low)]
+    outs = [expert_out] + [to_low(expert_out, k) for k in range(1, low)]
+    route_flat = routes[:, 0]
+    route_hot = route_flat[:, None] == jnp.arange(expert_total)[None, :]
+    route_float = route_hot.astype(jnp.float32)
+    counts = lax.psum(jnp.sum(route_float, axis=0), ("dp", "expert"))
+    earlier = (slot_order[None, :] < slot_order[:, None]).astype(jnp.bfloat16)
+    ahead_count = jnp.dot(
+        earlier, route_hot.astype(jnp.bfloat16), preferred_element_type=jnp.float32
+    )
+    slot_rank = jnp.sum(ahead_count * route_float, axis=1).astype(jnp.int32)
+    part_rows = owner_count * capacity
+    slot_index = (
+        route_flat % local_experts * part_rows + route_flat // local_experts * capacity + slot_rank
+    )
+    is_kept = slot_rank < capacity
+    slot_hot = (
+        (slot_index[:, None] == jnp.arange(expert_total * capacity)[None, :]) & is_kept[:, None]
+    ).astype(jnp.bfloat16)
+    cot_sets = []
+    for e in range(local_experts):
+        hot = slot_hot[:, e * part_rows : (e + 1) * part_rows]
+        mine = swap_owner(
+            contract_rows(hot, cotangent)
+            .astype(jnp.bfloat16)
+            .reshape(owner_count, capacity, model_width)
+        )
+        cot_sets.append([mine] + [to_high(mine, k) for k in range(1, high)])
     full_mixer = lax.all_gather(mixer_weight, ("dp", "expert"), axis=1, tiled=True)
     inner_weight = full_mixer[:, : 3 * model_width]
     outer_weight = full_mixer[:, 3 * model_width :]
@@ -187,102 +307,60 @@
     middle = inputs + jnp.dot(attended, outer_weight, preferred_element_type=jnp.float32)
     normed2, norm2_pull = jax.vjp(layer_norm, middle, ln2_gain, ln2_bias)
     normed2_low = normed2.astype(jnp.bfloat16)
-    route_flat = routes[:, 0]
-    route_hot = route_flat[:, None] == jnp.arange(expert_total)[None, :]
-    route_float = route_hot.astype(jnp.float32)
-    logits = jnp.dot(normed2_low, router_weight, preferred_element_type=jnp.float32)
-    chosen = jnp.sum(logits * route_float, axis=1)
+    chosen = jnp.sum(
+        jnp.dot(normed2_low, router_weight, preferred_element_type=jnp.float32) * route_float, axis=1
+    )
     gate_value = jax.nn.sigmoid(chosen)
-    counts = lax.psum(jnp.sum(route_float, axis=0), ("dp", "expert"))
-    earlier = (slot_order[None, :] < slot_order[:, None]).astype(jnp.bfloat16)
-    ahead_count = jnp.dot(
-        earlier, route_hot.astype(jnp.bfloat16), preferred_element_type=jnp.float32
-    )
-    slot_rank = jnp.sum(ahead_count * route_float, axis=1).astype(jnp.int32)
-    slot_index = route_flat * capacity + slot_rank
-    is_kept = slot_rank < capacity
-    slot_hot = (
-        (slot_index[:, None] == jnp.arange(expert_total * capacity)[None, :]) & is_kept[:, None]
-    ).astype(jnp.bfloat16)
-    slotted = contract_rows(slot_hot, normed2_low).astype(jnp.bfloat16)
-    outgoing = slotted.reshape(owner_count, local_experts * capacity, model_width)
-    arrived = lax.all_to_all(outgoing, "expert", split_axis=0, concat_axis=0, tiled=True).reshape(
-        owner_count, local_experts, capacity, model_width
-    )
-    full_in, full_out = (
-        lax.all_gather(expert_in, "dp", axis=1, tiled=True),
-        lax.all_gather(expert_out, "dp", axis=1, tiled=True),
-    )
-    pre_act = jnp.einsum("secd,efd->secf", arrived, full_in, preferred_element_type=jnp.float32)
-    activated = exact_gelu(pre_act).astype(jnp.bfloat16)
-    produced = jnp.einsum(
-        "secf,efd->secd", activated, full_out, preferred_element_type=jnp.float32
-    ).astype(jnp.bfloat16)
-    returned_slots = lax.all_to_all(
-        produced.reshape(owner_count, local_experts * capacity, model_width),
-        "expert",
-        split_axis=0,
-        concat_axis=0,
-        tiled=True,
-    )
-    returned = jnp.dot(
-        slot_hot,
-        returned_slots.reshape(expert_total * capacity, model_width),
-        preferred_element_type=jnp.float32,
-    )
-    output = middle + gate_value[:, None] * returned
-    mixed_out = output.astype(jnp.bfloat16)
+    first_expert = lax.axis_index("expert") * local_experts
+    back_rows, produced_rows, in_grads, out_grads = [], [], [], []
+    router_part = jnp.zeros((model_width, expert_total), jnp.float32)
+    row_sets = []
+    for e in range(local_experts):
+        hot = slot_hot[:, e * part_rows : (e + 1) * part_rows]
+        outgoing = contract_rows(hot, normed2_low).astype(jnp.bfloat16)
+        mine = swap_owner(outgoing.reshape(owner_count, capacity, model_width))
+        row_sets.append([mine] + [to_high(mine, k) for k in range(1, high)])
+    for e in range(local_experts):
+        column = (jnp.arange(expert_total) == first_expert + e).astype(jnp.float32)
+        router_column = jnp.sum(router_weight.astype(jnp.float32) * column[None, :], axis=1)
+        produced, slot_grad, in_part, out_part, router_row = run_expert(
+            e, router_column[None, :], row_sets[e], cot_sets[e], ins, outs
+        )
+        total = slot_grad[0]
+        for k in range(1, high):
+            total = total + to_high(slot_grad[k], -k).astype(jnp.float32)
+        back_rows.append(swap_owner(total.astype(jnp.bfloat16)))
+        total = produced[0]
+        for k in range(1, high):
+            total = total + to_high(produced[k], -k).astype(jnp.float32)
+        produced_rows.append(swap_owner(total.astype(jnp.bfloat16)))
+        for parts, sums in ((in_part, in_grads), (out_part, out_grads)):
+            total = parts[0]
+            for k in range(1, low):
+                total = total + to_low(parts[k], -k).astype(jnp.float32)
+            sums.append(total)
+        router_part = router_part + router_row[0][:, None] * column[None, :]
+    expert_in_grad, expert_out_grad = jnp.stack(in_grads), jnp.stack(out_grads)
     out_grad = cotangent.astype(jnp.float32)
     mean_load = jnp.sum(counts) / expert_total
     load_weight = (
         (jnp.sum(route_float * counts[None, :], axis=1) - mean_load) / mean_load / jnp.sum(counts)
     )
     balance_part = jnp.sum(load_weight * gate_value)
-    gate_grad = jnp.sum(out_grad * returned, axis=1) + load_weight
-    logit_grad = gate_grad * gate_value * (1.0 - gate_value)
-    logit_full = (logit_grad[:, None] * route_float).astype(jnp.bfloat16)
-    router_part = contract_rows(normed2_low, logit_full)
-    normed2_grad = times_transposed(logit_full, router_weight)
-    slot_grad = contract_rows(
-        slot_hot, (gate_value[:, None] * out_grad).astype(jnp.bfloat16)
-    ).astype(jnp.bfloat16)
-    sent_grad = lax.all_to_all(
-        slot_grad.reshape(owner_count, local_experts * capacity, model_width),
-        "expert",
-        split_axis=0,
-        concat_axis=0,
-        tiled=True,
-    )
-    sent_grad = sent_grad.reshape(owner_count, local_experts, capacity, model_width)
-    act_grad = jnp.einsum("secd,efd->secf", sent_grad, full_out, preferred_element_type=jnp.float32)
-    pre_grad = jax.vjp(exact_gelu, pre_act)[1](act_grad)[0].astype(jnp.bfloat16)
-    out_part = jnp.einsum(
-        "secf,secd->efd", activated, sent_grad, preferred_element_type=jnp.float32
-    )
-    in_part = jnp.einsum("secf,secd->efd", pre_grad, arrived, preferred_element_type=jnp.float32)
-    slotted_grad = jnp.einsum(
-        "secf,efd->secd", pre_grad, full_in, preferred_element_type=jnp.float32
-    ).astype(jnp.bfloat16)
-    expert_in_grad, expert_out_grad = (
-        lax.psum_scatter(
-            in_part.astype(jnp.bfloat16), "dp", scatter_dimension=1, tiled=True
-        ).astype(jnp.float32),
-        lax.psum_scatter(
-            out_part.astype(jnp.bfloat16), "dp", scatter_dimension=1, tiled=True
-        ).astype(jnp.float32),
-    )
-    back_grad = lax.all_to_all(
-        slotted_grad.reshape(owner_count, local_experts * capacity, model_width),
-        "expert",
-        split_axis=0,
-        concat_axis=0,
-        tiled=True,
-    )
-    normed2_grad = normed2_grad + jnp.dot(
+    load_grad = load_weight * gate_value * (1.0 - gate_value)
+    load_full = (load_grad[:, None] * route_float).astype(jnp.bfloat16)
+    router_part = router_part + contract_rows(normed2_low, load_full)
+    normed2_grad = times_transposed(load_full, router_weight) + jnp.dot(
         slot_hot,
-        back_grad.reshape(expert_total * capacity, model_width),
+        jnp.concatenate([r.reshape(part_rows, model_width) for r in back_rows]),
         preferred_element_type=jnp.float32,
     )
+    returned = jnp.dot(
+        slot_hot,
+        jnp.concatenate([r.reshape(part_rows, model_width) for r in produced_rows]),
+        preferred_element_type=jnp.float32,
+    )
+    mixed_out = (middle + gate_value[:, None] * returned).astype(jnp.bfloat16)
     middle_part, ln2_gain_part, ln2_bias_part = norm2_pull(normed2_grad)
     middle_grad = out_grad + middle_part
     attn_grad = middle_grad.astype(jnp.bfloat16)

time: 628 us -> 681 us (1.084)
  matrix products: 151 us -> 60.1 us
  Pallas kernels: 56.9 us -> 118 us
  waiting for transfers between devices: 240 us -> 290 us
  starting transfers between devices: 18 us -> 54.7 us
  other arithmetic: 23.1 us -> 39.1 us
  blocking collectives: 96.8 us -> 82.3 us
    ppermute x0 -> x14, waiting for transfers between devices: none -> 197 us  [the longest x6 119 us: on_device(): to_low = lambda a, k: lax.ppermute(a, 'dp', low_shift(dp_count, low, k))]
    dot_general x8 -> x2, matrix products: 106 us -> 8.32 us  [on_device(): jnp.dot(slot_hot, jnp.concatenate([r.reshape(part_rows, model_width) for...]
    reduce_scatter x1, waiting for transfers between devices: 79.7 us -> 0.01 us  [on_device(): lax.psum_scatter(jnp.concatenate([inner_grad, outer_grad], axis=1), ('dp'...]
    pallas_call x0 -> x2, Pallas kernels: none -> 61.4 us  [run_expert(): pl.pallas_call(functools.partial(expert_kernel, nr, nw, tiles), grid=(nw...]
    all_gather x2 -> x0, waiting for transfers between devices: 31 us -> none  [the longest x1 31 us: on_device(): lax.all_gather(expert_out, 'dp', axis=1, tiled=True)]
    all_to_all x4 -> x8, waiting for transfers between devices: 62.4 us -> 36.8 us  [on_device(): lax.all_to_all(a, 'expert', split_axis=0, concat_axis=0, tiled=True)]
    all_to_all x4 -> x8, starting transfers between devices: 17.2 us -> 36.7 us  [on_device(): lax.all_to_all(a, 'expert', split_axis=0, concat_axis=0, tiled=True)]
    ppermute x0 -> x14, starting transfers between devices: none -> 17.8 us  [the longest x8 10 us: on_device(): to_high = lambda a, k: lax.ppermute(a, 'dp', high_shift(dp_count, low, k))]
  transfers between devices with their start and end apart: 10 -> 24, of which waited for: 6 -> 15; matrix products, arithmetic and copies ran while one was open for 30% -> 13% of each run, Pallas kernels for 9% -> 12%
where the time goes in v2:
time: 681 us; the launch traced here: 677 us
  waiting for transfers between devices  290 us (43%)
  Pallas kernels  118 us (17%)
  blocking collectives  82.3 us (12%)
  matrix products  60.1 us (9%)
  starting transfers between devices  54.7 us (8%)
  other arithmetic  39.1 us (6%)
  between operations  16.8 us (2%)
  local copies, waits for them, and re-layouts  14.9 us (2%)
    ppermute x6, waiting for transfers between devices, on_device(): to_low = lambda a, k: lax.ppermute(a, 'dp', low_shift(dp_count, low, k))  119 us
    ppermute x8, waiting for transfers between devices, on_device(): to_high = lambda a, k: lax.ppermute(a, 'dp', high_shift(dp_count, low, k))  77.8 us
    pallas_call x2, Pallas kernels, run_expert(): pl.pallas_call(functools.partial(expert_kernel, nr, nw, tiles), grid=(nw...  61.4 us
    all_gather x1, waiting for transfers between devices, on_device(): lax.all_gather(mixer_weight, ('dp', 'expert'), axis=1, tiled=True)  56 us
    psum x1, blocking collectives, on_device(): lax.psum((ln1_gain_part, ln1_bias_part, ln2_gain_part, ln2_bias_part, rou...  42.2 us
    psum x1, blocking collectives, on_device(): counts = lax.psum(jnp.sum(route_float, axis=0), ('dp', 'expert'))  40.1 us
    all_to_all x8, waiting for transfers between devices, on_device(): lax.all_to_all(a, 'expert', split_axis=0, concat_axis=0, tiled=True)  36.8 us
    all_to_all x8, starting transfers between devices, on_device(): lax.all_to_all(a, 'expert', split_axis=0, concat_axis=0, tiled=True)  36.7 us
  transfers between devices with their start and end apart: 24, of which 15 were waited for; matrix products, arithmetic and copies ran while one was open for 13% of the time, Pallas kernels for 12%

profile of v2, /device:TPU:0, one launch (start us, length us, event | category | flops | bytes accessed | tf_op | source)
XLA Modules:
  0.0 676.5 jit_solution(9349165786097643671)
XLA Ops:
  15.5 6.6 all-to-all-start.4
  24.3 56.0 %all-gather.2.cloned.1.call-done = bf16[768,3072]{0,1:T(8,128)(2,1)} async-done(((bf16[768,96]{0,1:T(8,128)(2,1)}), bf16[768,3072]{0,1:T(8,128)(2,1)}) %all-gather.2.cloned.1.call-update) | async-done | bytes 4718608 | tf_op jit(solution)/shard_map/all_gather | solution.py:297
  80.3 8.1 %convolution_convert_fusion.q_ref.k_ref.v_ref = bf16[1024,2304]{1,0:T(8,128)(2,1)} fusion(bf16[768,3072]{0,1:T(8,128)(2,1)} %all-gather.2.cloned.1.call-done, bf16[1024,768]{0,1:T(8,128)(2,1)S(1)} %copy.24, f32[768]{0:T(1024)S(1)} %copy-done.27, f32[768]{0:T(1024)S(1)} %copy-done.21, f32[1024]{0:T(1024)S(1)} %fusion.62, f32[1024]{0:T(1024)S(1)} %broadcast_multiply_fusion.1), kind=kOutput, calls=%fused_computation.1 | convolution fusion | flops 3630956544 | bytes 9844736 | tf_op jit(solution)/shard_map/dot_general | solution.py:303
  88.4 22.6 %attn_fwd.1 = (bf16[1024,768]{1,0:T(8,128)(2,1)}, f32[6,2,1024]{2,1,0:T(2,128)}) custom-call(s32[1]{0:T(128)S(6)} %copy.41.pre_ref, bf16[1024,2304]{1,0:T(8,128)(2,1)} %convolution_convert_fusion.q_ref.k_ref.v_ref, bf16[1024,2304]{1,0:T(8,128)(2,1)} %convolution_convert_fusion.q_ref.k_ref.v_ref, bf16[1024,2304]{1,0:T(8,128)(2,1)} %convolution_convert_fusion.q_ref.k_ref.v_ref), custom_call_target="tpu_custom_call" | custom-call | tf_op jit(solution)/shard_map/attn_fwd/pallas_call | solution.py:89
  128.8 15.0 %all-to-all-done.3.refs_1_ = bf16[8,64,768]{2,1,0:T(8,128)(2,1)} async-done(((bf16[8,64,768]{2,1,0:T(8,128)(2,1)}), bf16[8,64,768]{2,1,0:T(8,128)(2,1)}, u32[]{:S(2)}, u32[]{:S(2)}) %all-to-all-start.3) | async-done | bytes 786464 | tf_op jit(solution)/shard_map/all_to_all | solution.py:268
  153.8 15.2 %all-to-all-done.1.refs_3_ = bf16[8,64,768]{2,1,0:T(8,128)(2,1)} async-done(((bf16[8,64,768]{2,1,0:T(8,128)(2,1)}), bf16[8,64,768]{2,1,0:T(8,128)(2,1)}, u32[]{:S(2)}, u32[]{:S(2)}) %all-to-all-start.1) | async-done | bytes 786464 | tf_op jit(solution)/shard_map/all_to_all | solution.py:268
  169.0 4.6 all-to-all-start
  177.4 49.9 %collective-permute-done.3.refs_8_ = bf16[2,768,768]{2,1,0:T(8,128)(2,1)} collective-permute-done((bf16[2,768,768]{2,1,0:T(8,128)(2,1)}, bf16[2,768,768]{2,1,0:T(8,128)(2,1)}, u32[]{:S(2)}, u32[]{:S(2)}) %collective-permute-start.3) | collective-permute-done | bytes 2359328 | tf_op jit(solution)/shard_map/ppermute | solution.py:266
  227.3 30.7 %expert.3 = (f32[8,64,768]{2,1,0:T(8,128)}, bf16[8,64,768]{2,1,0:T(8,128)(2,1)}, f32[8,64,768]{2,1,0:T(8,128)}, bf16[8,64,768]{2,1,0:T(8,128)(2,1)}, f32[768,768...) custom-call(f32[1,768]{1,0:T(1,128)} %broadcast_in_dim.13.refs_0_, ...), custom_call_target="tpu_custom_call" | custom-call | flops 14495514624 | bytes 19660800 | tf_op jit(solution)/shard_map/expert/pallas_call | solution.py:227
  262.1 16.6 %collective-permute-done.9 = bf16[8,64,768]{2,1,0:T(8,128)(2,1)} collective-permute-done((bf16[8,64,768]{2,1,0:T(8,128)(2,1)}, bf16[8,64,768]{2,1,0:T(8,128)(2,1)}, u32[]{:S(2)}, u32[]{:S(2)}) %collective-permute-start.9) | collective-permute-done | bytes 786464 | tf_op jit(solution)/shard_map/ppermute | solution.py:267
  281.5 4.8 all-to-all-start.7
  286.2 9.4 %collective-permute-done.1.refs_4_ = bf16[8,64,768]{2,1,0:T(8,128)(2,1)} collective-permute-done((bf16[8,64,768]{2,1,0:T(8,128)(2,1)}, bf16[8,64,768]{2,1,0:T(8,128)(2,1)}, u32[]{:S(2)}, u32[]{:S(2)}) %collective-permute-start.1) | collective-permute-done | bytes 786464 | tf_op jit(solution)/shard_map/ppermute | solution.py:267
  295.6 15.3 %collective-permute-done.refs_2_ = bf16[8,64,768]{2,1,0:T(8,128)(2,1)} collective-permute-done((bf16[8,64,768]{2,1,0:T(8,128)(2,1)}, bf16[8,64,768]{2,1,0:T(8,128)(2,1)}, u32[]{:S(2)}, u32[]{:S(2)}) %collective-permute-start) | collective-permute-done | bytes 786464 | tf_op jit(solution)/shard_map/ppermute | solution.py:267
  311.0 30.7 %expert.2 = (f32[8,64,768]{2,1,0:T(8,128)}, bf16[8,64,768]{2,1,0:T(8,128)(2,1)}, f32[8,64,768]{2,1,0:T(8,128)}, bf16[8,64,768]{2,1,0:T(8,128)(2,1)}, f32[768,768...) custom-call(f32[1,768]{1,0:T(1,128)} %broadcast_in_dim.12.refs_0_, ...), custom_call_target="tpu_custom_call" | custom-call | flops 14495514624 | bytes 19660800 | tf_op jit(solution)/shard_map/expert/pallas_call | solution.py:227
  343.2 16.8 %collective-permute-done.8 = bf16[8,64,768]{2,1,0:T(8,128)(2,1)S(1)} collective-permute-done((bf16[8,64,768]{2,1,0:T(8,128)(2,1)}, bf16[8,64,768]{2,1,0:T(8,128)(2,1)S(1)}, u32[]{:S(2)}, u32[]{:S(2)}) %collective-permute-start.8) | collective-permute-done | bytes 786464 | tf_op jit(solution)/shard_map/ppermute | solution.py:267
  367.1 40.1 %psum.49 = f32[16]{0:T(128)S(1)} all-reduce(f32[16]{0:T(128)S(1)} %convert_reduce_fusion.1), channel_id=1, replica_groups=mesh['dp'=4,'expert'=8] {'dp','expert'}, use_global_device_ids=true, to_apply=%region_9.10 | all-reduce | flops 16 | bytes 128 | tf_op jit(solution)/shard_map/psum | solution.py:274
  427.4 34.3 %attn_bwd.1 = (bf16[1024,768]{1,0:T(8,128)(2,1)}, bf16[1024,768]{1,0:T(8,128)(2,1)}, bf16[1024,768]{1,0:T(8,128)(2,1)}) custom-call(s32[1]{0:T(128)S(6)} %copy.41.pre_ref, bf16[1024,2304]{1,0:T(8,128)(2,1)} %convolution_convert_fusion.q_ref.k_ref.v_ref, bf16[1024,2304]{1,0:T(8,128)(2,1)} %convolution_convert_fusion.q_ref.k_ref.v_ref, ...), custom_call_target="tpu_custom_call" | custom-call | tf_op jit(solution)/shard_map/attn_bwd/pallas_call | solution.py:141
  477.1 16.5 %collective-permute-done.7 = bf16[8,64,768]{2,1,0:T(8,128)(2,1)S(1)} collective-permute-done((bf16[8,64,768]{2,1,0:T(8,128)(2,1)}, bf16[8,64,768]{2,1,0:T(8,128)(2,1)S(1)}, u32[]{:S(2)}, u32[]{:S(2)}) %collective-permute-start.7) | collective-permute-done | bytes 786464 | tf_op jit(solution)/shard_map/ppermute | solution.py:267
  514.9 6.6 all-to-all-done.5
  525.2 7.9 %collective-permute-done.10 = bf16[768,768]{1,0:T(8,128)(2,1)} collective-permute-done((bf16[768,768]{1,0:T(8,128)(2,1)}, bf16[768,768]{1,0:T(8,128)(2,1)}, u32[]{:S(2)}, u32[]{:S(2)}) %collective-permute-start.10) | collective-permute-done | bytes 1179680 | tf_op jit(solution)/shard_map/ppermute | solution.py:266
  537.9 25.6 %collective-permute-done.13 = bf16[768,768]{1,0:T(8,128)(2,1)} collective-permute-done((bf16[768,768]{1,0:T(8,128)(2,1)}, bf16[768,768]{1,0:T(8,128)(2,1)}, u32[]{:S(2)}, u32[]{:S(2)}) %collective-permute-start.13) | collective-permute-done | bytes 1179680 | tf_op jit(solution)/shard_map/ppermute | solution.py:266
  565.0 31.8 %collective-permute-done.12 = bf16[768,768]{1,0:T(8,128)(2,1)} collective-permute-done((bf16[768,768]{1,0:T(8,128)(2,1)}, bf16[768,768]{1,0:T(8,128)(2,1)}, u32[]{:S(2)}, u32[]{:S(2)}) %collective-permute-start.12) | collective-permute-done | bytes 1179680 | tf_op jit(solution)/shard_map/ppermute | solution.py:266
  602.1 4.6 add_convert_fusion
  627.2 42.2 %all-reduce = (f32[768]{0:T(1024)}, f32[768]{0:T(1024)}, f32[768]{0:T(1024)}, f32[768]{0:T(1024)}, f32[768,16]{0,1:T(8,128)}, /*index=5*/f32[]{:T(128)}) all-reduce(f32[768]{0:T(1024)S(1)} %get-tuple-element.70, f32[768]{0:T(1024)S(1)} %get-tuple-element.73, ...), channel_id=1, replica_groups=mesh['dp'=4,'expert'=8] {'dp','expert'}, use_global_device_ids=true, to_apply=%region_17.18 | all-reduce | flops 15361 | bytes 122888 | tf_op jit(solution)/shard_map/psum | solution.py:383
  (154 shorter events, 147.7 us)
Async XLA Ops:
  7.2 73.1 %all-gather.2.cloned.1.call-start = ((), (), s32[]{:S(2)}) async-start(), calls=%async_computation.9 | async-start | bytes 4866048 | tf_op jit(solution)/shard_map/all_gather | solution.py:297
  15.5 103.1 %all-to-all-start.4 = ((bf16[8,64,768]{2,1,0:T(8,128)(2,1)}), bf16[8,64,768]{2,1,0:T(8,128)(2,1)}, u32[]{:S(2)}, u32[]{:S(2)}) async-start(bf16[8,64,768]{2,1,0:T(8,128)(2,1)} %bitcast.40), calls=%async_computation.4 | async-start | bytes 1572864 | tf_op jit(solution)/shard_map/all_to_all | solution.py:268
  118.6 25.2 %all-to-all-start.3 = ((bf16[8,64,768]{2,1,0:T(8,128)(2,1)}), bf16[8,64,768]{2,1,0:T(8,128)(2,1)}, u32[]{:S(2)}, u32[]{:S(2)}) async-start(bf16[8,64,768]{2,1,0:T(8,128)(2,1)} %bitcast.41), calls=%async_computation.3 | async-start | bytes 1572864 | tf_op jit(solution)/shard_map/all_to_all | solution.py:268
  122.9 54.5 %collective-permute-start.2 = (bf16[2,768,768]{2,1,0:T(8,128)(2,1)}, bf16[2,768,768]{2,1,0:T(8,128)(2,1)}, u32[]{:S(2)}, u32[]{:S(2)}) collective-permute-start(bf16[2,768,768]{2,1,0:T(8,128)(2,1)} %refs_5_.3), channel_id=1, source_target_pairs={{0,8},{8,0},{16,24},{24,16},{1,9},{9,1},{17,25},{25,17},{2,10},{10... | collective-permute-start | bytes 7077896 | tf_op jit(solution)/shard_map/ppermute | solution.py:266
  124.4 102.9 %collective-permute-start.3 = (bf16[2,768,768]{2,1,0:T(8,128)(2,1)}, bf16[2,768,768]{2,1,0:T(8,128)(2,1)}, u32[]{:S(2)}, u32[]{:S(2)}) collective-permute-start(bf16[2,768,768]{2,1,0:T(8,128)(2,1)} %refs_7_.3), channel_id=1, source_target_pairs={{0,8},{8,0},{16,24},{24,16},{1,9},{9,1},{17,25},{25,17},{2,10},{10... | collective-permute-start | bytes 7077896 | tf_op jit(solution)/shard_map/ppermute | solution.py:266
  143.8 25.2 %all-to-all-start.1 = ((bf16[8,64,768]{2,1,0:T(8,128)(2,1)}), bf16[8,64,768]{2,1,0:T(8,128)(2,1)}, u32[]{:S(2)}, u32[]{:S(2)}) async-start(bf16[8,64,768]{2,1,0:T(8,128)(2,1)} %bitcast.39), calls=%async_computation.1 | async-start | bytes 1572864 | tf_op jit(solution)/shard_map/all_to_all | solution.py:268
  148.1 25.6 %collective-permute-start.6 = (bf16[8,64,768]{2,1,0:T(8,128)(2,1)}, bf16[8,64,768]{2,1,0:T(8,128)(2,1)}, u32[]{:S(2)}, u32[]{:S(2)}) collective-permute-start(bf16[8,64,768]{2,1,0:T(8,128)(2,1)} %all-to-all-done.4.refs_3_), channel_id=1, source_target_pairs={{0,16},{8,24},{16,0},{24,8},{1,17},{9,25},{17,1},{25,9},{2,18},{10... | collective-permute-start | bytes 2359304 | tf_op jit(solution)/shard_map/ppermute | solution.py:267
  149.6 77.7 %collective-permute-start.5 = (bf16[8,64,768]{2,1,0:T(8,128)(2,1)}, bf16[8,64,768]{2,1,0:T(8,128)(2,1)}, u32[]{:S(2)}, u32[]{:S(2)}) collective-permute-start(bf16[8,64,768]{2,1,0:T(8,128)(2,1)} %all-to-all-done.3.refs_1_), channel_id=1, source_target_pairs={{0,16},{8,24},{16,0},{24,8},{1,17},{9,25},{17,1},{25,9},{2,18},{10... | collective-permute-start | bytes 2359304 | tf_op jit(solution)/shard_map/ppermute | solution.py:267
  169.0 91.1 %all-to-all-start = ((bf16[8,64,768]{2,1,0:T(8,128)(2,1)}), bf16[8,64,768]{2,1,0:T(8,128)(2,1)}, u32[]{:S(2)}, u32[]{:S(2)}) async-start(bf16[8,64,768]{2,1,0:T(8,128)(2,1)} %bitcast.37), calls=%async_computation | async-start | bytes 1572864 | tf_op jit(solution)/shard_map/all_to_all | solution.py:268
  258.0 20.8 %collective-permute-start.9 = (bf16[8,64,768]{2,1,0:T(8,128)(2,1)}, bf16[8,64,768]{2,1,0:T(8,128)(2,1)}, u32[]{:S(2)}, u32[]{:S(2)}) collective-permute-start(bf16[8,64,768]{2,1,0:T(8,128)(2,1)} %get-tuple-element.42), channel_id=1, source_target_pairs={{0,16},{8,24},{16,0},{24,8},{1,17},{9,25},{17,1},{25,9},{2,18},{10... | collective-permute-start | bytes 2359304 | tf_op jit(solution)/shard_map/ppermute | solution.py:267
  259.5 36.1 %collective-permute-start.1 = (bf16[8,64,768]{2,1,0:T(8,128)(2,1)}, bf16[8,64,768]{2,1,0:T(8,128)(2,1)}, u32[]{:S(2)}, u32[]{:S(2)}) collective-permute-start(bf16[8,64,768]{2,1,0:T(8,128)(2,1)} %all-to-all-done.1.refs_3_), channel_id=1, source_target_pairs={{0,16},{8,24},{16,0},{24,8},{1,17},{9,25},{17,1},{25,9},{2,18},{10... | collective-permute-start | bytes 2359304 | tf_op jit(solution)/shard_map/ppermute | solution.py:267
  260.1 50.9 %collective-permute-start = (bf16[8,64,768]{2,1,0:T(8,128)(2,1)}, bf16[8,64,768]{2,1,0:T(8,128)(2,1)}, u32[]{:S(2)}, u32[]{:S(2)}) collective-permute-start(bf16[8,64,768]{2,1,0:T(8,128)(2,1)} %all-to-all-done.refs_1_), channel_id=1, source_target_pairs={{0,16},{8,24},{16,0},{24,8},{1,17},{9,25},{17,1},{25,9},{2,18},{10... | collective-permute-start | bytes 2359304 | tf_op jit(solution)/shard_map/ppermute | solution.py:267
  281.5 81.1 %all-to-all-start.7 = ((bf16[8,64,768]{2,1,0:T(8,128)(2,1)}), bf16[8,64,768]{2,1,0:T(8,128)(2,1)}, u32[]{:S(2)}, u32[]{:S(2)}) async-start(bf16[8,64,768]{2,1,0:T(8,128)(2,1)} %add_convert_fusion.2), calls=%async_computation.7 | async-start | bytes 1572864 | tf_op jit(solution)/shard_map/all_to_all | solution.py:268
  341.7 18.3 %collective-permute-start.8 = (bf16[8,64,768]{2,1,0:T(8,128)(2,1)}, bf16[8,64,768]{2,1,0:T(8,128)(2,1)S(1)}, u32[]{:S(2)}, u32[]{:S(2)}) collective-permute-start(bf16[8,64,768]{2,1,0:T(8,128)(2,1)} %get-tuple-element.40), channel_id=1, source_target_pairs={{0,16},{8,24},{16,0},{24,8},{1,17},{9,25},{17,1},{25,9},{2,18},{10... | collective-permute-start | bytes 2359304 | tf_op jit(solution)/shard_map/ppermute | solution.py:267
  362.6 49.6 %all-to-all-start.6 = ((bf16[8,64,768]{2,1,0:T(8,128)(2,1)}), bf16[8,64,768]{2,1,0:T(8,128)(2,1)}, u32[]{:S(2)}, u32[]{:S(2)}) async-start(bf16[8,64,768]{2,1,0:T(8,128)(2,1)} %add_convert_fusion.3), calls=%async_computation.6 | async-start | bytes 1572864 | tf_op jit(solution)/shard_map/all_to_all | solution.py:268
  366.9 302.5 %reduce-scatter.2.cloned.1.call-start = ((), (), s32[]{:S(2)}) async-start(), calls=%async_computation.10 | async-start | bytes 9732096 | tf_op jit(solution)/shard_map/reduce_scatter | solution.py:377
  472.8 20.9 %collective-permute-start.7 = (bf16[8,64,768]{2,1,0:T(8,128)(2,1)}, bf16[8,64,768]{2,1,0:T(8,128)(2,1)S(1)}, u32[]{:S(2)}, u32[]{:S(2)}) collective-permute-start(bf16[8,64,768]{2,1,0:T(8,128)(2,1)} %get-tuple-element.38), channel_id=1, source_target_pairs={{0,16},{8,24},{16,0},{24,8},{1,17},{9,25},{17,1},{25,9},{2,18},{10... | collective-permute-start | bytes 2359304 | tf_op jit(solution)/shard_map/ppermute | solution.py:267
  475.1 36.7 %collective-permute-start.11 = (bf16[768,768]{1,0:T(8,128)(2,1)}, bf16[768,768]{1,0:T(8,128)(2,1)}, u32[]{:S(2)}, u32[]{:S(2)}) collective-permute-start(bf16[768,768]{1,0:T(8,128)(2,1)} %get-tuple-element.52), channel_id=1, source_target_pairs={{0,8},{8,0},{16,24},{24,16},{1,9},{9,1},{17,25},{25,17},{2,10},{10... | collective-permute-start | bytes 3538952 | tf_op jit(solution)/shard_map/ppermute | solution.py:266
  476.6 32.4 %collective-permute-start.4 = (bf16[8,64,768]{2,1,0:T(8,128)(2,1)}, bf16[8,64,768]{2,1,0:T(8,128)(2,1)}, u32[]{:S(2)}, u32[]{:S(2)}) collective-permute-start(bf16[8,64,768]{2,1,0:T(8,128)(2,1)} %get-tuple-element.36), channel_id=1, source_target_pairs={{0,16},{8,24},{16,0},{24,8},{1,17},{9,25},{17,1},{25,9},{2,18},{10... | collective-permute-start | bytes 2359304 | tf_op jit(solution)/shard_map/ppermute | solution.py:267
  496.3 25.2 %all-to-all-start.5 = ((bf16[8,64,768]{2,1,0:T(8,128)(2,1)}), bf16[8,64,768]{2,1,0:T(8,128)(2,1)}, u32[]{:S(2)}, u32[]{:S(2)}) async-start(bf16[8,64,768]{2,1,0:T(8,128)(2,1)} %add_convert_fusion.4), calls=%async_computation.5 | async-start | bytes 1572864 | tf_op jit(solution)/shard_map/all_to_all | solution.py:268
  500.5 32.6 %collective-permute-start.10 = (bf16[768,768]{1,0:T(8,128)(2,1)}, bf16[768,768]{1,0:T(8,128)(2,1)}, u32[]{:S(2)}, u32[]{:S(2)}) collective-permute-start(bf16[768,768]{1,0:T(8,128)(2,1)} %get-tuple-element.50), channel_id=1, source_target_pairs={{0,8},{8,0},{16,24},{24,16},{1,9},{9,1},{17,25},{25,17},{2,10},{10... | collective-permute-start | bytes 3538952 | tf_op jit(solution)/shard_map/ppermute | solution.py:266
  503.2 60.2 %collective-permute-start.13 = (bf16[768,768]{1,0:T(8,128)(2,1)}, bf16[768,768]{1,0:T(8,128)(2,1)}, u32[]{:S(2)}, u32[]{:S(2)}) collective-permute-start(bf16[768,768]{1,0:T(8,128)(2,1)} %get-tuple-element.56), channel_id=1, source_target_pairs={{0,8},{8,0},{16,24},{24,16},{1,9},{9,1},{17,25},{25,17},{2,10},{10... | collective-permute-start | bytes 3538952 | tf_op jit(solution)/shard_map/ppermute | solution.py:266
  503.3 93.5 %collective-permute-start.12 = (bf16[768,768]{1,0:T(8,128)(2,1)}, bf16[768,768]{1,0:T(8,128)(2,1)}, u32[]{:S(2)}, u32[]{:S(2)}) collective-permute-start(bf16[768,768]{1,0:T(8,128)(2,1)} %get-tuple-element.54), channel_id=1, source_target_pairs={{0,8},{8,0},{16,24},{24,16},{1,9},{9,1},{17,25},{25,17},{2,10},{10... | collective-permute-start | bytes 3538952 | tf_op jit(solution)/shard_map/ppermute | solution.py:266
  521.4 79.7 %all-to-all-start.2 = ((bf16[8,64,768]{2,1,0:T(8,128)(2,1)}), bf16[8,64,768]{2,1,0:T(8,128)(2,1)S(1)}, u32[]{:S(2)}, u32[]{:S(2)}) async-start(bf16[8,64,768]{2,1,0:T(8,128)(2,1)} %add_convert_fusion.5), calls=%async_computation.2 | async-start | bytes 1572864 | tf_op jit(solution)/shard_map/all_to_all | solution.py:268
  (28 other events, 382.2 us)
Sparse Core Ops, SparseCore 0:
  11.0 69.2 all-gather.1
  472.9 164.1 reduce-scatter.1

commit v3 on v2

--- a/solution.py
+++ b/solution.py
@@ -187,7 +187,7 @@
     for w in range(nw):
         @pl.when(step//tiles==w)
         def _(w=w):
-            wi=wi_refs[w][0]; wo=wo_refs[w][0]
+            wi=wi_refs[w][...]; wo=wo_refs[w][...]
             pre=nt(x_s[...],wi)
             da=nt(g_s[...],wo)
             phi=0.5+0.5*erf32(pre*0.7071067811865476)
@@ -213,19 +213,19 @@
 
 def run_expert(e,rw,xs,cs,wis,wos):
     nr,nw=len(xs),len(wis)
-    S,C,D=xs[0].shape; Q=wis[0].shape[1]; R=nr*S*C
+    S,C,D=xs[0].shape; Q=wis[0].shape[0]; R=nr*S*C
     tile=Q
     for t in (384,256,192,128):
         if Q%t==0: tile=t; break
     tiles=Q//tile
     whole=lambda shape: pl.BlockSpec(shape,lambda i:(0,)*len(shape))
     at=lambda w: (lambda i: jnp.clip(i-w*tiles,0,tiles-1))
-    wspec=lambda w: pl.BlockSpec((1,tile,D),lambda i,f=at(w):(e,f(i),0))
+    wspec=lambda w: pl.BlockSpec((tile,D),lambda i,f=at(w):(f(i),0))
     gspec=lambda w: pl.BlockSpec((tile,D),lambda i,f=at(w):(f(i),0))
     rows_spec=whole((S,C,D))
     kind=lambda k: F32 if k==0 else BF
     outs=pl.pallas_call(functools.partial(expert_kernel,nr,nw,tiles),grid=(nw*tiles,),
-        in_specs=[whole((1,D))]+[rows_spec]*(2*nr)+[wspec(w) for w in range(nw)]*2,
+        in_specs=[whole((1,D))]+[rows_spec]*nr+[pl.BlockSpec((S,1,C,D),lambda i:(0,e,0,0))]*nr+[wspec(w) for w in range(nw)]*2,
         out_specs=[rows_spec]*(2*nr)+[gspec(w) for w in range(nw)]*2+[whole((1,D))],
         out_shape=[jax.ShapeDtypeStruct((S,C,D),kind(r)) for r in range(nr)]*2
           +[jax.ShapeDtypeStruct((Q,D),kind(w)) for w in range(nw)]*2+[jax.ShapeDtypeStruct((1,D),F32)],
@@ -234,6 +234,181 @@
         cost_estimate=pl.CostEstimate(flops=12*R*nw*Q*D,bytes_accessed=nw*Q*D*10+R*D*10,transcendentals=R*nw*Q),
         name="expert")(rw,*xs,*cs,*wis,*wos)
     return outs[:nr],outs[nr:2*nr],outs[2*nr:2*nr+nw],outs[2*nr+nw:2*nr+2*nw],outs[-1]
+
+MESH=pl.DeviceIdType.MESH
+
+class Grid:
+    def __init__(self):
+        self.dp=lax.axis_size("dp"); self.expert=lax.axis_size("expert")
+        bits=lambda n: n.bit_length()-1
+        dp_bits=[("dp",1<<i) for i in range(bits(self.dp))]
+        ex_bits=[("expert",1<<i) for i in range(bits(self.expert))]
+        h=len(dp_bits)//2
+        xs,ys,zs=dp_bits[:h],dp_bits[h:],ex_bits[1:]
+        self.core=ex_bits[0]
+        self.orders=[xs+ys+zs,ys+xs+zs,zs+xs+ys]
+        self.all_bits=[self.core]+zs+xs+ys
+    def here(self): self.at={"dp":lax.axis_index("dp"),"expert":lax.axis_index("expert")}
+    def flip(self,k): return (1-2*(self.at[k[0]]//k[1]%2))*k[1]
+    def partner(self,k): return {k[0]:self.at[k[0]]+self.flip(k)}
+    def block(self,place):
+        dp,ex=self.at["dp"],self.at["expert"]
+        for k in place:
+            if k[0]=="dp": dp=dp+self.flip(k)
+            else: ex=ex+self.flip(k)
+        return dp*self.expert+ex
+    def greet(self):
+        barrier=pltpu.get_barrier_semaphore()
+        for k in self.all_bits: pl.semaphore_signal(barrier,inc=1,device_id=self.partner(k),device_id_type=MESH)
+        pl.semaphore_wait(barrier,len(self.all_bits))
+
+def place_of(order,code):
+    m=len(order)
+    return frozenset(order[i] for i in range(m) if code>>(m-1-i)&1)
+
+class SmallSum:
+    def __init__(self,g,small_ref,sum_ref,buf,arrive,ssem,rsem):
+        self.g,self.sum_ref,self.buf,self.arrive,self.ssem,self.rsem=g,sum_ref,buf,arrive,ssem,rsem
+        self.i=0
+        buf[0]=small_ref[...]
+    def start(self):
+        i=self.i
+        self.copy=pltpu.make_async_remote_copy(self.buf.at[i],self.arrive.at[i],self.ssem.at[i],self.rsem.at[i],device_id=self.g.partner(self.g.all_bits[i]),device_id_type=MESH)
+        self.copy.start()
+    def step(self):
+        i=self.i
+        if i>=len(self.g.all_bits): return
+        self.copy.wait()
+        v=self.buf[i]+self.arrive[i]
+        self.i=i+1
+        if self.i<len(self.g.all_bits): self.buf[i+1]=v; self.start()
+        else: self.sum_ref[...]=v
+
+def gather_kernel(w_ref,small_ref,out_ref,sum_ref,s_buf,s_in,ssem,rsem,cs,cr,sssem,srsem):
+    g=Grid(); g.here(); g.greet()
+    small=SmallSum(g,small_ref,sum_ref,s_buf,s_in,sssem,srsem)
+    D=w_ref.shape[1]; n=len(g.orders); L=D//n
+    chip=g.orders[0]; number={place_of(chip,c):c for c in range(1<<len(chip))}
+    out_ref[g.block(())]=w_ref[...]
+    sends=[]; core_in=[]
+    def view(o,place): return out_ref.at[g.block(place),:,o*L:(o+1)*L]
+    def source(o,place): return view(o,place) if place else w_ref.at[:,o*L:(o+1)*L]
+    def send(o,place,k):
+        to=number[place^{k}]
+        c=pltpu.make_async_remote_copy(source(o,place),view(o,place),ssem.at[o,to],rsem.at[o,to],device_id=g.partner(k),device_id_type=MESH)
+        c.start(); sends.append(c)
+    def arrived(o,place,k):
+        i=number[place]
+        pltpu.make_async_remote_copy(view(o,place),view(o,place),ssem.at[o,i],rsem.at[o,i],device_id=g.partner(k),device_id_type=MESH).wait_recv()
+    def across(o,place):
+        i=number[place]
+        c=pltpu.make_async_remote_copy(source(o,place),view(o,place),cs.at[o,i],cr.at[o,i],device_id=g.partner(g.core),device_id_type=MESH)
+        c.start(); sends.append(c)
+        v=view(o,place|{g.core})
+        core_in.append(pltpu.make_async_remote_copy(v,v,cs.at[o,i],cr.at[o,i],device_id=g.partner(g.core),device_id_type=MESH))
+    m=len(chip)
+    held=[[frozenset()] for _ in g.orders]
+    fresh=[[] for _ in g.orders]
+    for j in range(m):
+        for o,order in enumerate(g.orders):
+            k=order[m-1-j]
+            for p in held[o]: send(o,p,k)
+            if j==0: across(o,frozenset())
+        if j==0: small.start()
+        else: small.step()
+        for o,order in enumerate(g.orders):
+            k=order[m-1-j]
+            for p in fresh[o]:
+                arrived(o,p,order[m-j]); send(o,p,k); across(o,p)
+            held[o]=held[o]+fresh[o]
+            fresh[o]=[p|{k} for p in held[o]]
+    for i in range(len(fresh[0])):
+        for o,order in enumerate(g.orders):
+            arrived(o,fresh[o][i],order[0]); across(o,fresh[o][i])
+    for _ in g.all_bits: small.step()
+    for c in core_in: c.wait_recv()
+    for c in sends: c.wait_send()
+
+def gather_mixer(w,small):
+    g=Grid(); n=g.dp*g.expert; half=n//2; k=len(g.orders); nb=len(g.all_bits)
+    V=pl.BlockSpec(memory_space=pltpu.VMEM); S=pltpu.SemaphoreType.DMA
+    D=w.shape[1]
+    return pl.pallas_call(gather_kernel,
+        in_specs=[V,V],out_specs=[V,V],
+        out_shape=[jax.ShapeDtypeStruct((n,)+w.shape,w.dtype),jax.ShapeDtypeStruct(small.shape,F32)],
+        scratch_shapes=[pltpu.VMEM((nb,)+small.shape,F32)]*2+[S((k,half))]*4+[S((nb,))]*2,
+        compiler_params=pltpu.CompilerParams(collective_id=0,has_side_effects=True,vmem_limit_bytes=60<<20),
+        cost_estimate=pl.CostEstimate(flops=0,bytes_accessed=n*w.size*2,transcendentals=0),
+        name="gather_mixer")(w,small)
+
+def scatter_kernel(g_ref,small_ref,out_ref,sum_ref,c_in,acc,out_buf,in_buf,s_buf,s_in,csem,crem,ssem,rsem,sssem,srsem):
+    g=Grid(); g.here(); g.greet()
+    D=g_ref.shape[2]; n=len(g.orders); L=D//n
+    chip=g.orders[0]; m=len(chip); full=1<<m
+    number={place_of(chip,c):c for c in range(full)}
+    sends=[]; here=set(); pending=[]
+    def flush():
+        for c in pending: c.start(); sends.append(c)
+        pending.clear()
+    small=SmallSum(g,small_ref,sum_ref,s_buf,s_in,sssem,srsem)
+    cross=[]
+    for s in range(full-1,-1,-1):
+        for order in g.orders:
+            p=place_of(order,s)
+            if p in cross: continue
+            cross.append(p)
+    for p in cross:
+        i=number[p]
+        c=pltpu.make_async_remote_copy(g_ref.at[g.block(p|{g.core})],c_in.at[i],csem.at[i],crem.at[i],device_id=g.partner(g.core),device_id_type=MESH)
+        c.start(); sends.append(c)
+    small.start()
+    def first(o,s):
+        p=place_of(g.orders[o],s); i=number[p]
+        if p not in here:
+            here.add(p)
+            pltpu.make_async_remote_copy(c_in.at[i],c_in.at[i],csem.at[i],crem.at[i],device_id=g.partner(g.core),device_id_type=MESH).wait_recv()
+        lanes=slice(o*L,(o+1)*L)
+        return g_ref[g.block(p),:,lanes].astype(F32)+c_in[i,:,lanes].astype(F32)
+    def send(o,s,j,v):
+        out_buf[o,s]=v.astype(BF)
+        flush()
+        pending.append(pltpu.make_async_remote_copy(out_buf.at[o,s],in_buf.at[o,s],ssem.at[o,s],rsem.at[o,s],device_id=g.partner(g.orders[o][j]),device_id_type=MESH))
+    def arrived(o,s,j):
+        pltpu.make_async_remote_copy(out_buf.at[o,s],in_buf.at[o,s],ssem.at[o,s],rsem.at[o,s],device_id=g.partner(g.orders[o][j]),device_id_type=MESH).wait_recv()
+        return in_buf[o,s].astype(F32)
+    half=full//2
+    for s in range(full-1,half-1,-1):
+        for o in range(n): send(o,s,0,first(o,s))
+    flush()
+    for s in range(half-1,-1,-1):
+        for o in range(n): acc[o,s]=first(o,s)
+    small.step()
+    for j in range(1,m):
+        half=full>>(j+1)
+        for s in range(2*half-1,half-1,-1):
+            for o in range(n): send(o,s,j,acc[o,s]+arrived(o,s+2*half,j-1))
+        flush()
+        for s in range(half-1,-1,-1):
+            for o in range(n): acc[o,s]+=arrived(o,s+2*half,j-1)
+        small.step()
+    for o in range(n): out_ref[:,o*L:(o+1)*L]=acc[o,0]+arrived(o,1,m-1)
+    for _ in g.all_bits: small.step()
+    for c in sends: c.wait_send()
+
+def scatter_mixer(grad,small):
+    g=Grid(); n=len(g.orders); full=1<<len(g.orders[0]); nb=len(g.all_bits)
+    _,w,D=grad.shape; L=D//n
+    V=pl.BlockSpec(memory_space=pltpu.VMEM); S=pltpu.SemaphoreType.DMA
+    return pl.pallas_call(scatter_kernel,in_specs=[V,V],out_specs=[V,V],
+        out_shape=[jax.ShapeDtypeStruct((w,D),F32),jax.ShapeDtypeStruct(small.shape,F32)],
+        scratch_shapes=[pltpu.VMEM((full,w,D),BF),pltpu.VMEM((n,full//2,w,L),F32),pltpu.VMEM((n,full,w,L),BF),pltpu.VMEM((n,full,w,L),BF),
+          pltpu.VMEM((nb,)+small.shape,F32),pltpu.VMEM((nb,)+small.shape,F32),
+          S((full,)),S((full,)),S((n,full)),S((n,full)),S((nb,)),S((nb,))],
+        compiler_params=pltpu.CompilerParams(collective_id=1,has_side_effects=True,vmem_limit_bytes=60<<20),
+        cost_estimate=pl.CostEstimate(flops=0,bytes_accessed=grad.size*4,transcendentals=0),
+        name="scatter_mixer")(grad,small)
+
+def tie(*xs): return lax.optimization_barrier(xs)
 
 def low_shift(n,nx,k): return [(i,i//nx*nx+(i%nx+k)%nx) for i in range(n)]
 def high_shift(n,nx,k): return [(i,(i+k*nx)%n) for i in range(n)]
@@ -266,12 +441,13 @@
     to_low = lambda a, k: lax.ppermute(a, "dp", low_shift(dp_count, low, k))
     to_high = lambda a, k: lax.ppermute(a, "dp", high_shift(dp_count, low, k))
     swap_owner = lambda a: lax.all_to_all(a, "expert", split_axis=0, concat_axis=0, tiled=True)
-    ins = [expert_in] + [to_low(expert_in, k) for k in range(1, low)]
-    outs = [expert_out] + [to_low(expert_out, k) for k in range(1, low)]
     route_flat = routes[:, 0]
     route_hot = route_flat[:, None] == jnp.arange(expert_total)[None, :]
     route_float = route_hot.astype(jnp.float32)
-    counts = lax.psum(jnp.sum(route_float, axis=0), ("dp", "expert"))
+    count_pad = jnp.pad(jnp.sum(route_float, axis=0)[None, :], ((0, 7), (0, 128 - expert_total)))
+    gathered, count_sum = gather_mixer(mixer_weight.T, count_pad)
+    counts = count_sum[0, :expert_total]
+    full_mixer = gathered.reshape(4 * model_width, model_width)
     earlier = (slot_order[None, :] < slot_order[:, None]).astype(jnp.bfloat16)
     ahead_count = jnp.dot(
         earlier, route_hot.astype(jnp.bfloat16), preferred_element_type=jnp.float32
@@ -285,26 +461,30 @@
     slot_hot = (
         (slot_index[:, None] == jnp.arange(expert_total * capacity)[None, :]) & is_kept[:, None]
     ).astype(jnp.bfloat16)
-    cot_sets = []
-    for e in range(local_experts):
-        hot = slot_hot[:, e * part_rows : (e + 1) * part_rows]
-        mine = swap_owner(
-            contract_rows(hot, cotangent)
-            .astype(jnp.bfloat16)
-            .reshape(owner_count, capacity, model_width)
-        )
-        cot_sets.append([mine] + [to_high(mine, k) for k in range(1, high)])
-    full_mixer = lax.all_gather(mixer_weight, ("dp", "expert"), axis=1, tiled=True)
-    inner_weight = full_mixer[:, : 3 * model_width]
-    outer_weight = full_mixer[:, 3 * model_width :]
+    experts = range(local_experts)
+    outgoing = contract_rows(slot_hot, cotangent).astype(jnp.bfloat16)
+    outgoing, *shards, full_mixer = tie(
+        outgoing,
+        *[expert_in[e] for e in experts],
+        *[expert_out[e] for e in experts],
+        full_mixer,
+    )
+    cot_home = swap_owner(
+        outgoing.reshape(local_experts, owner_count, capacity, model_width)
+        .transpose(1, 0, 2, 3)
+        .reshape(owner_count, local_experts * capacity, model_width)
+    )
+    ins = [[a] + [to_low(a, k) for k in range(1, low)] for a in shards[:local_experts]]
+    outs = [[a] + [to_low(a, k) for k in range(1, low)] for a in shards[local_experts:]]
+    inner_weight = full_mixer[: 3 * model_width]
+    outer_weight = full_mixer[3 * model_width :]
     inputs = tokens.astype(jnp.float32)
     normed, norm_pull = jax.vjp(layer_norm, inputs, ln1_gain, ln1_bias)
     normed_low = normed.astype(jnp.bfloat16)
-    projected = jnp.dot(normed_low, inner_weight, preferred_element_type=jnp.float32).astype(
-        jnp.bfloat16
-    )
+    projected = times_transposed(normed_low, inner_weight).astype(jnp.bfloat16)
     attended, head_lse = attn_fwd(prefix_len, projected)
-    middle = inputs + jnp.dot(attended, outer_weight, preferred_element_type=jnp.float32)
+    attended, *ins[0] = tie(attended, *ins[0])
+    middle = inputs + times_transposed(attended, outer_weight)
     normed2, norm2_pull = jax.vjp(layer_norm, middle, ln2_gain, ln2_bias)
     normed2_low = normed2.astype(jnp.bfloat16)
     chosen = jnp.sum(
@@ -312,35 +492,60 @@
     )
     gate_value = jax.nn.sigmoid(chosen)
     first_expert = lax.axis_index("expert") * local_experts
-    back_rows, produced_rows, in_grads, out_grads = [], [], [], []
+    grad_rows, produced_parts, moved, in_grads, out_grads = [], [], [], [], []
     router_part = jnp.zeros((model_width, expert_total), jnp.float32)
-    row_sets = []
-    for e in range(local_experts):
+    normed2_low, cot_home = tie(normed2_low, cot_home)
+    cot_rows = [cot_home] + [to_high(cot_home, k) for k in range(1, high)]
+    cot_sets = [
+        [
+            a.reshape(owner_count, local_experts, capacity, model_width)
+            for a in cot_rows
+        ]
+        for e in experts
+    ]
+    home = []
+    for e in experts:
         hot = slot_hot[:, e * part_rows : (e + 1) * part_rows]
-        outgoing = contract_rows(hot, normed2_low).astype(jnp.bfloat16)
-        mine = swap_owner(outgoing.reshape(owner_count, capacity, model_width))
-        row_sets.append([mine] + [to_high(mine, k) for k in range(1, high)])
-    for e in range(local_experts):
+        source = normed2_low
+        if e == 1:
+            source, *outs[0] = tie(normed2_low, *outs[0])
+        outgoing = contract_rows(hot, source).astype(jnp.bfloat16)
+        home.append(swap_owner(outgoing.reshape(owner_count, capacity, model_width)))
+    row_sets = [[a] + [to_high(a, k) for k in range(1, high)] for a in home]
+    tied = tie(*row_sets[0], *home[1:], *[a for e in experts[1:] for a in ins[e]])
+    row_sets[0], tied = list(tied[:high]), tied[high:]
+    for e in range(1, local_experts):
+        row_sets[e][0] = tied[e - 1]
+        ins[e] = list(tied[local_experts - 1 + (e - 1) * low :][:low])
+    for e in experts:
         column = (jnp.arange(expert_total) == first_expert + e).astype(jnp.float32)
         router_column = jnp.sum(router_weight.astype(jnp.float32) * column[None, :], axis=1)
         produced, slot_grad, in_part, out_part, router_row = run_expert(
-            e, router_column[None, :], row_sets[e], cot_sets[e], ins, outs
+            e, router_column[None, :], row_sets[e], cot_sets[e], ins[e], outs[e]
         )
-        total = slot_grad[0]
+        grad_rows.append(slot_grad)
+        produced_parts.append(produced)
+        moved.append([to_high(slot_grad[k], -k) for k in range(1, high)])
+        for parts, sums in ((in_part, in_grads), (out_part, out_grads)):
+            sums.append([parts[0]] + [to_low(parts[k], -k) for k in range(1, low)])
+        router_part = router_part + router_row[0][:, None] * column[None, :]
+    router_part, *held = tie(router_part, *[a for e in experts[:-1] for a in moved[e]])
+    moved[:-1] = [held[e * (high - 1) : (e + 1) * (high - 1)] for e in experts[:-1]]
+    back_rows = []
+    for e in experts:
+        total = grad_rows[e][0]
+        for a in moved[e]:
+            total = total + a.astype(jnp.float32)
+        back_rows.append(swap_owner(total.astype(jnp.bfloat16)))
+    tied = tie(*[a for p in produced_parts for a in p[1:]], *moved[-1])
+    totals = []
+    for e in experts:
+        total = produced_parts[e][0]
         for k in range(1, high):
-            total = total + to_high(slot_grad[k], -k).astype(jnp.float32)
-        back_rows.append(swap_owner(total.astype(jnp.bfloat16)))
-        total = produced[0]
-        for k in range(1, high):
-            total = total + to_high(produced[k], -k).astype(jnp.float32)
-        produced_rows.append(swap_owner(total.astype(jnp.bfloat16)))
-        for parts, sums in ((in_part, in_grads), (out_part, out_grads)):
-            total = parts[0]
-            for k in range(1, low):
-                total = total + to_low(parts[k], -k).astype(jnp.float32)
-            sums.append(total)
-        router_part = router_part + router_row[0][:, None] * column[None, :]
-    expert_in_grad, expert_out_grad = jnp.stack(in_grads), jnp.stack(out_grads)
+            total = total + to_high(tied[e * (high - 1) + k - 1], -k).astype(jnp.float32)
+        totals.append(total.astype(jnp.bfloat16))
+    produced_home = swap_owner(jnp.concatenate(totals, axis=1))
+    produced_home = produced_home.reshape(owner_count, local_experts, capacity, model_width)
     out_grad = cotangent.astype(jnp.float32)
     mean_load = jnp.sum(counts) / expert_total
     load_weight = (
@@ -357,45 +562,52 @@
     )
     returned = jnp.dot(
         slot_hot,
-        jnp.concatenate([r.reshape(part_rows, model_width) for r in produced_rows]),
+        produced_home.transpose(1, 0, 2, 3).reshape(expert_total * capacity, model_width),
         preferred_element_type=jnp.float32,
     )
     mixed_out = (middle + gate_value[:, None] * returned).astype(jnp.bfloat16)
     middle_part, ln2_gain_part, ln2_bias_part = norm2_pull(normed2_grad)
     middle_grad = out_grad + middle_part
     attn_grad = middle_grad.astype(jnp.bfloat16)
-    outer_grad = contract_rows(attended, attn_grad)
-    attended_grad = times_transposed(attn_grad, outer_weight).astype(jnp.bfloat16)
+    outer_grad = contract_rows(attn_grad, attended).astype(jnp.bfloat16)
+    attended_grad = nn(attn_grad, outer_weight).astype(jnp.bfloat16)
     parts = attn_bwd(prefix_len, projected, attended, attended_grad, head_lse)
-    inner_grad = jnp.concatenate([contract_rows(normed_low, part) for part in parts], axis=1)
+    grad_blocks = jnp.concatenate(
+        [contract_rows(part, normed_low).astype(jnp.bfloat16) for part in parts] + [outer_grad]
+    ).reshape(dp_count * owner_count, -1, model_width)
     normed_grad = sum(
-        times_transposed(part, inner_weight[:, c * model_width : (c + 1) * model_width])
+        nn(part, inner_weight[c * model_width : (c + 1) * model_width])
         for c, part in enumerate(parts)
     )
+    flat = [a for group in in_grads + out_grads for a in group[1:]]
+    normed_grad, *flat = tie(normed_grad, *flat)
+    join = lambda groups: jnp.stack(
+        [sum((flat.pop(0).astype(jnp.float32) for _ in g[1:]), g[0]) for g in groups]
+    )
+    expert_in_grad = join(in_grads)
+    expert_out_grad = join(out_grads)
     input_part, ln1_gain_part, ln1_bias_part = norm_pull(normed_grad)
     tokens_grad = middle_grad + input_part
-    mixer_grad = lax.psum_scatter(
-        jnp.concatenate([inner_grad, outer_grad], axis=1),
-        ("dp", "expert"),
-        scatter_dimension=1,
-        tiled=True,
-    )
-    summed = lax.psum(
-        (ln1_gain_part, ln1_bias_part, ln2_gain_part, ln2_bias_part, router_part, balance_part),
-        ("dp", "expert"),
-    )
+    small = jnp.concatenate(
+        [
+            jnp.stack([ln1_gain_part, ln1_bias_part, ln2_gain_part, ln2_bias_part]),
+            jnp.full((4, model_width), balance_part),
+            router_part.T,
+        ]
+    )
+    mixer_grad, summed = scatter_mixer(grad_blocks, small)
     return (
         mixed_out,
         tokens_grad,
         summed[0],
         summed[1],
-        mixer_grad,
+        mixer_grad.T,
         summed[2],
         summed[3],
-        summed[4],
+        summed[8:].T,
         expert_in_grad,
         expert_out_grad,
-        summed[5],
+        summed[4, 0],
     )
 
 

time: 681 us -> 503 us (0.74)
  waiting for transfers between devices: 290 us -> 144 us
  blocking collectives: 82.3 us -> 0 us
  Pallas kernels: 118 us -> 189 us
  local copies, waits for them, and re-layouts: 14.9 us -> 28.7 us
  between operations: 16.8 us -> 3.47 us
  starting transfers between devices: 54.7 us -> 42.5 us
  matrix products: 60.1 us -> 49.9 us
    ppermute x6 -> x8, waiting for transfers between devices: 119 us -> 23.6 us  [on_device(): to_low = lambda a, k: lax.ppermute(a, 'dp', low_shift(dp_count, low, k))]
    psum x2 -> x0, blocking collectives: 82.3 us -> none  [the longest x1 42.2 us: on_device(): lax.psum((ln1_gain_part, ln1_bias_part, ln2_gain_part, ln2_bias_part, rou...]
    pallas_call x0 -> x2, Pallas kernels: none -> 70.6 us  [the longest x1 35.9 us: scatter_mixer(): pl.pallas_call(scatter_kernel, in_specs=[V, V], out_specs=[V, V], out_sha...]
    all_gather x1 -> x0, waiting for transfers between devices: 56 us -> none  [on_device(): lax.all_gather(mixer_weight, ('dp', 'expert'), axis=1, tiled=True)]
    ppermute x8 -> x7, waiting for transfers between devices: 77.8 us -> 89.3 us  [on_device(): to_high = lambda a, k: lax.ppermute(a, 'dp', high_shift(dp_count, low, k))]
    all_to_all x8 -> x6, starting transfers between devices: 36.7 us -> 28.4 us  [on_device(): lax.all_to_all(a, 'expert', split_axis=0, concat_axis=0, tiled=True)]
    all_to_all x8 -> x6, waiting for transfers between devices: 36.8 us -> 31.2 us  [on_device(): lax.all_to_all(a, 'expert', split_axis=0, concat_axis=0, tiled=True)]
    dot_general x9 -> x8, matrix products: 23.4 us -> 18.1 us  [contract_rows(): lax.dot_general(first_op, second_op, (((0,), (0,)), ((), ())), preferred_...]
  transfers between devices with their start and end apart: 24 -> 21, of which waited for: 15 -> 11; matrix products, arithmetic and copies ran while one was open for 13% -> 18% of each run, Pallas kernels for 12% -> 25%
where the time goes in v3:
time: 503 us; the launch traced here: 497 us
  Pallas kernels  189 us (38%)
  waiting for transfers between devices  144 us (29%)
  matrix products  49.9 us (10%)
  starting transfers between devices  42.5 us (8%)
  other arithmetic  39.8 us (8%)
  local copies, waits for them, and re-layouts  28.7 us (6%)
    ppermute x7, waiting for transfers between devices, on_device(): to_high = lambda a, k: lax.ppermute(a, 'dp', high_shift(dp_count, low, k))  89.3 us
    pallas_call x2, Pallas kernels, run_expert(): pl.pallas_call(functools.partial(expert_kernel, nr, nw, tiles), grid=(nw...  61.6 us
    pallas_call x1, Pallas kernels, scatter_mixer(): pl.pallas_call(scatter_kernel, in_specs=[V, V], out_specs=[V, V], out_sha...  35.9 us
    pallas_call x1, Pallas kernels, gather_mixer(): pl.pallas_call(gather_kernel, in_specs=[V, V], out_specs=[V, V], out_shap...  34.8 us
    pallas_call x1, Pallas kernels, attn_bwd(): pl.pallas_call(bwd_kernel, grid=(n,), in_specs=[pl.BlockSpec(memory_space...  34.1 us
    all_to_all x6, waiting for transfers between devices, on_device(): lax.all_to_all(a, 'expert', split_axis=0, concat_axis=0, tiled=True)  31.2 us
    all_to_all x6, starting transfers between devices, on_device(): lax.all_to_all(a, 'expert', split_axis=0, concat_axis=0, tiled=True)  28.4 us
    ppermute x8, waiting for transfers between devices, on_device(): to_low = lambda a, k: lax.ppermute(a, 'dp', low_shift(dp_count, low, k))  23.6 us
  transfers between devices with their start and end apart: 21, of which 11 were waited for; matrix products, arithmetic and copies ran while one was open for 18% of the time, Pallas kernels for 25%

profile of v3, /device:TPU:0, one launch (start us, length us, event | category | flops | bytes accessed | tf_op | source)
XLA Modules:
  0.0 497.4 jit_solution(14800579328866442430)
XLA Ops:
  4.4 4.7 slice_bitcast_fusion
  9.1 34.8 %gather_mixer.1 = (bf16[32,96,768]{2,1,0:T(8,128)(2,1)}, f32[8,128]{1,0:T(8,128)}) custom-call(bf16[96,768]{1,0:T(8,128)(2,1)} %bitcast.83, f32[8,128]{1,0:T(8,128)} %pad.4.small_ref), custom_call_target="tpu_custom_call" | custom-call | bytes 4718592 | tf_op jit(solution)/shard_map/gather_mixer/pallas_call | solution.py:336
  47.6 4.5 all-to-all-start
  56.5 8.1 %convolution_convert_fusion.q_ref.k_ref.v_ref = bf16[1024,2304]{1,0:T(8,128)(2,1)} fusion(bf16[3072,768]{1,0:T(8,128)(2,1)} %bitcast.68, bf16[1024,768]{0,1:T(8,128)(2,1)S(1)} %copy.35, f32[768]{0:T(1024)S(1)} %copy-done.26, f32[768]{0:T(1024)S(1)} %copy-done.20, f32[1024]{0:T(1024)S(1)} %fusion.50, f32[1024]{0:T(1024)S(1)} %broadcast_multiply_fusion.1), kind=kOutput, calls=%fused_computation | convolution fusion | flops 3630956544 | bytes 9844736 | tf_op jit(solution)/shard_map/dot_general | solution.py:27
  64.5 22.6 %attn_fwd.1 = (bf16[1024,768]{1,0:T(8,128)(2,1)}, f32[6,2,1024]{2,1,0:T(2,128)}) custom-call(s32[1]{0:T(128)S(6)} %copy.55.pre_ref, bf16[1024,2304]{1,0:T(8,128)(2,1)} %convolution_convert_fusion.q_ref.k_ref.v_ref, bf16[1024,2304]{1,0:T(8,128)(2,1)} %convolution_convert_fusion.q_ref.k_ref.v_ref, bf16[1024,2304]{1,0:T(8,128)(2,1)} %convolution_convert_fusion.q_ref.k_ref.v_ref), custom_call_target="tpu_custom_call" | custom-call | tf_op jit(solution)/shard_map/attn_fwd/pallas_call | solution.py:89
  97.4 5.1 %all-to-all-start.1 = ((bf16[8,64,768]{2,1,0:T(8,128)(2,1)}), bf16[8,64,768]{2,1,0:T(8,128)(2,1)}, u32[]{:S(2)}, u32[]{:S(2)}) async-start(bf16[8,64,768]{2,1,0:T(8,128)(2,1)} %bitcast.67), calls=%async_computation.1 | async-start | bytes 1572864 | tf_op jit(solution)/shard_map/all_to_all | solution.py:443
  109.2 14.4 %all-to-all-done.1.refs_1_ = bf16[8,64,768]{2,1,0:T(8,128)(2,1)} async-done(((bf16[8,64,768]{2,1,0:T(8,128)(2,1)}), bf16[8,64,768]{2,1,0:T(8,128)(2,1)}, u32[]{:S(2)}, u32[]{:S(2)}) %all-to-all-start.1) | async-done | bytes 786464 | tf_op jit(solution)/shard_map/all_to_all | solution.py:443
  131.9 16.8 %all-to-all-done.2.refs_1_ = bf16[8,64,768]{2,1,0:T(8,128)(2,1)} async-done(((bf16[8,64,768]{2,1,0:T(8,128)(2,1)}), bf16[8,64,768]{2,1,0:T(8,128)(2,1)}, u32[]{:S(2)}, u32[]{:S(2)}) %all-to-all-start.2) | async-done | bytes 786464 | tf_op jit(solution)/shard_map/all_to_all | solution.py:443
  150.1 7.6 %collective-permute-done.3.refs_6_ = bf16[768,768]{1,0:T(8,128)(2,1)} collective-permute-done((bf16[768,768]{1,0:T(8,128)(2,1)}, bf16[768,768]{1,0:T(8,128)(2,1)}, u32[]{:S(2)}, u32[]{:S(2)}) %collective-permute-start.3) | collective-permute-done | bytes 1179680 | tf_op jit(solution)/shard_map/ppermute | solution.py:441
  157.7 24.5 %collective-permute-done.1.refs_2_ = bf16[8,64,768]{2,1,0:T(8,128)(2,1)} collective-permute-done((bf16[8,64,768]{2,1,0:T(8,128)(2,1)}, bf16[8,64,768]{2,1,0:T(8,128)(2,1)}, u32[]{:S(2)}, u32[]{:S(2)}) %collective-permute-start.1) | collective-permute-done | bytes 786464 | tf_op jit(solution)/shard_map/ppermute | solution.py:442
  182.3 16.2 %collective-permute-done.5.refs_2_ = bf16[8,64,768]{2,1,0:T(8,128)(2,1)} collective-permute-done((bf16[8,64,768]{2,1,0:T(8,128)(2,1)}, bf16[8,64,768]{2,1,0:T(8,128)(2,1)}, u32[]{:S(2)}, u32[]{:S(2)}) %collective-permute-start.5) | collective-permute-done | bytes 786464 | tf_op jit(solution)/shard_map/ppermute | solution.py:442
  198.5 31.0 %expert.3 = (f32[8,64,768]{2,1,0:T(8,128)}, bf16[8,64,768]{2,1,0:T(8,128)(2,1)}, f32[8,64,768]{2,1,0:T(8,128)}, bf16[8,64,768]{2,1,0:T(8,128)(2,1)}, f32[768,768...) custom-call(f32[1,768]{1,0:T(1,128)} %broadcast_in_dim.18.refs_0_, ...), custom_call_target="tpu_custom_call" | custom-call | flops 14495514624 | bytes 19660800 | tf_op jit(solution)/shard_map/expert/pallas_call | solution.py:227
  230.9 17.8 %collective-permute-done.7 = bf16[8,64,768]{2,1,0:T(8,128)(2,1)S(1)} collective-permute-done((bf16[8,64,768]{2,1,0:T(8,128)(2,1)}, bf16[8,64,768]{2,1,0:T(8,128)(2,1)S(1)}, u32[]{:S(2)}, u32[]{:S(2)}) %collective-permute-start.7) | collective-permute-done | bytes 786464 | tf_op jit(solution)/shard_map/ppermute | solution.py:442
  251.2 4.8 all-to-all-start.5
  256.0 30.6 %expert.2 = (f32[8,64,768]{2,1,0:T(8,128)}, bf16[8,64,768]{2,1,0:T(8,128)(2,1)}, f32[8,64,768]{2,1,0:T(8,128)}, bf16[8,64,768]{2,1,0:T(8,128)(2,1)}, f32[768,768...) custom-call(f32[1,768]{1,0:T(1,128)} %broadcast_in_dim.17.refs_0_, ...), custom_call_target="tpu_custom_call" | custom-call | flops 14495514624 | bytes 19660800 | tf_op jit(solution)/shard_map/expert/pallas_call | solution.py:227
  295.5 11.9 %collective-permute-done.10 = bf16[8,64,768]{2,1,0:T(8,128)(2,1)} collective-permute-done((bf16[8,64,768]{2,1,0:T(8,128)(2,1)}, bf16[8,64,768]{2,1,0:T(8,128)(2,1)}, u32[]{:S(2)}, u32[]{:S(2)}) %collective-permute-start.10) | collective-permute-done | bytes 786464 | tf_op jit(solution)/shard_map/ppermute | solution.py:442
  310.1 5.1 %all-to-all-start.4 = ((bf16[8,64,768]{2,1,0:T(8,128)(2,1)}), bf16[8,64,768]{2,1,0:T(8,128)(2,1)}, u32[]{:S(2)}, u32[]{:S(2)}) async-start(bf16[8,64,768]{2,1,0:T(8,128)(2,1)} %add_convert_fusion.3), calls=%async_computation.4 | async-start | bytes 1572864 | tf_op jit(solution)/shard_map/all_to_all | solution.py:443
  319.1 5.1 %collective-permute-done.8 = bf16[8,64,768]{2,1,0:T(8,128)(2,1)} collective-permute-done((bf16[8,64,768]{2,1,0:T(8,128)(2,1)}, bf16[8,64,768]{2,1,0:T(8,128)(2,1)}, u32[]{:S(2)}, u32[]{:S(2)}) %collective-permute-start.8) | collective-permute-done | bytes 786464 | tf_op jit(solution)/shard_map/ppermute | solution.py:442
  326.9 13.7 %collective-permute-done.9 = bf16[8,64,768]{2,1,0:T(8,128)(2,1)S(1)} collective-permute-done((bf16[8,64,768]{2,1,0:T(8,128)(2,1)}, bf16[8,64,768]{2,1,0:T(8,128)(2,1)S(1)}, u32[]{:S(2)}, u32[]{:S(2)}) %collective-permute-start.9) | collective-permute-done | bytes 786464 | tf_op jit(solution)/shard_map/ppermute | solution.py:442
  342.1 4.7 all-to-all-start.3
  361.7 34.1 %attn_bwd.1 = (bf16[1024,768]{1,0:T(8,128)(2,1)}, bf16[1024,768]{1,0:T(8,128)(2,1)}, bf16[1024,768]{1,0:T(8,128)(2,1)}) custom-call(s32[1]{0:T(128)S(6)} %copy.55.pre_ref, bf16[1024,2304]{1,0:T(8,128)(2,1)} %convolution_convert_fusion.q_ref.k_ref.v_ref, bf16[1024,2304]{1,0:T(8,128)(2,1)} %convolution_convert_fusion.q_ref.k_ref.v_ref, ...), custom_call_target="tpu_custom_call" | custom-call | tf_op jit(solution)/shard_map/attn_bwd/pallas_call | solution.py:141
  408.5 12.3 %collective-permute-done.13 = bf16[768,768]{1,0:T(8,128)(2,1)} collective-permute-done((bf16[768,768]{1,0:T(8,128)(2,1)}, bf16[768,768]{1,0:T(8,128)(2,1)}, u32[]{:S(2)}, u32[]{:S(2)}) %collective-permute-start.13) | collective-permute-done | bytes 1179680 | tf_op jit(solution)/shard_map/ppermute | solution.py:441
  427.4 35.9 %scatter_mixer.1 = (f32[96,768]{1,0:T(8,128)}, f32[24,768]{1,0:T(8,128)}) custom-call(bf16[32,96,768]{2,1,0:T(8,128)(2,1)} %bitcast.63, f32[24,768]{1,0:T(8,128)} %concatenate.15.small_ref), custom_call_target="tpu_custom_call" | custom-call | bytes 9437184 | tf_op jit(solution)/shard_map/scatter_mixer/pallas_call | solution.py:402
  464.5 5.9 %add_add_fusion.2 = f32[1024,768]{0,1:T(8,128)} fusion(f32[1024,768]{0,1:T(8,128)} %copy-done.4, bf16[1024,768]{0,1:T(8,128)(2,1)S(1)} %copy-done.5, f32[1024]{0:T(1024)S(1)} %negate_multiply_fusion, f32[1024]{0:T(1024)S(1)} %negate_multiply_fusion.1, f32[1024]{0:T(1024)S(1)} %multiply_multiply_fusion, f32[1024]{0:T(1024)S(1)} %broadcast_multiply_fusion.1, ...), kind=kLoop, calls=%fused_computation.26 | loop fusion | flops 9437184 | bytes 12606464 | tf_op jit(solution)/shard_map/add | solution.py:590
  (166 shorter events, 121.6 us)
Async XLA Ops:
  4.4 39.5 %copy-start.12 = (bf16[1024,768]{1,0:T(8,128)(2,1)S(1)}, bf16[1024,768]{1,0:T(8,128)(2,1)}, u32[]{:S(2)}) copy-start(bf16[1024,768]{1,0:T(8,128)(2,1)} %param.25) | copy-start | bytes 4718596
  47.6 46.7 %all-to-all-start = ((bf16[8,128,768]{2,1,0:T(8,128)(2,1)}), bf16[8,128,768]{2,1,0:T(8,128)(2,1)}, u32[]{:S(2)}, u32[]{:S(2)}) async-start(bf16[8,128,768]{2,1,0:T(8,128)(2,1)} %bitcast.12), calls=%async_computation | async-start | bytes 3145728 | tf_op jit(solution)/shard_map/all_to_all | solution.py:443
  52.2 36.8 %collective-permute-start = (bf16[768,768]{1,0:T(8,128)(2,1)}, bf16[768,768]{1,0:T(8,128)(2,1)}, u32[]{:S(2)}, u32[]{:S(2)}) collective-permute-start(bf16[768,768]{1,0:T(8,128)(2,1)} %get-tuple-element.79.refs_5_), channel_id=1, source_target_pairs={{0,8},{8,0},{16,24},{24,16},{1,9},{9,1},{17,25},{25,17},{2,10},{10... | collective-permute-start | bytes 3538952 | tf_op jit(solution)/shard_map/ppermute | solution.py:441
  53.1 53.1 %collective-permute-start.2 = (bf16[768,768]{1,0:T(8,128)(2,1)}, bf16[768,768]{1,0:T(8,128)(2,1)}, u32[]{:S(2)}, u32[]{:S(2)}) collective-permute-start(bf16[768,768]{1,0:T(8,128)(2,1)} %get-tuple-element.81.refs_7_), channel_id=1, source_target_pairs={{0,8},{8,0},{16,24},{24,16},{1,9},{9,1},{17,25},{25,17},{2,10},{10... | collective-permute-start | bytes 3538952 | tf_op jit(solution)/shard_map/ppermute | solution.py:441
  97.4 26.1 %all-to-all-start.1 = ((bf16[8,64,768]{2,1,0:T(8,128)(2,1)}), bf16[8,64,768]{2,1,0:T(8,128)(2,1)}, u32[]{:S(2)}, u32[]{:S(2)}) async-start(bf16[8,64,768]{2,1,0:T(8,128)(2,1)} %bitcast.67), calls=%async_computation.1 | async-start | bytes 1572864 | tf_op jit(solution)/shard_map/all_to_all | solution.py:443
  102.5 47.0 %copy-start.16 = (bf16[768,16]{0,1:T(8,128)(2,1)S(1)}, bf16[768,16]{0,1:T(8,128)(2,1)}, u32[]{:S(2)}) copy-start(bf16[768,16]{0,1:T(8,128)(2,1)} %param.22) | copy-start | bytes 73732
  123.5 25.2 %all-to-all-start.2 = ((bf16[8,64,768]{2,1,0:T(8,128)(2,1)}), bf16[8,64,768]{2,1,0:T(8,128)(2,1)}, u32[]{:S(2)}, u32[]{:S(2)}) async-start(bf16[8,64,768]{2,1,0:T(8,128)(2,1)} %bitcast.66), calls=%async_computation.2 | async-start | bytes 1572864 | tf_op jit(solution)/shard_map/all_to_all | solution.py:443
  127.8 54.5 %collective-permute-start.4 = (bf16[8,128,768]{2,1,0:T(8,128)(2,1)}, bf16[8,128,768]{2,1,0:T(8,128)(2,1)}, u32[]{:S(2)}, u32[]{:S(2)}) collective-permute-start(bf16[8,128,768]{2,1,0:T(8,128)(2,1)} %all-to-all-done), channel_id=1, source_target_pairs={{0,16},{8,24},{16,0},{24,8},{1,17},{9,25},{17,1},{25,9},{2,18},{10... | collective-permute-start | bytes 4718600 | tf_op jit(solution)/shard_map/ppermute | solution.py:442
  128.6 29.2 %collective-permute-start.3 = (bf16[768,768]{1,0:T(8,128)(2,1)}, bf16[768,768]{1,0:T(8,128)(2,1)}, u32[]{:S(2)}, u32[]{:S(2)}) collective-permute-start(bf16[768,768]{1,0:T(8,128)(2,1)} %get-tuple-element.86.refs_5_), channel_id=1, source_target_pairs={{0,8},{8,0},{16,24},{24,16},{1,9},{9,1},{17,25},{25,17},{2,10},{10... | collective-permute-start | bytes 3538952 | tf_op jit(solution)/shard_map/ppermute | solution.py:441
  129.1 53.1 %collective-permute-start.6 = (bf16[768,768]{1,0:T(8,128)(2,1)}, bf16[768,768]{1,0:T(8,128)(2,1)}, u32[]{:S(2)}, u32[]{:S(2)}) collective-permute-start(bf16[768,768]{1,0:T(8,128)(2,1)} %get-tuple-element.88.refs_7_), channel_id=1, source_target_pairs={{0,8},{8,0},{16,24},{24,16},{1,9},{9,1},{17,25},{25,17},{2,10},{10... | collective-permute-start | bytes 3538952 | tf_op jit(solution)/shard_map/ppermute | solution.py:441
  130.6 51.7 %collective-permute-start.1 = (bf16[8,64,768]{2,1,0:T(8,128)(2,1)}, bf16[8,64,768]{2,1,0:T(8,128)(2,1)}, u32[]{:S(2)}, u32[]{:S(2)}) collective-permute-start(bf16[8,64,768]{2,1,0:T(8,128)(2,1)} %all-to-all-done.1.refs_1_), channel_id=1, source_target_pairs={{0,16},{8,24},{16,0},{24,8},{1,17},{9,25},{17,1},{25,9},{2,18},{10... | collective-permute-start | bytes 2359304 | tf_op jit(solution)/shard_map/ppermute | solution.py:442
  148.7 49.8 %collective-permute-start.5 = (bf16[8,64,768]{2,1,0:T(8,128)(2,1)}, bf16[8,64,768]{2,1,0:T(8,128)(2,1)}, u32[]{:S(2)}, u32[]{:S(2)}) collective-permute-start(bf16[8,64,768]{2,1,0:T(8,128)(2,1)} %all-to-all-done.2.refs_1_), channel_id=1, source_target_pairs={{0,16},{8,24},{16,0},{24,8},{1,17},{9,25},{17,1},{25,9},{2,18},{10... | collective-permute-start | bytes 2359304 | tf_op jit(solution)/shard_map/ppermute | solution.py:442
  229.5 19.2 %collective-permute-start.7 = (bf16[8,64,768]{2,1,0:T(8,128)(2,1)}, bf16[8,64,768]{2,1,0:T(8,128)(2,1)S(1)}, u32[]{:S(2)}, u32[]{:S(2)}) collective-permute-start(bf16[8,64,768]{2,1,0:T(8,128)(2,1)} %get-tuple-element.90), channel_id=1, source_target_pairs={{0,16},{8,24},{16,0},{24,8},{1,17},{9,25},{17,1},{25,9},{2,18},{10... | collective-permute-start | bytes 2359304 | tf_op jit(solution)/shard_map/ppermute | solution.py:442
  251.2 58.9 %all-to-all-start.5 = ((bf16[8,64,768]{2,1,0:T(8,128)(2,1)}), bf16[8,64,768]{2,1,0:T(8,128)(2,1)}, u32[]{:S(2)}, u32[]{:S(2)}) async-start(bf16[8,64,768]{2,1,0:T(8,128)(2,1)} %add_convert_fusion.2), calls=%async_computation.5 | async-start | bytes 1572864 | tf_op jit(solution)/shard_map/all_to_all | solution.py:443
  286.6 20.8 %collective-permute-start.10 = (bf16[8,64,768]{2,1,0:T(8,128)(2,1)}, bf16[8,64,768]{2,1,0:T(8,128)(2,1)}, u32[]{:S(2)}, u32[]{:S(2)}) collective-permute-start(bf16[8,64,768]{2,1,0:T(8,128)(2,1)} %get-tuple-element.98), channel_id=1, source_target_pairs={{0,16},{8,24},{16,0},{24,8},{1,17},{9,25},{17,1},{25,9},{2,18},{10... | collective-permute-start | bytes 2359304 | tf_op jit(solution)/shard_map/ppermute | solution.py:442
  294.2 30.1 %collective-permute-start.8 = (bf16[8,64,768]{2,1,0:T(8,128)(2,1)}, bf16[8,64,768]{2,1,0:T(8,128)(2,1)}, u32[]{:S(2)}, u32[]{:S(2)}) collective-permute-start(bf16[8,64,768]{2,1,0:T(8,128)(2,1)} %get-tuple-element.91), channel_id=1, source_target_pairs={{0,16},{8,24},{16,0},{24,8},{1,17},{9,25},{17,1},{25,9},{2,18},{10... | collective-permute-start | bytes 2359304 | tf_op jit(solution)/shard_map/ppermute | solution.py:442
  310.1 32.0 %all-to-all-start.4 = ((bf16[8,64,768]{2,1,0:T(8,128)(2,1)}), bf16[8,64,768]{2,1,0:T(8,128)(2,1)}, u32[]{:S(2)}, u32[]{:S(2)}) async-start(bf16[8,64,768]{2,1,0:T(8,128)(2,1)} %add_convert_fusion.3), calls=%async_computation.4 | async-start | bytes 1572864 | tf_op jit(solution)/shard_map/all_to_all | solution.py:443
  315.2 25.4 %copy-start.13 = (f32[8,64,768]{2,1,0:T(8,128)S(1)}, f32[8,64,768]{2,1,0:T(8,128)}, u32[]{:S(2)}) copy-start(f32[8,64,768]{2,1,0:T(8,128)} %get-tuple-element.92) | copy-start | bytes 4718596
  315.2 25.3 %collective-permute-start.9 = (bf16[8,64,768]{2,1,0:T(8,128)(2,1)}, bf16[8,64,768]{2,1,0:T(8,128)(2,1)S(1)}, u32[]{:S(2)}, u32[]{:S(2)}) collective-permute-start(bf16[8,64,768]{2,1,0:T(8,128)(2,1)} %get-tuple-element.93), channel_id=1, source_target_pairs={{0,16},{8,24},{16,0},{24,8},{1,17},{9,25},{17,1},{25,9},{2,18},{10... | collective-permute-start | bytes 2359304 | tf_op jit(solution)/shard_map/ppermute | solution.py:442
  316.5 91.9 %collective-permute-start.12 = (bf16[768,768]{1,0:T(8,128)(2,1)}, bf16[768,768]{1,0:T(8,128)(2,1)}, u32[]{:S(2)}, u32[]{:S(2)}) collective-permute-start(bf16[768,768]{1,0:T(8,128)(2,1)} %get-tuple-element.106), channel_id=1, source_target_pairs={{0,8},{8,0},{16,24},{24,16},{1,9},{9,1},{17,25},{25,17},{2,10},{10... | collective-permute-start | bytes 3538952 | tf_op jit(solution)/shard_map/ppermute | solution.py:441
  317.1 91.4 %collective-permute-start.14 = (bf16[768,768]{1,0:T(8,128)(2,1)}, bf16[768,768]{1,0:T(8,128)(2,1)}, u32[]{:S(2)}, u32[]{:S(2)}) collective-permute-start(bf16[768,768]{1,0:T(8,128)(2,1)} %get-tuple-element.108), channel_id=1, source_target_pairs={{0,8},{8,0},{16,24},{24,16},{1,9},{9,1},{17,25},{25,17},{2,10},{10... | collective-permute-start | bytes 3538952 | tf_op jit(solution)/shard_map/ppermute | solution.py:441
  318.6 89.9 %collective-permute-start.11 = (bf16[768,768]{1,0:T(8,128)(2,1)}, bf16[768,768]{1,0:T(8,128)(2,1)}, u32[]{:S(2)}, u32[]{:S(2)}) collective-permute-start(bf16[768,768]{1,0:T(8,128)(2,1)} %get-tuple-element.105), channel_id=1, source_target_pairs={{0,8},{8,0},{16,24},{24,16},{1,9},{9,1},{17,25},{25,17},{2,10},{10... | collective-permute-start | bytes 3538952 | tf_op jit(solution)/shard_map/ppermute | solution.py:441
  324.3 96.5 %collective-permute-start.13 = (bf16[768,768]{1,0:T(8,128)(2,1)}, bf16[768,768]{1,0:T(8,128)(2,1)}, u32[]{:S(2)}, u32[]{:S(2)}) collective-permute-start(bf16[768,768]{1,0:T(8,128)(2,1)} %get-tuple-element.107), channel_id=1, source_target_pairs={{0,8},{8,0},{16,24},{24,16},{1,9},{9,1},{17,25},{25,17},{2,10},{10... | collective-permute-start | bytes 3538952 | tf_op jit(solution)/shard_map/ppermute | solution.py:441
  342.1 145.7 %all-to-all-start.3 = ((bf16[8,128,768]{2,1,0:T(8,128)(2,1)}), bf16[8,128,768]{2,1,0:T(8,128)(2,1)}, u32[]{:S(2)}, u32[]{:S(2)}) async-start(bf16[8,128,768]{2,1,0:T(8,128)(2,1)} %pad_maximum_fusion.3), calls=%async_computation.3 | async-start | bytes 3145728 | tf_op jit(solution)/shard_map/all_to_all | solution.py:443
  (26 other events, 107.9 us)

commit v4 on v3

--- a/solution.py
+++ b/solution.py
@@ -161,79 +161,88 @@
     for c in ERF_DEN[1:]: d=d*y+c
     return x*n/d
 
-def expert_kernel(nr,nw,tiles,*refs):
-    rw_ref=refs[0]; refs=refs[1:]
-    x_refs,refs=refs[:nr],refs[nr:]
-    c_refs,refs=refs[:nr],refs[nr:]
-    wi_refs,refs=refs[:nw],refs[nw:]
-    wo_refs,refs=refs[:nw],refs[nw:]
-    p_refs,refs=refs[:nr],refs[nr:]
-    d_refs,refs=refs[:nr],refs[nr:]
-    gi_refs,refs=refs[:nw],refs[nw:]
-    go_refs,refs=refs[:nw],refs[nw:]
-    rg_ref,x_s,g_s,gate_s,p_acc,d_acc=refs
+def rows_kernel(nw,tiles,rw_ref,x_ref,c_ref,*refs):
+    wi_refs,wo_refs=refs[:nw],refs[nw:2*nw]
+    p_ref,d_ref,act_ref,dp_ref,g_ref,rg_ref,gate_s,p_acc,d_acc=refs[2*nw:]
     step=pl.program_id(0)
-    S,C,D=x_refs[0].shape; R=S*C
+    S,C,D=x_ref.shape; R=S*C
     @pl.when(step==0)
     def _():
-        for r in range(nr):
-            rows=slice(r*R,(r+1)*R)
-            x=x_refs[r][...].reshape(R,D)
-            gate=jax.nn.sigmoid(jnp.sum(x.astype(F32)*rw_ref[...],axis=1,keepdims=True))
-            x_s[rows,:]=x
-            g_s[rows,:]=(gate*c_refs[r][...].reshape(R,D).astype(F32)).astype(BF)
-            gate_s[rows,:]=gate
-        p_acc[...]=jnp.zeros_like(p_acc); d_acc[...]=jnp.zeros_like(d_acc)
+        gate=jax.nn.sigmoid(jnp.sum(x_ref[...].reshape(R,D).astype(F32)*rw_ref[...],axis=1,keepdims=True))
+        g_ref[...]=(gate*c_ref[...].reshape(R,D).astype(F32)).astype(BF)
+        gate_s[...]=gate
     for w in range(nw):
         @pl.when(step//tiles==w)
         def _(w=w):
             wi=wi_refs[w][...]; wo=wo_refs[w][...]
-            pre=nt(x_s[...],wi)
-            da=nt(g_s[...],wo)
-            phi=0.5+0.5*erf32(pre*0.7071067811865476)
-            act=(pre*phi).astype(BF)
-            dens=0.3989422804014327*jnp.exp(-0.5*pre*pre)
-            dp=(da*(phi+pre*dens)).astype(BF)
-            p_acc[...]+=nn(act,wo)
-            d_acc[...]+=nn(dp,wi)
-            gi_refs[w][...]=tn(dp,x_s[...]).astype(gi_refs[w].dtype)
-            go_refs[w][...]=tn(act,g_s[...]).astype(go_refs[w].dtype)
+            F=wi.shape[0]; sub=256 if F%256==0 else F
+            x=x_ref[...].reshape(R,D); g=g_ref[...]
+            for i in range(0,F,sub):
+                pre=nt(x,wi[i:i+sub])
+                da=nt(g,wo[i:i+sub])
+                phi=0.5+0.5*erf32(pre*0.7071067811865476)
+                act_ref[:,i:i+sub]=(pre*phi).astype(BF)
+                dens=0.3989422804014327*jnp.exp(-0.5*pre*pre)
+                dp_ref[:,i:i+sub]=(da*(phi+pre*dens)).astype(BF)
+            p=nn(act_ref[...],wo); d=nn(dp_ref[...],wi)
+            if w==0:
+                @pl.when(step==0)
+                def _(): p_acc[...]=p; d_acc[...]=d
+                @pl.when(step>0)
+                def _(): p_acc[...]+=p; d_acc[...]+=d
+            else: p_acc[...]+=p; d_acc[...]+=d
     @pl.when(step==nw*tiles-1)
     def _():
-        rg=jnp.zeros((1,D),F32)
-        for r in range(nr):
-            rows=slice(r*R,(r+1)*R)
-            p=p_acc[rows,:]; gate=gate_s[rows,:]
-            dot=jnp.sum(p*c_refs[r][...].reshape(R,D).astype(F32),axis=1,keepdims=True)
-            lg=dot*(gate*(1.0-gate))
-            p_refs[r][...]=p.reshape(S,C,D).astype(p_refs[r].dtype)
-            d_refs[r][...]=(d_acc[rows,:]+lg*rw_ref[...]).reshape(S,C,D).astype(d_refs[r].dtype)
-            rg=rg+jnp.sum(lg*x_s[rows,:].astype(F32),axis=0,keepdims=True)
-        rg_ref[...]=rg
-
-def run_expert(e,rw,xs,cs,wis,wos):
-    nr,nw=len(xs),len(wis)
-    S,C,D=xs[0].shape; Q=wis[0].shape[0]; R=nr*S*C
-    tile=Q
-    for t in (384,256,192,128):
-        if Q%t==0: tile=t; break
-    tiles=Q//tile
+        p=p_acc[...]; gate=gate_s[...]
+        dot=jnp.sum(p*c_ref[...].reshape(R,D).astype(F32),axis=1,keepdims=True)
+        lg=dot*(gate*(1.0-gate))
+        p_ref[...]=p.reshape(S,C,D).astype(p_ref.dtype)
+        d_ref[...]=(d_acc[...]+lg*rw_ref[...]).reshape(S,C,D).astype(d_ref.dtype)
+        rg_ref[...]=jnp.sum(lg*x_ref[...].reshape(R,D).astype(F32),axis=0,keepdims=True)
+
+def tile_of(Q):
+    return Q
+
+def run_rows(kind,rw,x,c,wis,wos):
+    nw=len(wis); S,C,D=x.shape; Q=wis[0].shape[0]; R=S*C; tile=tile_of(Q); tiles=Q//tile
     whole=lambda shape: pl.BlockSpec(shape,lambda i:(0,)*len(shape))
     at=lambda w: (lambda i: jnp.clip(i-w*tiles,0,tiles-1))
     wspec=lambda w: pl.BlockSpec((tile,D),lambda i,f=at(w):(f(i),0))
-    gspec=lambda w: pl.BlockSpec((tile,D),lambda i,f=at(w):(f(i),0))
-    rows_spec=whole((S,C,D))
-    kind=lambda k: F32 if k==0 else BF
-    outs=pl.pallas_call(functools.partial(expert_kernel,nr,nw,tiles),grid=(nw*tiles,),
-        in_specs=[whole((1,D))]+[rows_spec]*nr+[pl.BlockSpec((S,1,C,D),lambda i:(0,e,0,0))]*nr+[wspec(w) for w in range(nw)]*2,
-        out_specs=[rows_spec]*(2*nr)+[gspec(w) for w in range(nw)]*2+[whole((1,D))],
-        out_shape=[jax.ShapeDtypeStruct((S,C,D),kind(r)) for r in range(nr)]*2
-          +[jax.ShapeDtypeStruct((Q,D),kind(w)) for w in range(nw)]*2+[jax.ShapeDtypeStruct((1,D),F32)],
-        scratch_shapes=[pltpu.VMEM((R,D),BF),pltpu.VMEM((R,D),BF),pltpu.VMEM((R,1),F32),pltpu.VMEM((R,D),F32),pltpu.VMEM((R,D),F32)],
+    wide=pl.BlockSpec((None,R,tile),lambda i:(i,0,0))
+    return pl.pallas_call(functools.partial(rows_kernel,nw,tiles),grid=(nw*tiles,),
+        in_specs=[whole((1,D)),whole((S,C,D)),whole((S,C,D))]+[wspec(w) for w in range(nw)]*2,
+        out_specs=[whole((S,C,D))]*2+[wide,wide,whole((R,D)),whole((1,D))],
+        out_shape=[jax.ShapeDtypeStruct((S,C,D),kind)]*2+[jax.ShapeDtypeStruct((nw*tiles,R,tile),BF)]*2
+          +[jax.ShapeDtypeStruct((R,D),BF),jax.ShapeDtypeStruct((1,D),F32)],
+        scratch_shapes=[pltpu.VMEM((R,1),F32),pltpu.VMEM((R,D),F32),pltpu.VMEM((R,D),F32)],
         compiler_params=pltpu.CompilerParams(vmem_limit_bytes=60<<20),
-        cost_estimate=pl.CostEstimate(flops=12*R*nw*Q*D,bytes_accessed=nw*Q*D*10+R*D*10,transcendentals=R*nw*Q),
-        name="expert")(rw,*xs,*cs,*wis,*wos)
-    return outs[:nr],outs[nr:2*nr],outs[2*nr:2*nr+nw],outs[2*nr+nw:2*nr+2*nw],outs[-1]
+        cost_estimate=pl.CostEstimate(flops=8*R*nw*Q*D,bytes_accessed=nw*Q*(4*D+4*R)+R*D*10,transcendentals=R*nw*Q),
+        name="expert_rows")(rw,x,c,*wis,*wos)
+
+def grads_kernel(nr,nw,tiles,*refs):
+    x_refs,g_refs,act_refs,dp_refs=(refs[i*nr:(i+1)*nr] for i in range(4))
+    gi_refs,go_refs=refs[4*nr:4*nr+nw],refs[4*nr+nw:]
+    step=pl.program_id(0)
+    S,C,D=x_refs[0].shape
+    gi=sum(tn(d[...],x[...].reshape(S*C,D)) for d,x in zip(dp_refs,x_refs)).astype(BF)
+    go=sum(tn(a[...],g[...]) for a,g in zip(act_refs,g_refs)).astype(BF)
+    for w in range(nw):
+        @pl.when(step//tiles==w)
+        def _(w=w):
+            gi_refs[w][...]=gi; go_refs[w][...]=go
+
+def run_grads(nw,xs,gs,acts,dps):
+    nr=len(xs); S,C,D=xs[0].shape; R=S*C; tile=acts[0].shape[2]; tiles=acts[0].shape[0]//nw; Q=tiles*tile
+    whole=lambda shape: pl.BlockSpec(shape,lambda i:(0,)*len(shape))
+    gspec=lambda w: pl.BlockSpec((tile,D),lambda i:(jnp.clip(i-w*tiles,0,tiles-1),0))
+    outs=pl.pallas_call(functools.partial(grads_kernel,nr,nw,tiles),grid=(nw*tiles,),
+        in_specs=[whole((S,C,D))]*nr+[whole((R,D))]*nr+[pl.BlockSpec((None,R,tile),lambda i:(i,0,0))]*(2*nr),
+        out_specs=[gspec(w) for w in range(nw)]*2,
+        out_shape=[jax.ShapeDtypeStruct((Q,D),BF)]*(2*nw),
+        compiler_params=pltpu.CompilerParams(vmem_limit_bytes=60<<20),
+        cost_estimate=pl.CostEstimate(flops=4*nr*R*nw*Q*D,bytes_accessed=nw*Q*D*4+nr*R*(4*D+4*nw*Q),transcendentals=0),
+        name="expert_grads")(*xs,*gs,*acts,*dps)
+    return list(outs[:nw]),list(outs[nw:])
 
 MESH=pl.DeviceIdType.MESH
 
@@ -284,8 +293,13 @@
         if self.i<len(self.g.all_bits): self.buf[i+1]=v; self.start()
         else: self.sum_ref[...]=v
 
-def gather_kernel(w_ref,small_ref,out_ref,sum_ref,s_buf,s_in,ssem,rsem,cs,cr,sssem,srsem):
+def gather_kernel(nx,w_ref,small_ref,*refs):
+    x_refs=refs[:nx]; out_ref,sum_ref=refs[nx:nx+2]; count=x_refs[0].shape[0]
+    y_refs=refs[nx+2:nx+2+nx*count]
+    s_buf,s_in,hold,ssem,rsem,cs,cr,sssem,srsem,isem,osem=refs[nx+2+nx*count:]
     g=Grid(); g.here(); g.greet()
+    loads=[pltpu.make_async_copy(x_refs[i//count].at[i%count],hold.at[i],isem.at[i]) for i in range(nx*count)]
+    stores=[pltpu.make_async_copy(hold.at[i],y_refs[i],osem.at[i]) for i in range(nx*count)]
     small=SmallSum(g,small_ref,sum_ref,s_buf,s_in,sssem,srsem)
     D=w_ref.shape[1]; n=len(g.orders); L=D//n
     chip=g.orders[0]; number={place_of(chip,c):c for c in range(1<<len(chip))}
@@ -314,7 +328,9 @@
             k=order[m-1-j]
             for p in held[o]: send(o,p,k)
             if j==0: across(o,frozenset())
-        if j==0: small.start()
+        if j==0:
+            small.start()
+            for c in loads: c.start()
         else: small.step()
         for o,order in enumerate(g.orders):
             k=order[m-1-j]
@@ -322,24 +338,30 @@
                 arrived(o,p,order[m-j]); send(o,p,k); across(o,p)
             held[o]=held[o]+fresh[o]
             fresh[o]=[p|{k} for p in held[o]]
+        if j==1:
+            for a,b in zip(loads,stores): a.wait(); b.start()
     for i in range(len(fresh[0])):
         for o,order in enumerate(g.orders):
             arrived(o,fresh[o][i],order[0]); across(o,fresh[o][i])
     for _ in g.all_bits: small.step()
     for c in core_in: c.wait_recv()
     for c in sends: c.wait_send()
-
-def gather_mixer(w,small):
+    for c in stores: c.wait()
+
+def gather_mixer(w,small,stacks):
     g=Grid(); n=g.dp*g.expert; half=n//2; k=len(g.orders); nb=len(g.all_bits)
     V=pl.BlockSpec(memory_space=pltpu.VMEM); S=pltpu.SemaphoreType.DMA
     D=w.shape[1]
-    return pl.pallas_call(gather_kernel,
-        in_specs=[V,V],out_specs=[V,V],
-        out_shape=[jax.ShapeDtypeStruct((n,)+w.shape,w.dtype),jax.ShapeDtypeStruct(small.shape,F32)],
-        scratch_shapes=[pltpu.VMEM((nb,)+small.shape,F32)]*2+[S((k,half))]*4+[S((nb,))]*2,
+    nx=len(stacks); count,Q,_=stacks[0].shape; A=pl.BlockSpec(memory_space=pl.ANY)
+    outs=pl.pallas_call(functools.partial(gather_kernel,nx),
+        in_specs=[V,V]+[A]*nx,out_specs=[V,V]+[A]*(nx*count),
+        out_shape=[jax.ShapeDtypeStruct((n,)+w.shape,w.dtype),jax.ShapeDtypeStruct(small.shape,F32)]
+          +[jax.ShapeDtypeStruct((Q,D),w.dtype)]*(nx*count),
+        scratch_shapes=[pltpu.VMEM((nb,)+small.shape,F32)]*2+[pltpu.VMEM((nx*count,Q,D),w.dtype)]+[S((k,half))]*4+[S((nb,))]*2+[S((nx*count,))]*2,
         compiler_params=pltpu.CompilerParams(collective_id=0,has_side_effects=True,vmem_limit_bytes=60<<20),
         cost_estimate=pl.CostEstimate(flops=0,bytes_accessed=n*w.size*2,transcendentals=0),
-        name="gather_mixer")(w,small)
+        name="gather_mixer")(w,small,*stacks)
+    return outs[0],outs[1],[list(outs[2+i*count:2+(i+1)*count]) for i in range(nx)]
 
 def scatter_kernel(g_ref,small_ref,out_ref,sum_ref,c_in,acc,out_buf,in_buf,s_buf,s_in,csem,crem,ssem,rsem,sssem,srsem):
     g=Grid(); g.here(); g.greet()
@@ -408,6 +430,24 @@
         cost_estimate=pl.CostEstimate(flops=0,bytes_accessed=grad.size*4,transcendentals=0),
         name="scatter_mixer")(grad,small)
 
+def join_kernel(count,sizes,*refs):
+    outs=refs[sum(sizes):]; refs=list(refs[:sum(sizes)])
+    for i,n in enumerate(sizes):
+        parts=[refs.pop(0) for _ in range(n)]
+        total=parts[0][...].astype(F32)
+        for p in parts[1:]: total=total+p[...].astype(F32)
+        outs[i//count][i%count]=total
+
+def join_grads(groups,count):
+    sizes=tuple(len(g) for g in groups); Q,D=groups[0][0].shape; tile=Q//4
+    return pl.pallas_call(functools.partial(join_kernel,count,sizes),grid=(4,),
+        in_specs=[pl.BlockSpec((tile,D),lambda i:(i,0))]*sum(sizes),
+        out_specs=[pl.BlockSpec((count,tile,D),lambda i:(0,i,0))]*2,
+        out_shape=[jax.ShapeDtypeStruct((count,Q,D),F32)]*2,
+        compiler_params=pltpu.CompilerParams(vmem_limit_bytes=60<<20),
+        cost_estimate=pl.CostEstimate(flops=0,bytes_accessed=Q*D*(8*count+2*sum(sizes)),transcendentals=0),
+        name="join_grads")(*[p for g in groups for p in g])
+
 def tie(*xs): return lax.optimization_barrier(xs)
 
 def low_shift(n,nx,k): return [(i,i//nx*nx+(i%nx+k)%nx) for i in range(n)]
@@ -445,7 +485,9 @@
     route_hot = route_flat[:, None] == jnp.arange(expert_total)[None, :]
     route_float = route_hot.astype(jnp.float32)
     count_pad = jnp.pad(jnp.sum(route_float, axis=0)[None, :], ((0, 7), (0, 128 - expert_total)))
-    gathered, count_sum = gather_mixer(mixer_weight.T, count_pad)
+    gathered, count_sum, (own_in, own_out) = gather_mixer(
+        mixer_weight.T, count_pad, [expert_in, expert_out]
+    )
     counts = count_sum[0, :expert_total]
     full_mixer = gathered.reshape(4 * model_width, model_width)
     earlier = (slot_order[None, :] < slot_order[:, None]).astype(jnp.bfloat16)
@@ -463,19 +505,18 @@
     ).astype(jnp.bfloat16)
     experts = range(local_experts)
     outgoing = contract_rows(slot_hot, cotangent).astype(jnp.bfloat16)
-    outgoing, *shards, full_mixer = tie(
-        outgoing,
-        *[expert_in[e] for e in experts],
-        *[expert_out[e] for e in experts],
-        full_mixer,
-    )
+    outgoing, full_mixer = tie(outgoing, full_mixer)
     cot_home = swap_owner(
         outgoing.reshape(local_experts, owner_count, capacity, model_width)
         .transpose(1, 0, 2, 3)
         .reshape(owner_count, local_experts * capacity, model_width)
     )
-    ins = [[a] + [to_low(a, k) for k in range(1, low)] for a in shards[:local_experts]]
-    outs = [[a] + [to_low(a, k) for k in range(1, low)] for a in shards[local_experts:]]
+    row_move = [(to_high, high) if e % 2 == 0 else (to_low, low) for e in experts]
+    weight_move = [(to_low, low) if e % 2 == 0 else (to_high, high) for e in experts]
+    spread = lambda a, move: [a] + [move[0](a, k) for k in range(1, move[1])]
+    gather_back = lambda parts, move: [parts[0]] + [move[0](parts[k], -k) for k in range(1, move[1])]
+    ins = [spread(own_in[e], weight_move[e]) for e in experts]
+    outs = [spread(own_out[e], weight_move[e]) for e in experts]
     inner_weight = full_mixer[: 3 * model_width]
     outer_weight = full_mixer[3 * model_width :]
     inputs = tokens.astype(jnp.float32)
@@ -483,7 +524,6 @@
     normed_low = normed.astype(jnp.bfloat16)
     projected = times_transposed(normed_low, inner_weight).astype(jnp.bfloat16)
     attended, head_lse = attn_fwd(prefix_len, projected)
-    attended, *ins[0] = tie(attended, *ins[0])
     middle = inputs + times_transposed(attended, outer_weight)
     normed2, norm2_pull = jax.vjp(layer_norm, middle, ln2_gain, ln2_bias)
     normed2_low = normed2.astype(jnp.bfloat16)
@@ -492,60 +532,65 @@
     )
     gate_value = jax.nn.sigmoid(chosen)
     first_expert = lax.axis_index("expert") * local_experts
-    grad_rows, produced_parts, moved, in_grads, out_grads = [], [], [], [], []
+    in_grads, out_grads = [], []
     router_part = jnp.zeros((model_width, expert_total), jnp.float32)
     normed2_low, cot_home = tie(normed2_low, cot_home)
-    cot_rows = [cot_home] + [to_high(cot_home, k) for k in range(1, high)]
-    cot_sets = [
-        [
-            a.reshape(owner_count, local_experts, capacity, model_width)
-            for a in cot_rows
-        ]
-        for e in experts
-    ]
+    cot_home = cot_home.reshape(owner_count, local_experts, capacity, model_width)
+    cot_rows = [spread(cot_home[:, e], row_move[e]) for e in experts]
     home = []
     for e in experts:
         hot = slot_hot[:, e * part_rows : (e + 1) * part_rows]
         source = normed2_low
         if e == 1:
-            source, *outs[0] = tie(normed2_low, *outs[0])
+            source, *tied = tie(normed2_low, *[a for g in ins + outs for a in g])
+            tied = [[tied.pop(0) for _ in g] for g in ins + outs]
+            ins, outs = tied[:local_experts], tied[local_experts:]
         outgoing = contract_rows(hot, source).astype(jnp.bfloat16)
         home.append(swap_owner(outgoing.reshape(owner_count, capacity, model_width)))
-    row_sets = [[a] + [to_high(a, k) for k in range(1, high)] for a in home]
-    tied = tie(*row_sets[0], *home[1:], *[a for e in experts[1:] for a in ins[e]])
-    row_sets[0], tied = list(tied[:high]), tied[high:]
-    for e in range(1, local_experts):
+    home[0], *cot_rows[0] = tie(home[0], *cot_rows[0])
+    first_rows = spread(home[0], row_move[0])
+    row_sets = [first_rows] + [spread(home[e], row_move[e]) for e in experts[1:]]
+    tied = tie(*first_rows, *ins[0], *outs[0], *home[1:])
+    row_sets[0], tied = list(tied[: len(first_rows)]), tied[len(first_rows) + 2 * len(ins[0]) :]
+    for e in experts[1:]:
         row_sets[e][0] = tied[e - 1]
-        ins[e] = list(tied[local_experts - 1 + (e - 1) * low :][:low])
+    done = {}
+    before = []
     for e in experts:
         column = (jnp.arange(expert_total) == first_expert + e).astype(jnp.float32)
         router_column = jnp.sum(router_weight.astype(jnp.float32) * column[None, :], axis=1)
-        produced, slot_grad, in_part, out_part, router_row = run_expert(
-            e, router_column[None, :], row_sets[e], cot_sets[e], ins[e], outs[e]
-        )
-        grad_rows.append(slot_grad)
-        produced_parts.append(produced)
-        moved.append([to_high(slot_grad[k], -k) for k in range(1, high)])
-        for parts, sums in ((in_part, in_grads), (out_part, out_grads)):
-            sums.append([parts[0]] + [to_low(parts[k], -k) for k in range(1, low)])
-        router_part = router_part + router_row[0][:, None] * column[None, :]
-    router_part, *held = tie(router_part, *[a for e in experts[:-1] for a in moved[e]])
-    moved[:-1] = [held[e * (high - 1) : (e + 1) * (high - 1)] for e in experts[:-1]]
+        for r in [*range(1, row_move[e][1]), 0]:
+            rows = row_sets[e][r]
+            if before:
+                rows = tie(rows, *before)[0]
+            kind = F32 if r == 0 else BF
+            done[e, r] = run_rows(
+                kind, router_column[None, :], rows, cot_rows[e][r], ins[e], outs[e]
+            )
+            before = [done[e, r][5]]
+            router_part = router_part + done[e, r][5][0][:, None] * column[None, :]
+        parts = [done[e, r] for r in range(row_move[e][1])]
+        tied = tie(*before, *[p[i] for p in parts for i in (4, 2, 3)])
+        in_part, out_part = run_grads(weight_move[e][1], row_sets[e], tied[1::3], tied[2::3], tied[3::3])
+        before = [in_part[0]]
+        for own, sums in ((in_part, in_grads), (out_part, out_grads)):
+            sums.append(gather_back(own, weight_move[e]))
+    returning = lambda e, i: gather_back(
+        [done[e, r][i] for r in range(row_move[e][1])], row_move[e]
+    )
+    moved = [returning(e, 1) for e in experts]
+    gate_row = done[local_experts - 1, row_move[-1][1] - 1][5]
+    moved[:-1] = [tie(*moved[e], gate_row)[:-1] for e in experts[:-1]]
     back_rows = []
     for e in experts:
-        total = grad_rows[e][0]
-        for a in moved[e]:
+        total = moved[e][0]
+        for a in moved[e][1:]:
             total = total + a.astype(jnp.float32)
         back_rows.append(swap_owner(total.astype(jnp.bfloat16)))
-    tied = tie(*[a for p in produced_parts for a in p[1:]], *moved[-1])
-    totals = []
     for e in experts:
-        total = produced_parts[e][0]
-        for k in range(1, high):
-            total = total + to_high(tied[e * (high - 1) + k - 1], -k).astype(jnp.float32)
-        totals.append(total.astype(jnp.bfloat16))
-    produced_home = swap_owner(jnp.concatenate(totals, axis=1))
-    produced_home = produced_home.reshape(owner_count, local_experts, capacity, model_width)
+        for r in range(1, row_move[e][1]):
+            done[e, r] = [tie(done[e, r][0], *moved[-1])[0]] + list(done[e, r][1:])
+    produced_moved = [returning(e, 0) for e in experts]
     out_grad = cotangent.astype(jnp.float32)
     mean_load = jnp.sum(counts) / expert_total
     load_weight = (
@@ -560,12 +605,6 @@
         jnp.concatenate([r.reshape(part_rows, model_width) for r in back_rows]),
         preferred_element_type=jnp.float32,
     )
-    returned = jnp.dot(
-        slot_hot,
-        produced_home.transpose(1, 0, 2, 3).reshape(expert_total * capacity, model_width),
-        preferred_element_type=jnp.float32,
-    )
-    mixed_out = (middle + gate_value[:, None] * returned).astype(jnp.bfloat16)
     middle_part, ln2_gain_part, ln2_bias_part = norm2_pull(normed2_grad)
     middle_grad = out_grad + middle_part
     attn_grad = middle_grad.astype(jnp.bfloat16)
@@ -579,13 +618,21 @@
         nn(part, inner_weight[c * model_width : (c + 1) * model_width])
         for c, part in enumerate(parts)
     )
-    flat = [a for group in in_grads + out_grads for a in group[1:]]
-    normed_grad, *flat = tie(normed_grad, *flat)
-    join = lambda groups: jnp.stack(
-        [sum((flat.pop(0).astype(jnp.float32) for _ in g[1:]), g[0]) for g in groups]
-    )
-    expert_in_grad = join(in_grads)
-    expert_out_grad = join(out_grads)
+    normed_grad, *tied = tie(normed_grad, *[a for p in produced_moved for a in p[1:]])
+    totals = []
+    for e in experts:
+        total = produced_moved[e][0]
+        for _ in produced_moved[e][1:]:
+            total = total + tied.pop(0).astype(jnp.float32)
+        totals.append(total.astype(jnp.bfloat16))
+    produced_home = swap_owner(jnp.concatenate(totals, axis=1))
+    produced_home = produced_home.reshape(owner_count, local_experts, capacity, model_width)
+    returned = jnp.dot(
+        slot_hot,
+        produced_home.transpose(1, 0, 2, 3).reshape(expert_total * capacity, model_width),
+        preferred_element_type=jnp.float32,
+    )
+    mixed_out = (middle + gate_value[:, None] * returned).astype(jnp.bfloat16)
     input_part, ln1_gain_part, ln1_bias_part = norm_pull(normed_grad)
     tokens_grad = middle_grad + input_part
     small = jnp.concatenate(
@@ -596,6 +643,9 @@
         ]
     )
     mixer_grad, summed = scatter_mixer(grad_blocks, small)
+    mixer_grad, *late = tie(mixer_grad, *[a for g in in_grads + out_grads for a in g])
+    late = [[late.pop(0) for _ in g] for g in in_grads + out_grads]
+    expert_in_grad, expert_out_grad = join_grads(late, local_experts)
     return (
         mixed_out,
         tokens_grad,

time: 503 us -> 423 us (0.84)
  waiting for transfers between devices: 144 us -> 43.8 us
  Pallas kernels: 189 us -> 222 us
  other arithmetic: 39.8 us -> 28.3 us
    ppermute x7 -> x8, waiting for transfers between devices: 89.3 us -> 4.61 us  [on_device(): to_high = lambda a, k: lax.ppermute(a, 'dp', high_shift(dp_count, low, k))]
    pallas_call x3 -> x8, Pallas kernels: 96.4 us -> 117 us  [the longest x4 52.7 us: run_rows(): pl.pallas_call(functools.partial(rows_kernel, nw, tiles), grid=(nw * tile...]
    ppermute x8, waiting for transfers between devices: 23.6 us -> 4.7 us  [on_device(): to_low = lambda a, k: lax.ppermute(a, 'dp', low_shift(dp_count, low, k))]
    pallas_call x1, Pallas kernels: 35.9 us -> 48.2 us  [scatter_mixer(): pl.pallas_call(scatter_kernel, in_specs=[V, V], out_specs=[V, V], out_sha...]
    another operation x6 -> x0, other arithmetic: 12.1 us -> none  [on_device(): jnp.stack([sum((flat.pop(0).astype(jnp.float32) for _ in g[1:]), g[0]) fo...]
    unnamed x63 -> x67, local copies, waits for them, and re-layouts: 14.9 us -> 12.8 us
  transfers between devices with their start and end apart: 21 -> 22, of which waited for: 11 -> 7; matrix products, arithmetic and copies ran while one was open for 18% -> 19% of each run, Pallas kernels for 25% -> 45%
where the time goes in v4:
time: 423 us; the launch traced here: 418 us
  Pallas kernels  222 us (52%)
  matrix products  51.3 us (12%)
  starting transfers between devices  44.7 us (11%)
  waiting for transfers between devices  43.8 us (10%)
  other arithmetic  28.3 us (7%)
  local copies, waits for them, and re-layouts  24.5 us (6%)
    pallas_call x4, Pallas kernels, run_rows(): pl.pallas_call(functools.partial(rows_kernel, nw, tiles), grid=(nw * tile...  52.7 us
    pallas_call x1, Pallas kernels, scatter_mixer(): pl.pallas_call(scatter_kernel, in_specs=[V, V], out_specs=[V, V], out_sha...  48.2 us
    pallas_call x1, Pallas kernels, gather_mixer(): pl.pallas_call(functools.partial(gather_kernel, nx), in_specs=[V, V] + [A...  34.9 us
    all_to_all x6, waiting for transfers between devices, on_device(): lax.all_to_all(a, 'expert', split_axis=0, concat_axis=0, tiled=True)  34.5 us
    pallas_call x1, Pallas kernels, attn_bwd(): pl.pallas_call(bwd_kernel, grid=(n,), in_specs=[pl.BlockSpec(memory_space...  34 us
    all_to_all x6, starting transfers between devices, on_device(): lax.all_to_all(a, 'expert', split_axis=0, concat_axis=0, tiled=True)  28.7 us
    pallas_call x1, Pallas kernels, attn_fwd(): pl.pallas_call(fwd_kernel, grid=(n,), in_specs=[pl.BlockSpec(memory_space...  22.7 us
    pallas_call x2, Pallas kernels, run_grads(): pl.pallas_call(functools.partial(grads_kernel, nr, nw, tiles), grid=(nw *...  21.9 us
  transfers between devices with their start and end apart: 22, of which 7 were waited for; matrix products, arithmetic and copies ran while one was open for 19% of the time, Pallas kernels for 45%

profile of v4, /device:TPU:0, one launch (start us, length us, event | category | flops | bytes accessed | tf_op | source)
XLA Modules:
  0.0 418.1 jit_solution(10772745791849821374)
XLA Ops:
  4.4 3.8 convolution_convert_fusion.2
  8.3 34.9 %gather_mixer.1 = (bf16[32,96,768]{2,1,0:T(8,128)(2,1)}, f32[8,128]{1,0:T(8,128)}, bf16[768,768]{1,0:T(8,128)(2,1)}, bf16[768,768]{1,0:T(8,128)(2,1)}, bf16[768,...) custom-call(bf16[96,768]{1,0:T(8,128)(2,1)} %bitcast.72, f32[8,128]{1,0:T(8,128)} %pad.4.small_ref, ...), custom_call_target="tpu_custom_call" | custom-call | bytes 4718592 | tf_op jit(solution)/shard_map/gather_mixer/pallas_call | solution.py:356
  44.5 4.5 %all-to-all-start = ((bf16[8,128,768]{2,1,0:T(8,128)(2,1)}), bf16[8,128,768]{2,1,0:T(8,128)(2,1)}, u32[]{:S(2)}, u32[]{:S(2)}) async-start(bf16[8,128,768]{2,1,0:T(8,128)(2,1)} %bitcast.8), calls=%async_computation | async-start | bytes 3145728 | tf_op jit(solution)/shard_map/all_to_all | solution.py:483
  55.2 8.1 %convolution_convert_fusion.q_ref.k_ref.v_ref = bf16[1024,2304]{1,0:T(8,128)(2,1)} fusion(bf16[3072,768]{1,0:T(8,128)(2,1)} %bitcast.57, bf16[1024,768]{0,1:T(8,128)(2,1)S(1)} %copy.34, f32[768]{0:T(1024)S(1)} %copy-done.28, f32[768]{0:T(1024)S(1)} %copy-done.20, f32[1024]{0:T(1024)S(1)} %fusion.50, f32[1024]{0:T(1024)S(1)} %broadcast_multiply_fusion.1), kind=kOutput, calls=%fused_computation | convolution fusion | flops 3630956544 | bytes 9844736 | tf_op jit(solution)/shard_map/dot_general | solution.py:27
  63.3 22.7 %attn_fwd.1 = (bf16[1024,768]{1,0:T(8,128)(2,1)}, f32[6,2,1024]{2,1,0:T(2,128)}) custom-call(s32[1]{0:T(128)S(6)} %copy.58.pre_ref, bf16[1024,2304]{1,0:T(8,128)(2,1)} %convolution_convert_fusion.q_ref.k_ref.v_ref, bf16[1024,2304]{1,0:T(8,128)(2,1)} %convolution_convert_fusion.q_ref.k_ref.v_ref, bf16[1024,2304]{1,0:T(8,128)(2,1)} %convolution_convert_fusion.q_ref.k_ref.v_ref), custom_call_target="tpu_custom_call" | custom-call | tf_op jit(solution)/shard_map/attn_fwd/pallas_call | solution.py:89
  95.7 5.1 %all-to-all-start.1 = ((bf16[8,64,768]{2,1,0:T(8,128)(2,1)}), bf16[8,64,768]{2,1,0:T(8,128)(2,1)}, u32[]{:S(2)}, u32[]{:S(2)}) async-start(bf16[8,64,768]{2,1,0:T(8,128)(2,1)} %bitcast.56), calls=%async_computation.1 | async-start | bytes 1572864 | tf_op jit(solution)/shard_map/all_to_all | solution.py:483
  108.7 13.1 %all-to-all-done.1.x_ref.refs_0_ = bf16[8,64,768]{2,1,0:T(8,128)(2,1)} async-done(((bf16[8,64,768]{2,1,0:T(8,128)(2,1)}), bf16[8,64,768]{2,1,0:T(8,128)(2,1)}, u32[]{:S(2)}, u32[]{:S(2)}) %all-to-all-start.1) | async-done | bytes 786464 | tf_op jit(solution)/shard_map/all_to_all | solution.py:483
  121.8 4.4 %all-to-all-start.2 = ((bf16[8,64,768]{2,1,0:T(8,128)(2,1)}), bf16[8,64,768]{2,1,0:T(8,128)(2,1)}, u32[]{:S(2)}, u32[]{:S(2)}) async-start(bf16[8,64,768]{2,1,0:T(8,128)(2,1)} %bitcast.55), calls=%async_computation.2 | async-start | bytes 1572864 | tf_op jit(solution)/shard_map/all_to_all | solution.py:483
  128.8 18.3 %all-to-all-done.2.x_ref.refs_0_ = bf16[8,64,768]{2,1,0:T(8,128)(2,1)} async-done(((bf16[8,64,768]{2,1,0:T(8,128)(2,1)}), bf16[8,64,768]{2,1,0:T(8,128)(2,1)}, u32[]{:S(2)}, u32[]{:S(2)}) %all-to-all-start.2) | async-done | bytes 786464 | tf_op jit(solution)/shard_map/all_to_all | solution.py:483
  148.0 12.9 %expert_rows.4 = (bf16[8,64,768]{2,1,0:T(8,128)(2,1)}, bf16[8,64,768]{2,1,0:T(8,128)(2,1)}, bf16[2,512,768]{2,1,0:T(8,128)(2,1)}, bf16[2,512,768]{2,1,0:T(8,128)...) custom-call(f32[1,768]{1,0:T(1,128)} %broadcast_in_dim.17.rw_ref, ...), custom_call_target="tpu_custom_call" | custom-call | flops 4831838208 | bytes 11796480 | tf_op jit(solution)/shard_map/expert_rows/pallas_call | solution.py:212
  160.9 13.7 %expert_rows.5 = (f32[8,64,768]{2,1,0:T(8,128)}, f32[8,64,768]{2,1,0:T(8,128)}, bf16[2,512,768]{2,1,0:T(8,128)(2,1)}, bf16[2,512,768]{2,1,0:T(8,128)(2,1)}, bf16[512,768]{1,0:T(8,128)(2,1)}, /*index=5*/f32[1,768]{1,0:T(1,128)}) custom-call(f32[1,768]{1,0:T(1,128)} %broadcast_in_dim.17.rw_ref, bf16[8,64,768]{2,1,0:T(8,128)(2,1)} %all-to-all-done.1.x_ref.refs_0_, ...), custom_call_target="tpu_custom_call" | custom-call | flops 4831838208 | bytes 11796480 | tf_op jit(solution)/shard_map/expert_rows/pallas_call | solution.py:212
  175.1 11.0 %expert_grads.2 = (bf16[768,768]{1,0:T(8,128)(2,1)}, bf16[768,768]{1,0:T(8,128)(2,1)}, bf16[768,768]{1,0:T(8,128)(2,1)}, bf16[768,768]{1,0:T(8,128)(2,1)}) custom-call(bf16[8,64,768]{2,1,0:T(8,128)(2,1)} %all-to-all-done.1.x_ref.refs_0_, bf16[8,64,768]{2,1,0:T(8,128)(2,1)} %collective-permute-done.1.x_ref.refs_1_, ...), custom_call_target="tpu_custom_call" | custom-call | flops 4831838208 | bytes 14155776 | tf_op jit(solution)/shard_map/expert_grads/pallas_call | solution.py:238
  186.1 12.9 %expert_rows.6 = (bf16[8,64,768]{2,1,0:T(8,128)(2,1)}, bf16[8,64,768]{2,1,0:T(8,128)(2,1)}, bf16[2,512,768]{2,1,0:T(8,128)(2,1)}, bf16[2,512,768]{2,1,0:T(8,128)...) custom-call(f32[1,768]{1,0:T(1,128)} %broadcast_in_dim.18.rw_ref, ...), custom_call_target="tpu_custom_call" | custom-call | flops 4831838208 | bytes 11796480 | tf_op jit(solution)/shard_map/expert_rows/pallas_call | solution.py:212
  201.6 4.6 %all-to-all-start.3 = ((bf16[8,64,768]{2,1,0:T(8,128)(2,1)}), bf16[8,64,768]{2,1,0:T(8,128)(2,1)}, u32[]{:S(2)}, u32[]{:S(2)}) async-start(bf16[8,64,768]{2,1,0:T(8,128)(2,1)} %add_convert_fusion.5), calls=%async_computation.3 | async-start | bytes 1572864 | tf_op jit(solution)/shard_map/all_to_all | solution.py:483
  213.2 13.2 %expert_rows.7 = (f32[8,64,768]{2,1,0:T(8,128)}, f32[8,64,768]{2,1,0:T(8,128)}, bf16[2,512,768]{2,1,0:T(8,128)(2,1)}, bf16[2,512,768]{2,1,0:T(8,128)(2,1)}, bf16[512,768]{1,0:T(8,128)(2,1)}, /*index=5*/f32[1,768]{1,0:T(1,128)}) custom-call(f32[1,768]{1,0:T(1,128)} %broadcast_in_dim.18.rw_ref, bf16[8,64,768]{2,1,0:T(8,128)(2,1)} %all-to-all-done.2.x_ref.refs_0_, ...), custom_call_target="tpu_custom_call" | custom-call | flops 4831838208 | bytes 11796480 | tf_op jit(solution)/shard_map/expert_rows/pallas_call | solution.py:212
  231.7 5.2 %all-to-all-start.4 = ((bf16[8,64,768]{2,1,0:T(8,128)(2,1)}), bf16[8,64,768]{2,1,0:T(8,128)(2,1)}, u32[]{:S(2)}, u32[]{:S(2)}) async-start(bf16[8,64,768]{2,1,0:T(8,128)(2,1)} %add_convert_fusion.4), calls=%async_computation.4 | async-start | bytes 1572864 | tf_op jit(solution)/shard_map/all_to_all | solution.py:483
  237.7 11.0 %expert_grads.3 = (bf16[768,768]{1,0:T(8,128)(2,1)}, bf16[768,768]{1,0:T(8,128)(2,1)}, bf16[768,768]{1,0:T(8,128)(2,1)}, bf16[768,768]{1,0:T(8,128)(2,1)}) custom-call(bf16[8,64,768]{2,1,0:T(8,128)(2,1)} %all-to-all-done.2.x_ref.refs_0_, bf16[8,64,768]{2,1,0:T(8,128)(2,1)} %collective-permute-done.7.x_ref.refs_1_, ...), custom_call_target="tpu_custom_call" | custom-call | flops 4831838208 | bytes 14155776 | tf_op jit(solution)/shard_map/expert_grads/pallas_call | solution.py:238
  266.3 4.4 %convolution_convert_fusion.1.g_ref = bf16[1024,768]{1,0:T(8,128)(2,1)} fusion(bf16[1024,768]{0,1:T(8,128)(2,1)S(1)} %fusion.17, bf16[3072,768]{1,0:T(8,128)(2,1)} %bitcast.59), kind=kOutput, calls=%fused_computation.37 | convolution fusion | flops 1208745984 | bytes 4325376 | tf_op jit(solution)/shard_map/dot_general | solution.py:39
  270.7 34.0 %attn_bwd.1 = (bf16[1024,768]{1,0:T(8,128)(2,1)}, bf16[1024,768]{1,0:T(8,128)(2,1)}, bf16[1024,768]{1,0:T(8,128)(2,1)}) custom-call(s32[1]{0:T(128)S(6)} %copy.58.pre_ref, bf16[1024,2304]{1,0:T(8,128)(2,1)} %convolution_convert_fusion.q_ref.k_ref.v_ref, bf16[1024,2304]{1,0:T(8,128)(2,1)} %convolution_convert_fusion.q_ref.k_ref.v_ref, ...), custom_call_target="tpu_custom_call" | custom-call | tf_op jit(solution)/shard_map/attn_bwd/pallas_call | solution.py:141
  315.4 4.1 collective-permute-done.10
  325.6 5.0 %all-to-all-start.5 = ((bf16[8,128,768]{2,1,0:T(8,128)(2,1)}), bf16[8,128,768]{2,1,0:T(8,128)(2,1)}, u32[]{:S(2)}, u32[]{:S(2)}) async-start(bf16[8,128,768]{2,1,0:T(8,128)(2,1)} %pad_maximum_fusion.1), calls=%async_computation.5 | async-start | bytes 3145728 | tf_op jit(solution)/shard_map/all_to_all | solution.py:483
  341.4 48.2 %scatter_mixer.1 = (f32[96,768]{1,0:T(8,128)}, f32[24,768]{1,0:T(8,128)}) custom-call(bf16[32,96,768]{2,1,0:T(8,128)(2,1)} %bitcast.52, f32[24,768]{1,0:T(8,128)} %concatenate.15.small_ref), custom_call_target="tpu_custom_call" | custom-call | bytes 9437184 | tf_op jit(solution)/shard_map/scatter_mixer/pallas_call | solution.py:424
  390.8 5.9 %add_add_fusion.2 = f32[1024,768]{0,1:T(8,128)} fusion(f32[1024,768]{0,1:T(8,128)} %copy-done.4, bf16[1024,768]{0,1:T(8,128)(2,1)S(1)} %copy-done.5, f32[1024]{0:T(1024)S(1)} %negate_multiply_fusion, f32[1024]{0:T(1024)S(1)} %negate_multiply_fusion.1, f32[1024]{0:T(1024)S(1)} %multiply_multiply_fusion, f32[1024]{0:T(1024)S(1)} %broadcast_multiply_fusion.1, ...), kind=kLoop, calls=%fused_computation.24 | loop fusion | flops 9437184 | bytes 12606464 | tf_op jit(solution)/shard_map/add | solution.py:637
  400.3 7.7 %join_grads.1 = (f32[2,768,768]{2,1,0:T(8,128)}, f32[2,768,768]{2,1,0:T(8,128)}) custom-call(bf16[768,768]{1,0:T(8,128)(2,1)} %get-tuple-element.195.refs_0_, bf16[768,768]{1,0:T(8,128)(2,1)} %collective-permute-done.12.refs_1_, bf16[768,768]{1,0:T(8,128)(2,1)} %get-tuple-element.197.refs_2_, bf16[768,768]{1,0:T(8,128)(2,1)} %collective-permute-done.13.refs_3_, ...), custom_call_target="tpu_custom_call" | custom-call | bytes 18874368 | tf_op jit(solution)/shard_map/join_grads/pallas_call | solution.py:443
  (170 shorter events, 106.1 us)
Async XLA Ops:
  44.5 48.2 %all-to-all-start = ((bf16[8,128,768]{2,1,0:T(8,128)(2,1)}), bf16[8,128,768]{2,1,0:T(8,128)(2,1)}, u32[]{:S(2)}, u32[]{:S(2)}) async-start(bf16[8,128,768]{2,1,0:T(8,128)(2,1)} %bitcast.8), calls=%async_computation | async-start | bytes 3145728 | tf_op jit(solution)/shard_map/all_to_all | solution.py:483
  48.9 51.8 %collective-permute-start.2 = (bf16[768,768]{1,0:T(8,128)(2,1)}, bf16[768,768]{1,0:T(8,128)(2,1)}, u32[]{:S(2)}, u32[]{:S(2)}) collective-permute-start(bf16[768,768]{1,0:T(8,128)(2,1)} %get-tuple-element.119.refs_0_), channel_id=1, source_target_pairs={{0,8},{8,0},{16,24},{24,16},{1,9},{9,1},{17,25},{25,17},{2,10},{10... | collective-permute-start | bytes 3538952 | tf_op jit(solution)/shard_map/ppermute | solution.py:481
  49.8 50.9 %collective-permute-start.3 = (bf16[768,768]{1,0:T(8,128)(2,1)}, bf16[768,768]{1,0:T(8,128)(2,1)}, u32[]{:S(2)}, u32[]{:S(2)}) collective-permute-start(bf16[768,768]{1,0:T(8,128)(2,1)} %get-tuple-element.149.refs_0_), channel_id=1, source_target_pairs={{0,16},{8,24},{16,0},{24,8},{1,17},{9,25},{17,1},{25,9},{2,18},{10... | collective-permute-start | bytes 3538952 | tf_op jit(solution)/shard_map/ppermute | solution.py:482
  50.3 52.6 %collective-permute-start.4 = (bf16[768,768]{1,0:T(8,128)(2,1)}, bf16[768,768]{1,0:T(8,128)(2,1)}, u32[]{:S(2)}, u32[]{:S(2)}) collective-permute-start(bf16[768,768]{1,0:T(8,128)(2,1)} %get-tuple-element.121.refs_2_), channel_id=1, source_target_pairs={{0,8},{8,0},{16,24},{24,16},{1,9},{9,1},{17,25},{25,17},{2,10},{10... | collective-permute-start | bytes 3538952 | tf_op jit(solution)/shard_map/ppermute | solution.py:481
  51.8 51.7 %collective-permute-start.5 = (bf16[768,768]{1,0:T(8,128)(2,1)}, bf16[768,768]{1,0:T(8,128)(2,1)}, u32[]{:S(2)}, u32[]{:S(2)}) collective-permute-start(bf16[768,768]{1,0:T(8,128)(2,1)} %get-tuple-element.151.refs_2_), channel_id=1, source_target_pairs={{0,16},{8,24},{16,0},{24,8},{1,17},{9,25},{17,1},{25,9},{2,18},{10... | collective-permute-start | bytes 3538952 | tf_op jit(solution)/shard_map/ppermute | solution.py:482
  95.7 26.1 %all-to-all-start.1 = ((bf16[8,64,768]{2,1,0:T(8,128)(2,1)}), bf16[8,64,768]{2,1,0:T(8,128)(2,1)}, u32[]{:S(2)}, u32[]{:S(2)}) async-start(bf16[8,64,768]{2,1,0:T(8,128)(2,1)} %bitcast.56), calls=%async_computation.1 | async-start | bytes 1572864 | tf_op jit(solution)/shard_map/all_to_all | solution.py:483
  106.2 20.9 %copy-start.16 = (bf16[768,16]{0,1:T(8,128)(2,1)S(1)}, bf16[768,16]{0,1:T(8,128)(2,1)}, u32[]{:S(2)}) copy-start(bf16[768,16]{0,1:T(8,128)(2,1)} %param.22) | copy-start | bytes 73732
  106.2 20.1 %collective-permute-start = (bf16[8,64,768]{2,1,0:T(8,128)(2,1)}, bf16[8,64,768]{2,1,0:T(8,128)(2,1)}, u32[]{:S(2)}, u32[]{:S(2)}) collective-permute-start(bf16[8,64,768]{2,1,0:T(8,128)(2,1)} %get-tuple-element.129.c_ref), channel_id=1, source_target_pairs={{0,16},{8,24},{16,0},{24,8},{1,17},{9,25},{17,1},{25,9},{2,18},{10... | collective-permute-start | bytes 2359304 | tf_op jit(solution)/shard_map/ppermute | solution.py:482
  121.8 25.4 %all-to-all-start.2 = ((bf16[8,64,768]{2,1,0:T(8,128)(2,1)}), bf16[8,64,768]{2,1,0:T(8,128)(2,1)}, u32[]{:S(2)}, u32[]{:S(2)}) async-start(bf16[8,64,768]{2,1,0:T(8,128)(2,1)} %bitcast.55), calls=%async_computation.2 | async-start | bytes 1572864 | tf_op jit(solution)/shard_map/all_to_all | solution.py:483
  126.2 21.7 %collective-permute-start.1 = (bf16[8,64,768]{2,1,0:T(8,128)(2,1)}, bf16[8,64,768]{2,1,0:T(8,128)(2,1)}, u32[]{:S(2)}, u32[]{:S(2)}) collective-permute-start(bf16[8,64,768]{2,1,0:T(8,128)(2,1)} %all-to-all-done.1.x_ref.refs_0_), channel_id=1, source_target_pairs={{0,16},{8,24},{16,0},{24,8},{1,17},{9,25},{17,1},{25,9},{2,18},{10... | collective-permute-start | bytes 2359304 | tf_op jit(solution)/shard_map/ppermute | solution.py:482
  128.3 57.8 %collective-permute-start.8 = (bf16[8,64,768]{2,1,0:T(8,128)(2,1)}, bf16[8,64,768]{2,1,0:T(8,128)(2,1)}, u32[]{:S(2)}, u32[]{:S(2)}) collective-permute-start(bf16[8,64,768]{2,1,0:T(8,128)(2,1)} %get-tuple-element.242.c_ref), channel_id=1, source_target_pairs={{0,8},{8,0},{16,24},{24,16},{1,9},{9,1},{17,25},{25,17},{2,10},{10... | collective-permute-start | bytes 2359304 | tf_op jit(solution)/shard_map/ppermute | solution.py:481
  147.2 38.9 %collective-permute-start.7 = (bf16[8,64,768]{2,1,0:T(8,128)(2,1)}, bf16[8,64,768]{2,1,0:T(8,128)(2,1)}, u32[]{:S(2)}, u32[]{:S(2)}) collective-permute-start(bf16[8,64,768]{2,1,0:T(8,128)(2,1)} %all-to-all-done.2.x_ref.refs_0_), channel_id=1, source_target_pairs={{0,8},{8,0},{16,24},{24,16},{1,9},{9,1},{17,25},{25,17},{2,10},{10... | collective-permute-start | bytes 2359304 | tf_op jit(solution)/shard_map/ppermute | solution.py:481
  174.5 24.4 %collective-permute-start.6 = (bf16[8,64,768]{2,1,0:T(8,128)(2,1)}, bf16[8,64,768]{2,1,0:T(8,128)(2,1)}, u32[]{:S(2)}, u32[]{:S(2)}) collective-permute-start(bf16[8,64,768]{2,1,0:T(8,128)(2,1)} %get-tuple-element.133), channel_id=1, source_target_pairs={{0,16},{8,24},{16,0},{24,8},{1,17},{9,25},{17,1},{25,9},{2,18},{10... | collective-permute-start | bytes 2359304 | tf_op jit(solution)/shard_map/ppermute | solution.py:482
  201.6 30.0 %all-to-all-start.3 = ((bf16[8,64,768]{2,1,0:T(8,128)(2,1)}), bf16[8,64,768]{2,1,0:T(8,128)(2,1)}, u32[]{:S(2)}, u32[]{:S(2)}) async-start(bf16[8,64,768]{2,1,0:T(8,128)(2,1)} %add_convert_fusion.5), calls=%async_computation.3 | async-start | bytes 1572864 | tf_op jit(solution)/shard_map/all_to_all | solution.py:483
  208.8 20.2 %collective-permute-start.9 = (bf16[8,64,768]{2,1,0:T(8,128)(2,1)}, bf16[8,64,768]{2,1,0:T(8,128)(2,1)}, u32[]{:S(2)}, u32[]{:S(2)}) collective-permute-start(bf16[8,64,768]{2,1,0:T(8,128)(2,1)} %get-tuple-element.159), channel_id=1, source_target_pairs={{0,8},{8,0},{16,24},{24,16},{1,9},{9,1},{17,25},{25,17},{2,10},{10... | collective-permute-start | bytes 2359304 | tf_op jit(solution)/shard_map/ppermute | solution.py:481
  231.7 26.2 %all-to-all-start.4 = ((bf16[8,64,768]{2,1,0:T(8,128)(2,1)}), bf16[8,64,768]{2,1,0:T(8,128)(2,1)}, u32[]{:S(2)}, u32[]{:S(2)}) async-start(bf16[8,64,768]{2,1,0:T(8,128)(2,1)} %add_convert_fusion.4), calls=%async_computation.4 | async-start | bytes 1572864 | tf_op jit(solution)/shard_map/all_to_all | solution.py:483
  237.7 14.5 %copy-start.22 = (f32[1,768]{1,0:T(1,128)S(1)}, f32[1,768]{1,0:T(1,128)}, u32[]{:S(2)}) copy-start(f32[1,768]{1,0:T(1,128)} %get-tuple-element.127) | copy-start | bytes 9220
  248.6 141.0 %collective-permute-start.13 = (bf16[768,768]{1,0:T(8,128)(2,1)}, bf16[768,768]{1,0:T(8,128)(2,1)}, u32[]{:S(2)}, u32[]{:S(2)}) collective-permute-start(bf16[768,768]{1,0:T(8,128)(2,1)} %get-tuple-element.189), channel_id=1, source_target_pairs={{0,16},{8,24},{16,0},{24,8},{1,17},{9,25},{17,1},{25,9},{2,18},{10... | collective-permute-start | bytes 3538952 | tf_op jit(solution)/shard_map/ppermute | solution.py:482
  250.2 139.4 %collective-permute-start.15 = (bf16[768,768]{1,0:T(8,128)(2,1)}, bf16[768,768]{1,0:T(8,128)(2,1)}, u32[]{:S(2)}, u32[]{:S(2)}) collective-permute-start(bf16[768,768]{1,0:T(8,128)(2,1)} %get-tuple-element.193), channel_id=1, source_target_pairs={{0,16},{8,24},{16,0},{24,8},{1,17},{9,25},{17,1},{25,9},{2,18},{10... | collective-permute-start | bytes 3538952 | tf_op jit(solution)/shard_map/ppermute | solution.py:482
  250.7 139.0 %collective-permute-start.12 = (bf16[768,768]{1,0:T(8,128)(2,1)}, bf16[768,768]{1,0:T(8,128)(2,1)}, u32[]{:S(2)}, u32[]{:S(2)}) collective-permute-start(bf16[768,768]{1,0:T(8,128)(2,1)} %get-tuple-element.175), channel_id=1, source_target_pairs={{0,8},{8,0},{16,24},{24,16},{1,9},{9,1},{17,25},{25,17},{2,10},{10... | collective-permute-start | bytes 3538952 | tf_op jit(solution)/shard_map/ppermute | solution.py:481
  252.7 61.1 %collective-permute-start.11 = (bf16[8,64,768]{2,1,0:T(8,128)(2,1)}, bf16[8,64,768]{2,1,0:T(8,128)(2,1)}, u32[]{:S(2)}, u32[]{:S(2)}) collective-permute-start(bf16[8,64,768]{2,1,0:T(8,128)(2,1)} %get-tuple-element.167), channel_id=1, source_target_pairs={{0,8},{8,0},{16,24},{24,16},{1,9},{9,1},{17,25},{25,17},{2,10},{10... | collective-permute-start | bytes 2359304 | tf_op jit(solution)/shard_map/ppermute | solution.py:481
  253.2 66.2 %collective-permute-start.10 = (bf16[8,64,768]{2,1,0:T(8,128)(2,1)}, bf16[8,64,768]{2,1,0:T(8,128)(2,1)}, u32[]{:S(2)}, u32[]{:S(2)}) collective-permute-start(bf16[8,64,768]{2,1,0:T(8,128)(2,1)} %get-tuple-element.165), channel_id=1, source_target_pairs={{0,16},{8,24},{16,0},{24,8},{1,17},{9,25},{17,1},{25,9},{2,18},{10... | collective-permute-start | bytes 2359304 | tf_op jit(solution)/shard_map/ppermute | solution.py:482
  313.8 75.8 %collective-permute-start.14 = (bf16[768,768]{1,0:T(8,128)(2,1)}, bf16[768,768]{1,0:T(8,128)(2,1)}, u32[]{:S(2)}, u32[]{:S(2)}) collective-permute-start(bf16[768,768]{1,0:T(8,128)(2,1)} %get-tuple-element.191), channel_id=1, source_target_pairs={{0,8},{8,0},{16,24},{24,16},{1,9},{9,1},{17,25},{25,17},{2,10},{10... | collective-permute-start | bytes 3538952 | tf_op jit(solution)/shard_map/ppermute | solution.py:481
  325.6 83.7 %all-to-all-start.5 = ((bf16[8,128,768]{2,1,0:T(8,128)(2,1)}), bf16[8,128,768]{2,1,0:T(8,128)(2,1)}, u32[]{:S(2)}, u32[]{:S(2)}) async-start(bf16[8,128,768]{2,1,0:T(8,128)(2,1)} %pad_maximum_fusion.1), calls=%async_computation.5 | async-start | bytes 3145728 | tf_op jit(solution)/shard_map/all_to_all | solution.py:483
  (29 other events, 134.6 us)
